TPU v7x, 128 devices: a whole 4x4x4 slice. The times are simulated.
128 devices in a mesh: gx: 8 (over x, core), gz: 16 (over y, z).
Axes of the slice: x: 4, y: 4, z: 4, core: 2. Of those that a mesh axis runs over, the one named last changes fastest.
Arguments:
- velocity: float32 [3, 2048, 8, 2048], P(None, 'gx', None, 'gz'), may hold values from -32 to 32
Outputs:
- grad_x: float32 [3, 2048, 8, 2048], P(None, 'gx', None, 'gz')
- grad_z: float32 [3, 2048, 8, 2048], P(None, 'gx', None, 'gz')
- convect: float32 [3, 2048, 8, 2048], P(None, 'gx', None, 'gz')
- rebuilt: float32 [2, 2048, 8, 2048], P(None, 'gx', None, 'gz')
All inputs are finite; a program needn't handle non-finite values.
Results may differ from a plain program's by a relative error of at most 0.0003.
Values sent between devices are 32-bit elements; how exact they have to be, the bound alone decides.
No kernel may reach another device: no remote copies, remote signals or barrier semaphores. Data moves between devices by JAX's collectives and lax.ppermute only.
A program may use at most 256 MiB of HBM per device.

v0:
```python
import math

import jax
import jax.numpy as jnp
from jax import lax
from jax.sharding import PartitionSpec as P

ALPHA = 1.0 / 3.0
COEF_A = 14.0 / 9.0
COEF_B = 1.0 / 9.0
BLOCK_CAP = 128


def with_halo(array, sides, width):
    for axis, dim in sides:
        peers, length = (lax.axis_size(axis), array.shape[dim])
        up = [(i, (i + 1) % peers) for i in range(peers)]
        down = [(j, i) for i, j in up]
        last = lax.slice_in_dim(array, length - width, length, axis=dim)
        initial = lax.slice_in_dim(array, 0, width, axis=dim)
        before = lax.ppermute(last, axis, up)
        after = lax.ppermute(initial, axis, down)
        array = jnp.concatenate([before, array, after], axis=dim)
    return array


def entering(array, axis, combine, identity):
    peers, mine = (lax.axis_size(axis), lax.axis_index(axis))
    everything = lax.all_gather(array, axis)
    start = jnp.broadcast_to(jnp.asarray(identity, array.dtype), array.shape)

    def hop(k, before):
        reached = k < mine
        new = combine(before, everything[k])
        return jnp.where(reached, new, before)

    return lax.fori_loop(0, peers, hop, start)


def matmul_high(left_matrix, right_matrix):
    return jnp.dot(left_matrix, right_matrix, precision=lax.Precision.HIGHEST)


def block_inverse(length):
    offsets = jnp.arange(length)
    neighbour = (jnp.abs(offsets[:, None] - offsets[None, :]) == 1).astype(jnp.float32) * ALPHA
    identity = jnp.eye(length, dtype=jnp.float32)
    inverse = identity - neighbour
    near_power = neighbour
    for squaring in range(7):
        near_power = matmul_high(near_power, near_power)
        inverse = matmul_high(inverse, identity + near_power)
    return inverse


def explicit(padded, axis_at, length):

    def cell_slice(offset):
        return lax.slice_in_dim(padded, offset, offset + length, axis=axis_at)

    return 0.5 * COEF_A * (cell_slice(3) - cell_slice(1)) + 0.25 * COEF_B * (
        cell_slice(4) - cell_slice(0)
    )


def apply_matrix(source, matrix, axis_at):
    shape_now = source.shape
    if axis_at == source.ndim - 1:
        return jnp.dot(source, matrix.T, precision=lax.Precision.HIGHEST)
    length = shape_now[axis_at]
    leading = math.prod(shape_now[:axis_at])
    trailing = math.prod(shape_now[axis_at + 1 :])
    flat = source.reshape(leading, length, trailing)
    batched = jnp.broadcast_to(matrix, (leading,) + matrix.shape)
    result = lax.dot_general(
        batched, flat, (((2,), (1,)), ((0,), (0,))), precision=lax.Precision.HIGHEST
    )
    return result.reshape(shape_now)


def blocked(values, axis_at, block):
    shape_now = values.shape
    return values.reshape(
        shape_now[:axis_at] + (shape_now[axis_at] // block, block) + shape_now[axis_at + 1 :]
    )


def correct(solved, inverse, axis_at, prev_last, next_first):
    length = solved.shape[axis_at]
    first_cell = lax.slice_in_dim(solved, 0, 1, axis=axis_at)
    last_cell = lax.slice_in_dim(solved, length - 1, length, axis=axis_at)
    pivot_term = ALPHA * inverse[0, 0]
    denom_pair = 1.0 - pivot_term * pivot_term
    left_value = (prev_last - pivot_term * first_cell) / denom_pair
    right_value = (next_first - pivot_term * last_cell) / denom_pair
    shape_list = [1] * solved.ndim
    shape_list[axis_at] = length
    left_column = inverse[:, 0].reshape(shape_list)
    right_column = inverse[:, length - 1].reshape(shape_list)
    return solved - ALPHA * (left_value * left_column + right_value * right_column)


def couple(solved, inverse, axis_at, edge_before, edge_after):
    block = solved.shape[axis_at + 1]
    count = solved.shape[axis_at]
    first_cells = lax.slice_in_dim(solved, 0, 1, axis=axis_at + 1)
    last_cells = lax.slice_in_dim(solved, block - 1, block, axis=axis_at + 1)
    prev_last = jnp.concatenate(
        [edge_before, lax.slice_in_dim(last_cells, 0, count - 1, axis=axis_at)], axis_at
    )
    next_first = jnp.concatenate(
        [lax.slice_in_dim(first_cells, 1, count, axis=axis_at), edge_after], axis_at
    )
    return correct(solved, inverse, axis_at + 1, prev_last, next_first)


def whole_lines(lines, axis_at, inverse):
    total = lines.shape[axis_at]
    block = inverse.shape[0]
    head_cells = lax.slice_in_dim(lines, total - 2, total, axis=axis_at)
    tail_cells = lax.slice_in_dim(lines, 0, 2, axis=axis_at)
    padded = jnp.concatenate([head_cells, lines, tail_cells], axis_at)
    source = explicit(padded, axis_at, total)
    solved = apply_matrix(blocked(source, axis_at, block), inverse, axis_at + 1)
    count = solved.shape[axis_at]
    last_cells = lax.slice_in_dim(solved, block - 1, block, axis=axis_at + 1)
    first_cells = lax.slice_in_dim(solved, 0, 1, axis=axis_at + 1)
    edge_before = lax.slice_in_dim(last_cells, count - 1, count, axis=axis_at)
    edge_after = lax.slice_in_dim(first_cells, 0, 1, axis=axis_at)
    return couple(solved, inverse, axis_at, edge_before, edge_after).reshape(lines.shape)


def running_sum(values, axis_at):
    length = values.shape[axis_at]
    offsets = jnp.arange(length)
    lower = (offsets[:, None] > offsets[None, :]).astype(jnp.float32)
    return apply_matrix(values, lower, axis_at)


def line_terms(values, axis_at, start, total_len):
    length = values.shape[axis_at]
    shape_list = [1] * values.ndim
    shape_list[axis_at] = length
    position = (start + jnp.arange(length)).astype(jnp.float32).reshape(shape_list)
    centred = position - 0.5 * (total_len - 1)
    return (jnp.sum(values, axis_at), jnp.sum(values * centred, axis_at), position)


def primitive(values, axis_at, position, before_sum, total_sum, centred_sum, total_len):
    mean_value = jnp.expand_dims(total_sum, axis_at) / total_len
    inside = running_sum(values, axis_at) + jnp.expand_dims(before_sum, axis_at)
    result = inside - position * mean_value + 0.5 * (values - mean_value)
    result = result + jnp.expand_dims(centred_sum, axis_at) / total_len
    return -result / math.sqrt(total_len)


def add_terms(earlier, later):
    return earlier + later


def body(velocity):
    cells_x = velocity.shape[1]
    cells_z = velocity.shape[3]
    total_x = cells_x * lax.axis_size("gx")
    total_z = cells_z * lax.axis_size("gz")
    block_x = min(cells_x, BLOCK_CAP)
    inverse_x = block_inverse(block_x)
    fields_x = jnp.concatenate([velocity, velocity[0][None] * velocity], 0)
    fields_z = jnp.concatenate([velocity, velocity[2][None] * velocity], 0)
    padded_x = with_halo(fields_x, (("gx", 1),), 2)
    solved_x = apply_matrix(blocked(explicit(padded_x, 1, cells_x), 1, block_x), inverse_x, 2)
    rimmed_x = with_halo(solved_x.reshape(fields_x.shape), (("gx", 1),), 1)
    edge_before_x = rimmed_x[:, 0:1][:, :, None]
    edge_after_x = rimmed_x[:, cells_x + 1 : cells_x + 2][:, :, None]
    deriv_x = couple(solved_x, inverse_x, 1, edge_before_x, edge_after_x).reshape(fields_x.shape)
    solved_lines_z = whole_lines(
        lax.all_to_all(fields_z, "gz", split_axis=1, concat_axis=3, tiled=True), 3, inverse_x
    )
    deriv_z = lax.all_to_all(solved_lines_z, "gz", split_axis=3, concat_axis=1, tiled=True)
    slope_u = deriv_x[0]
    slope_w = deriv_z[2]
    sum_z, moment_z, position_z = line_terms(slope_u, 2, lax.axis_index("gz") * cells_z, total_z)
    sum_x, moment_x, position_x = line_terms(slope_w, 0, lax.axis_index("gx") * cells_x, total_x)
    before_z = entering(sum_z, "gz", add_terms, jnp.zeros_like(sum_z))
    line_sum_z, centred_z = lax.psum((sum_z, moment_z), "gz")
    before_x = entering(sum_x, "gx", add_terms, jnp.zeros_like(sum_x))
    line_sum_x, centred_x = lax.psum((sum_x, moment_x), "gx")
    rebuilt_x = primitive(slope_w, 0, position_x, before_x, line_sum_x, centred_x, total_x)
    rebuilt_z = primitive(slope_u, 2, position_z, before_z, line_sum_z, centred_z, total_z)
    grad_x = deriv_x[0:3]
    grad_z = deriv_z[0:3]
    convect = deriv_x[3:6] + deriv_z[3:6]
    rebuilt = jnp.stack([rebuilt_x, rebuilt_z])
    return (grad_x, grad_z, convect, rebuilt)


def solution(mesh):
    placed = (P(None, "gx", None, "gz"),)
    return jax.shard_map(
        body,
        mesh=mesh,
        in_specs=placed,
        out_specs=(
            P(None, "gx", None, "gz"),
            P(None, "gx", None, "gz"),
            P(None, "gx", None, "gz"),
            P(None, "gx", None, "gz"),
        ),
        check_vma=False,
    )
```

profile of v0, /device:TPU:0, one launch (start us, length us, event | category | flops | bytes accessed | tf_op | source)
XLA Modules:
  0.0 584.9 jit_solution(7324294546043416370)
XLA Ops:
  3.8 3.1 pad_maximum_fusion.3
  7.0 8.2 %all-to-all-start = ((f32[6,256,8,128]{3,2,0,1:T(8,128)}), f32[6,256,8,128]{3,2,0,1:T(8,128)}, u32[]{:S(2)}, u32[]{:S(2)}) async-start(f32[6,256,8,128]{3,2,0,1:T(8,128)} %pad_maximum_fusion.3), calls=%async_computation | async-start | bytes 12582912 | tf_op jit(solution)/shard_map/all_to_all | solution.py:177
  26.5 3.8 pad_maximum_fusion
  30.2 3.5 fusion.9
  33.8 7.1 %reshape_reshape.6 = f32[12,128,1024]{2,1,0:T(8,128)} reshape(f32[6,256,8,128]{3,2,1,0:T(8,128)} %fusion.9) | data formatting | bytes 12582912 | tf_op jit(solution)/shard_map/reshape;reshape | solution.py:73
  40.9 7.7 %fusion.29 = f32[12,128,1024]{2,1,0:T(8,128)S(1)} fusion(f32[12,128,1024]{2,1,0:T(8,128)} %reshape_reshape.6, f32[128,128]{1,0:T(8,128)S(1)} %copy.125), kind=kOutput, calls=%fused_computation.58 | convolution fusion | flops 2415919104 | bytes 12648448 | tf_op jit(solution)/shard_map/dot_general | solution.py:75
  48.5 4.2 copy.159
  52.7 64.8 %all-to-all-done = f32[6,256,8,128]{3,2,0,1:T(8,128)} async-done(((f32[6,256,8,128]{3,2,0,1:T(8,128)}), f32[6,256,8,128]{3,2,0,1:T(8,128)}, u32[]{:S(2)}, u32[]{:S(2)}) %all-to-all-start) | async-done | bytes 6291488 | tf_op jit(solution)/shard_map/all_to_all | solution.py:177
  117.5 9.0 %copy.168 = f32[6,16,16,8,128]{4,1,3,2,0:T(8,128)} copy(f32[6,16,16,8,128]{4,3,0,2,1:T(8,128)} %bitcast.11) | data formatting | bytes 12582912 | tf_op jit(solution)/shard_map/all_to_all | solution.py:177
  126.5 7.3 %all_to_all.27 = f32[6,16,8,2048]{3,2,1,0:T(8,128)} reshape(f32[6,16,8,16,128]{4,3,2,1,0:T(8,128)} %bitcast.122) | data formatting | bytes 12582912 | tf_op jit(solution)/shard_map/all_to_all | solution.py:177
  135.1 15.6 %fusion.4 = f32[6,16,8,16,128]{4,2,3,1,0:T(8,128)S(1)} fusion(f32[6,16,8,2]{3,2,1,0:T(8,128)S(1)} %get-tuple-element.259, f32[6,16,8,2048]{3,2,1,0:T(8,128)} %all_to_all.27, f32[6,16,8,2]{3,2,1,0:T(8,128)S(1)} %get-tuple-element.258), kind=kLoop, calls=%fused_computation.12 | loop fusion | flops 14155776 | bytes 12595200 | tf_op jit(solution)/shard_map/reshape | solution.py:83
  150.6 5.6 fusion.11
  156.2 6.9 %fusion.66 = (f32[6,16,8,15,1]{4,3,2,1,0:T(8,128)}, f32[6,16,8,15,1]{4,3,2,1,0:T(8,128)}) fusion(f32[6,16,8,16,128]{4,3,2,1,0:T(8,128)S(1)} %fusion.11), kind=kLoop, calls=%fused_computation.122 | loop fusion | bytes 184320 | tf_op jit(solution)/shard_map/slice | solution.py:109
  163.1 6.9 %fusion.64 = (f32[6,16,8,16,1]{4,3,2,1,0:T(8,128)}, f32[6,16,8,16,1]{4,3,2,1,0:T(8,128)}) fusion(f32[6,16,8,16,128]{4,3,2,1,0:T(8,128)S(1)} %fusion.11), kind=kLoop, calls=%fused_computation.120 | loop fusion | bytes 196608 | tf_op jit(solution)/shard_map/slice | solution.py:90
  171.9 6.4 %copy.134 = f32[6,16,8,15,1]{3,2,4,1,0:T(8,128)S(1)} copy(f32[6,16,8,15,1]{4,3,2,1,0:T(8,128)} %get-tuple-element.256) | data formatting | bytes 92160 | tf_op jit(solution)/shard_map/slice | solution.py:109
  178.3 6.6 %copy.136 = f32[6,16,8,15,1]{3,2,4,1,0:T(8,128)S(1)} copy(f32[6,16,8,15,1]{4,3,2,1,0:T(8,128)} %get-tuple-element.257) | data formatting | bytes 92160 | tf_op jit(solution)/shard_map/slice | solution.py:112
  184.8 6.3 %copy.157 = f32[6,16,8,16,1]{3,2,4,1,0:T(8,128)S(1)} copy(f32[6,16,8,16,1]{4,3,2,1,0:T(8,128)} %get-tuple-element.252) | data formatting | bytes 98304
  191.2 6.3 %copy.158 = f32[6,16,8,16,1]{3,2,4,1,0:T(8,128)S(1)} copy(f32[6,16,8,16,1]{4,3,2,1,0:T(8,128)} %get-tuple-element.253) | data formatting | bytes 98304
  197.8 9.0 %multiply_subtract_fusion = f32[6,16,8,16,128]{4,3,2,1,0:T(8,128)} fusion(f32[6,16,8,16,128]{4,3,2,1,0:T(8,128)} %copy-done, f32[128]{0:T(128)S(1)} %get-tuple-element.275, f32[6,16,8,16]{3,2,1,0:T(8,128)S(1)} %get-tuple-element.277, f32[128]{0:T(128)S(1)} %get-tuple-element.274, f32[6,16,8,16]{3,2,1,0:T(8,128)S(1)} %get-tuple-element.276), kind=kLoop, calls=%fused_computation.27 | loop fusion | flops 7864320 | bytes 12682240 | tf_op jit(solution)/shard_map/sub | solution.py:100
  206.8 22.5 %copy.153 = f32[6,16,8,16,128]{1,2,0,4,3:T(8,128)} copy(f32[6,16,8,16,128]{4,3,2,1,0:T(8,128)} %multiply_subtract_fusion) | data formatting | bytes 12582912 | tf_op jit(solution)/shard_map/reshape | solution.py:130
  229.3 28.2 %reshape.123 = f32[16,1,98304]{2,1,0:T(1,128)} reshape(f32[2048,6,8,16]{3,2,1,0:T(8,128)} %bitcast.113) | data formatting | bytes 12582912
  257.5 11.2 %all-to-all-start.1 = ((f32[16,1,98304]{2,1,0:T(1,128)}), f32[16,1,98304]{2,1,0:T(1,128)}, u32[]{:S(2)}, u32[]{:S(2)}) async-start(f32[16,1,98304]{2,1,0:T(1,128)} %reshape.123), calls=%async_computation.1 | async-start | bytes 12582912 | tf_op jit(solution)/shard_map/all_to_all | solution.py:179
  269.5 3.0 collective-permute-start.3
  274.9 3.6 multiply_subtract_fusion.1
  282.1 138.9 %all-reduce = (f32[256,8]{0,1:T(8,128)S(1)}, f32[256,8]{0,1:T(8,128)S(1)}) all-reduce(f32[256,8]{0,1:T(8,128)S(1)} %copy.149, f32[256,8]{0,1:T(8,128)S(1)} %copy.148), channel_id=1, replica_groups=mesh['gx'=8,'gz'=16] {'gz'}, use_global_device_ids=true, to_apply=%region_11.12 | all-reduce | flops 4096 | bytes 32768 | tf_op jit(solution)/shard_map/psum | solution.py:185
  421.0 20.6 %all_gather.15 = f32[16,256,8]{1,2,0:T(8,128)S(1)} all-gather(f32[1,256,8]{1,2,0:T(8,128)S(1)} %copy.147), channel_id=1, replica_groups=mesh['gx'=8,'gz'=16] {'gz'}, dimensions={0}, use_global_device_ids=true | all-gather | bytes 139264 | tf_op jit(solution)/shard_map/all_gather | solution.py:29
  444.4 5.9 %fusion.63 = (f32[3,2,128,8,128]{4,3,2,1,0:T(8,128)}, f32[3,2,128,8,128]{4,3,2,1,0:T(8,128)}) fusion(f32[6,2,128,8,128]{4,3,2,1,0:T(8,128)} %copy-done.3), kind=kLoop, calls=%fused_computation.119 | loop fusion | bytes 12582912 | tf_op jit(solution)/shard_map/slice | solution.py:192
  450.9 19.4 %reduce.4 = f32[16,98304]{1,0:T(8,128)} reduce(f32[16,1,98304]{2,1,0:T(1,128)} %all-to-all-done.1, f32[]{:T(128)} %broadcast.110), dimensions={1}, to_apply=%all_to_all.28.reduce_sub_computation | reduce | bytes 12582916 | tf_op jit(solution)/shard_map/all_to_all | solution.py:179
  470.3 37.0 %reshape.124 = f32[2048,6,8,16]{3,2,1,0:T(8,128)} reshape(f32[16,98304]{1,0:T(8,128)} %reduce.4) | data formatting | bytes 12582912
  507.3 25.3 %copy.154 = f32[6,16,8,16,128]{4,3,2,1,0:T(8,128)} copy(f32[6,16,8,16,128]{1,2,0,4,3:T(8,128)} %bitcast.114) | data formatting | bytes 12582912 | tf_op jit(solution)/shard_map/all_to_all | solution.py:179
  539.3 13.1 %all-gather = f32[64,128]{1,0:T(8,128)S(1)} all-gather(f32[8,128]{1,0:T(8,128)S(1)} %get-tuple-element.222), channel_id=2, replica_groups=mesh['gx'=8,'gz'=16] {'gx'}, dimensions={0}, use_global_device_ids=true | all-gather | bytes 36864 | tf_op jit(solution)/shard_map/all_gather | solution.py:29
  552.4 14.9 %all-reduce.1 = (f32[8,128]{1,0:T(8,128)S(1)}, f32[8,128]{1,0:T(8,128)S(1)}) all-reduce(f32[8,128]{1,0:T(8,128)S(1)} %get-tuple-element.223, f32[8,128]{1,0:T(8,128)S(1)} %get-tuple-element.222), channel_id=1, replica_groups=mesh['gx'=8,'gz'=16] {'gx'}, use_global_device_ids=true, to_apply=%region_5.6 | all-reduce | flops 2048 | bytes 16384 | tf_op jit(solution)/shard_map/psum | solution.py:187
  (109 shorter events, 50.3 us)
Async XLA Ops:
  0.6 2.8 copy-start.1
  7.0 110.5 %all-to-all-start = ((f32[6,256,8,128]{3,2,0,1:T(8,128)}), f32[6,256,8,128]{3,2,0,1:T(8,128)}, u32[]{:S(2)}, u32[]{:S(2)}) async-start(f32[6,256,8,128]{3,2,0,1:T(8,128)} %pad_maximum_fusion.3), calls=%async_computation | async-start | bytes 12582912 | tf_op jit(solution)/shard_map/all_to_all | solution.py:177
  16.6 1.7 copy-start.4
  18.3 8.1 %collective-permute-start = (f32[6,2,8,128]{3,2,1,0:T(8,128)S(1)}, f32[6,2,8,128]{3,2,1,0:T(8,128)S(1)}, u32[]{:S(2)}, u32[]{:S(2)}) collective-permute-start(f32[6,2,8,128]{3,2,1,0:T(8,128)S(1)} %get-tuple-element.268), channel_id=1, source_target_pairs={{16,0},{32,16},{48,32},{64,48},{80,64},{96,80},{112,96},{0,112},{1... | collective-permute-start | bytes 147464 | tf_op jit(solution)/shard_map/ppermute | solution.py:22
  20.2 6.2 %collective-permute-start.1 = (f32[6,2,8,128]{3,2,1,0:T(8,128)S(1)}, f32[6,2,8,128]{3,2,1,0:T(8,128)S(1)}, u32[]{:S(2)}, u32[]{:S(2)}) collective-permute-start(f32[6,2,8,128]{3,2,1,0:T(8,128)S(1)} %get-tuple-element.269), channel_id=1, source_target_pairs={{0,16},{16,32},{32,48},{48,64},{64,80},{80,96},{96,112},{112,0},{1... | collective-permute-start | bytes 147464 | tf_op jit(solution)/shard_map/ppermute | solution.py:21
  156.2 13.9 %copy-start = (f32[6,16,8,16,128]{4,3,2,1,0:T(8,128)}, f32[6,16,8,16,128]{4,3,2,1,0:T(8,128)S(1)}, u32[]{:S(2)}) copy-start(f32[6,16,8,16,128]{4,3,2,1,0:T(8,128)S(1)} %fusion.11) | copy-start | bytes 18874372
  184.8 12.7 %copy-start.7 = (f32[6,16,8,1,1]{4,3,2,1,0:T(1,128)S(1)}, f32[6,16,8,1,1]{4,3,2,1,0:T(1,128)}, u32[]{:S(2)}) copy-start(f32[6,16,8,1,1]{4,3,2,1,0:T(1,128)} %get-tuple-element.255) | copy-start | bytes 9220
  257.5 192.9 %all-to-all-start.1 = ((f32[16,1,98304]{2,1,0:T(1,128)}), f32[16,1,98304]{2,1,0:T(1,128)}, u32[]{:S(2)}, u32[]{:S(2)}) async-start(f32[16,1,98304]{2,1,0:T(1,128)} %reshape.123), calls=%async_computation.1 | async-start | bytes 12582912 | tf_op jit(solution)/shard_map/all_to_all | solution.py:179
  269.5 4.5 collective-permute-start.2
  269.5 4.5 collective-permute-start.3
  278.4 2.6 copy-start.3
  532.6 4.5 copy-start.2
  537.0 35.2 %copy-start.8 = (f32[8,128]{1,0:T(8,128)S(1)}, f32[8,128]{1,0:T(8,128)}, u32[]{:S(2)}) copy-start(f32[8,128]{1,0:T(8,128)} %custom-call) | copy-start | bytes 12292
  537.0 35.5 %copy-start.9 = (f32[256]{0:T(256)S(1)}, f32[256]{0:T(256)}, u32[]{:S(2)}) copy-start(f32[256]{0:T(256)} %add_convert_fusion) | copy-start | bytes 3076
  572.5 6.6 %copy-start.5 = (f32[3,16,16,8,128]{4,1,3,2,0:T(8,128)S(1)}, f32[3,16,16,8,128]{4,1,3,2,0:T(8,128)}, u32[]{:S(2)}) copy-start(f32[3,16,16,8,128]{4,1,3,2,0:T(8,128)} %get-tuple-element.248) | copy-start | bytes 9437188
  579.1 3.6 copy-start.6
where the time goes:
time: 597 us; the launch traced here: 585 us
  local copies, waits for them, and re-layouts  215 us (36%)
  blocking collectives  187 us (31%)
  other arithmetic  67.4 us (11%)
  waiting for transfers between devices  65.5 us (11%)
  starting transfers between devices  24.3 us (4%)
  matrix products  20.7 us (3%)
    psum x1, blocking collectives, body(): line_sum_z, centred_z = lax.psum((sum_z, moment_z), 'gz')  139 us
    unnamed x28, local copies, waits for them, and re-layouts  91.9 us
    all_to_all x1, waiting for transfers between devices, body(): lax.all_to_all(fields_z, 'gz', split_axis=1, concat_axis=3, tiled=True)  64.8 us
    all_gather x2, blocking collectives, entering(): everything = lax.all_gather(array, axis)  33.7 us
    all_to_all x2, local copies, waits for them, and re-layouts, body(): lax.all_to_all(solved_lines_z, 'gz', split_axis=3, concat_axis=1, tiled=T...  25.8 us
    reshape x1, local copies, waits for them, and re-layouts, whole_lines(): couple(solved, inverse, axis_at, edge_before, edge_after)  22.5 us
    all_to_all x1, other arithmetic, body(): lax.all_to_all(solved_lines_z, 'gz', split_axis=3, concat_axis=1, tiled=T...  19.4 us
    all_to_all x2, local copies, waits for them, and re-layouts, body(): lax.all_to_all(fields_z, 'gz', split_axis=1, concat_axis=3, tiled=True)  16.3 us
  transfers between devices with their start and end apart: 6, of which 2 were waited for; matrix products, arithmetic and copies ran while one was open for 8% of the time, Pallas kernels for 0%

commit v1 on v0

v1 whole, which is shorter than its diff:
```python
import math

import jax
import jax.numpy as jnp
import numpy as np
from jax import lax
from jax.experimental import pallas as pl
from jax.experimental.pallas import tpu as pltpu
from jax.sharding import PartitionSpec as P

ALPHA = 1.0 / 3.0
COEF_A = 14.0 / 9.0
COEF_B = 1.0 / 9.0
LANES = 128
F32 = jnp.float32
BF16 = jnp.bfloat16

RHO = (-1.0 + math.sqrt(1.0 - 4.0 * ALPHA * ALPHA)) / (2.0 * ALPHA)


def kernel_weights():
    reach = 400
    k = np.arange(-reach, reach + 1)
    green = RHO ** np.abs(k).astype(np.float64) / math.sqrt(1.0 - 4.0 * ALPHA * ALPHA)

    def shifted(s):
        out = np.zeros_like(green)
        if s >= 0:
            out[s:] = green[: len(green) - s]
        else:
            out[:s] = green[-s:]
        return out

    direct = 0.5 * COEF_A * (shifted(-1) - shifted(1)) + 0.25 * COEF_B * (shifted(-2) - shifted(2))
    total = np.concatenate([[0.0], np.cumsum(direct)])
    return {m: total[m + reach] for m in range(-2, 4)}


_W = kernel_weights()
NEAR = _W[1]
TAIL = _W[2] / RHO**2
KAPPA = TAIL * RHO * RHO
REACH = 96


def h_of(m):
    m = np.asarray(m)
    m = np.where(m <= 0, 1 - m, m)
    return np.where(m == 1, NEAR, TAIL * RHO ** m.astype(np.float64))


def split_np(x):
    hi = x.astype(BF16)
    lo = (x - hi.astype(np.float64)).astype(BF16)
    return hi, lo


def going_up(length):
    j = np.arange(length)
    w = (RHO - 1.0) * RHO ** (length - j).astype(np.float64)
    w[-1] = RHO**2
    return w


def going_down(length):
    return going_up(length)[::-1] * -1.0


def z_matrices():
    j = np.arange(LANES)
    inner = h_of(j[None, :] - j[:, None])
    inner[LANES - 1] = 0.0
    inner_hi, inner_lo = split_np(inner)
    rim = np.stack(
        [
            h_of(j + 1),
            TAIL * RHO ** j.astype(np.float64),
            h_of(LANES - j),
            TAIL * RHO ** (LANES - 1 - j).astype(np.float64),
        ]
    )
    rim_hi, rim_lo = split_np(rim)
    pad = np.zeros((LANES - 12, LANES), BF16)
    first = np.concatenate([inner_hi, inner_hi], 0)
    second = np.concatenate([inner_lo, rim_hi, rim_hi, rim_lo, pad], 0)
    return np.stack([first, second])


def sum_matrices():
    j = np.arange(LANES)
    lower = (j[:, None] < j[None, :]) + 0.5 * (j[:, None] == j[None, :])
    ones = np.ones((3, LANES))
    slope = -np.broadcast_to(j, (3, LANES))
    pad = np.zeros((LANES - 6, LANES))
    first = np.concatenate([lower, lower], 0)
    second = np.concatenate([lower, ones, slope, pad], 0)
    return np.stack([first, second]).astype(BF16)


def split2(x):
    hi = x.astype(BF16)
    return hi, (x - hi.astype(F32)).astype(BF16)


def split3(x):
    hi = x.astype(BF16)
    rest = x - hi.astype(F32)
    mid = rest.astype(BF16)
    return hi, mid, (rest - mid.astype(F32)).astype(BF16)


def dot(a, b):
    return lax.dot_general(a, b, (((1,), (0,)), ((), ())), preferred_element_type=F32)


def product(values, name):
    out = values[name[0]]
    for c in name[1:]:
        out = out * values[c]
    return out


COMP = {"u": 0, "v": 1, "w": 2}


def edges_call(velocity, x_sums, x_cells, z_sums, z_cells):
    comps, nx, ny, nz = velocity.shape
    step = 32
    steps = nx // step
    reach = min(REACH // step, steps)
    sub = LANES // ny
    chunks = nx // sub
    per = step // sub
    names_x = sorted(set("".join(x_sums + x_cells)))
    names_z = sorted(set("".join(z_sums + z_cells)))
    nqx = len(x_sums) + len(x_cells)
    nqz = len(z_sums) + len(z_cells)
    up_x = going_up(nx)
    down_x = going_down(nx)
    cut = min(REACH, nz)

    def body(v_ref, w_ref, xu_ref, xd_ref, zu_ref, zd_ref):
        i = pl.program_id(0)

        def x_part(ref, weights, rows_of, cell_at, start):
            for blk, at in rows_of:

                @pl.when(i == at)
                def _(blk=blk, at=at):
                    for q, name in enumerate(x_sums):
                        acc = None
                        for k in range(step):
                            vals = {c: v_ref[COMP[c], k] for c in set(name)}
                            term = product(vals, name) * np.float32(weights[at * step + k])
                            acc = term if acc is None else acc + term
                        if at == start:
                            ref[q] = acc
                        else:
                            ref[q] = ref[q] + acc
                    if at * step <= cell_at < (at + 1) * step:
                        for q, name in enumerate(x_cells):
                            ref[len(x_sums) + q] = v_ref[COMP[name], cell_at - at * step]

        ups = list(range(steps - reach, steps))
        downs = list(range(reach))
        x_part(xu_ref, up_x, list(enumerate(ups)), nx - 1, ups[0])
        x_part(xd_ref, down_x, list(enumerate(downs)), 0, downs[0])

        for s in range(per):
            at = i * per + s
            t = {}
            for c in names_z:
                t[c] = v_ref[COMP[c], s * sub : (s + 1) * sub].reshape(LANES, nz).T
            for q, name in enumerate(z_sums):
                f = product(t, name)
                up = jnp.sum(f[nz - cut :] * w_ref[0, nz - cut :], axis=0, keepdims=True)
                down = jnp.sum(f[:cut] * w_ref[1, :cut], axis=0, keepdims=True)
                zu_ref[q, pl.ds(at, 1), :] = up
                zd_ref[q, pl.ds(at, 1), :] = down
            for q, name in enumerate(z_cells):
                zu_ref[len(z_sums) + q, pl.ds(at, 1), :] = t[name][nz - 1 : nz]
                zd_ref[len(z_sums) + q, pl.ds(at, 1), :] = t[name][0:1]

    weights = np.stack([going_up(nz), going_down(nz)]).astype(np.float32)
    weights = jnp.asarray(np.broadcast_to(weights[:, :, None], (2, nz, LANES)))
    xs = jax.ShapeDtypeStruct((nqx, ny, nz), F32)
    zs = jax.ShapeDtypeStruct((nqz, chunks, LANES), F32)
    xspec = pl.BlockSpec(xs.shape, lambda i: (0, 0, 0))
    zspec = pl.BlockSpec(zs.shape, lambda i: (0, 0, 0))
    return pl.pallas_call(
        body,
        grid=(steps,),
        in_specs=[
            pl.BlockSpec((comps, step, ny, nz), lambda i: (0, i, 0, 0)),
            pl.BlockSpec(weights.shape, lambda i: (0, 0, 0)),
        ],
        out_specs=[xspec, xspec, zspec, zspec],
        out_shape=[xs, xs, zs, zs],
        name="edges",
        cost_estimate=pl.CostEstimate(
            flops=40 * len(z_sums) * nx * ny * nz, transcendentals=0, bytes_accessed=4 * comps * nx * ny * nz
        ),
    )(velocity, weights)


def x_derivative(read, write, scratch, nx, sum_before, cell_before, sum_after, cell_after):
    unroll = 8
    blocks = nx // unroll

    def forward(b, carry):
        state, before, here = carry
        base = b * unroll
        for k in range(unroll):
            i = base + k
            if k == unroll - 1:
                nxt = jnp.where(b == blocks - 1, cell_after, read(jnp.minimum(i + 1, nx - 1)))
            else:
                nxt = read(i + 1)
            scratch[i] = state + NEAR * (nxt - before)
            state = RHO * state + KAPPA * (here - before)
            before, here = here, nxt
        return state, before, here

    lax.fori_loop(0, blocks, forward, (TAIL * sum_before, cell_before, read(0)))

    def backward(b, carry):
        state, after = carry
        base = (blocks - 1 - b) * unroll
        for k in reversed(range(unroll)):
            i = base + k
            here = read(i)
            write(i, scratch[i] + state)
            state = RHO * state + KAPPA * (after - here)
            after = here
        return state, after

    lax.fori_loop(0, blocks, backward, (TAIL * sum_after, cell_after))


def rim_rows(scratch, sum_before, cell_before, first, last, sum_after, cell_after):
    terms = [first - cell_before, sum_before, cell_after - last, sum_after]
    for q, term in enumerate(terms):
        hi = term.astype(BF16).astype(F32)
        lo = (term - hi).astype(BF16).astype(F32)
        scratch[:, q, :] = hi
        scratch[:, 4 + q, :] = lo
        scratch[:, 8 + q, :] = hi


def z_derivative(read, write, rim, mats, chunks, together=2):
    lane = lax.broadcasted_iota(jnp.int32, (LANES, LANES), 1)
    keep = lane < LANES - 1

    def step(b, _):
        his, los, rims = [], [], []
        for k in range(together):
            c = b * together + k
            f = read(c)
            e = jnp.where(keep, pltpu.roll(f, LANES - 1, 1) - f, 0.0)
            hi, lo = split2(e)
            his.append(hi)
            los.append(lo)
            rims.append(rim[c].T.astype(BF16))
        hi = jnp.concatenate(his, 0)
        lo = jnp.concatenate(los, 0)
        st = jnp.concatenate(rims, 0)
        g = dot(jnp.concatenate([hi, lo], 1), mats[0]) + dot(jnp.concatenate([hi, st], 1), mats[1])
        for k in range(together):
            write(b * together + k, g[k * LANES : (k + 1) * LANES])
        return 0

    lax.fori_loop(0, chunks // together, step, 0)


def whole(shape):
    return pl.BlockSpec(shape, lambda *_: (0,) * len(shape))


def comp_spec(shape, at):
    return pl.BlockSpec((None,) + tuple(shape[1:]), lambda *g: (at(*g), 0, 0, 0))


def params():
    return pltpu.CompilerParams(vmem_limit_bytes=40 * 2**20)


def cost(fields, size):
    return pl.CostEstimate(flops=fields * size * 512, transcendentals=0, bytes_accessed=fields * size * 8)


def slopes_first(velocity, x_halo, z_halo, mats):
    _, nx, ny, nz = velocity.shape
    sub = LANES // ny
    chunks = nx // sub

    def body(u_ref, w_ref, xl, xr, zl, zr, zown_l, zown_r, m_ref, gx, gz, sx, sz, scratch, rim):
        rim[...] = jnp.zeros_like(rim)
        rim_rows(rim, zl[0], zl[1], zown_l[1], zown_r[1], zr[0], zr[1])

        def read(c):
            return w_ref[pl.ds(c * sub, sub)].reshape(LANES, nz)

        def write(c, g):
            gz[pl.ds(c * sub, sub)] = g.reshape(sub, ny, nz)

        z_derivative(read, write, rim, m_ref, chunks)

        def write_x(i, g):
            gx[i] = g

        x_derivative(lambda i: u_ref[i], write_x, scratch, nx, xl[0], xl[1], xr[0], xr[1])

        def add(b, carry):
            total, moment = carry
            for k in range(8):
                g = gz[b * 8 + k]
                at = (b * 8 + k).astype(F32) - 0.5 * (nx - 1)
                total = total + g
                moment = moment + at * g
            return total, moment

        zero = jnp.zeros((ny, nz), F32)
        total, moment = lax.fori_loop(0, nx // 8, add, (zero, zero))
        sx[0] = total
        sx[1] = moment

        at = lax.broadcasted_iota(jnp.int32, (nz, LANES), 0).astype(F32) - 0.5 * (nz - 1)
        for c in range(chunks):
            t = gx[c * sub : (c + 1) * sub].reshape(LANES, nz).T
            sz[0, c : c + 1, :] = jnp.sum(t, axis=0, keepdims=True)
            sz[1, c : c + 1, :] = jnp.sum(t * at, axis=0, keepdims=True)

    full = jax.ShapeDtypeStruct(velocity.shape, F32)
    sx = jax.ShapeDtypeStruct((2, ny, nz), F32)
    sz = jax.ShapeDtypeStruct((2, chunks, LANES), F32)
    small = [*x_halo, *z_halo, mats]
    return pl.pallas_call(
        body,
        grid=(1,),
        in_specs=[comp_spec(velocity.shape, lambda i: 0), comp_spec(velocity.shape, lambda i: 2)]
        + [whole(a.shape) for a in small],
        out_specs=[
            comp_spec(velocity.shape, lambda i: 0),
            comp_spec(velocity.shape, lambda i: 2),
            whole(sx.shape),
            whole(sz.shape),
        ],
        out_shape=[full, full, sx, sz],
        scratch_shapes=[pltpu.VMEM((nx, ny, nz), F32), pltpu.VMEM((chunks, LANES, LANES), F32)],
        compiler_params=params(),
        name="slopes_first",
        cost_estimate=cost(2, nx * ny * nz),
    )(velocity, velocity, *small)


def slopes_x(velocity, x_halo, gx):
    _, nx, ny, nz = velocity.shape

    def body(f_ref, xl, xr, _, out, scratch):
        c = pl.program_id(0)

        def write(i, g):
            out[i] = g

        x_derivative(
            lambda i: f_ref[i], write, scratch, nx, xl[c], xl[6 + c], xr[c], xr[6 + c]
        )

    return pl.pallas_call(
        body,
        grid=(2,),
        in_specs=[comp_spec(velocity.shape, lambda c: c + 1)]
        + [whole(a.shape) for a in x_halo]
        + [pl.BlockSpec(memory_space=pl.ANY)],
        out_specs=comp_spec(velocity.shape, lambda c: c + 1),
        out_shape=jax.ShapeDtypeStruct(velocity.shape, F32),
        scratch_shapes=[pltpu.VMEM((nx, ny, nz), F32)],
        input_output_aliases={3: 0},
        compiler_params=params(),
        name="slopes_x",
        cost_estimate=cost(2, nx * ny * nz),
    )(velocity, *x_halo, gx)


def slopes_z(velocity, z_halo, mats, gz):
    _, nx, ny, nz = velocity.shape
    sub = LANES // ny
    chunks = nx // sub

    def body(f_ref, zl, zr, zown_l, zown_r, m_ref, _, out, rim):
        c = pl.program_id(0)

        @pl.when(c == 0)
        def _():
            rim[...] = jnp.zeros_like(rim)

        rim_rows(rim, zl[c], zl[5 + c], zown_l[5 + c], zown_r[5 + c], zr[c], zr[5 + c])

        def read(k):
            return f_ref[pl.ds(k * sub, sub)].reshape(LANES, nz)

        def write(k, g):
            out[pl.ds(k * sub, sub)] = g.reshape(sub, ny, nz)

        z_derivative(read, write, rim, m_ref, chunks)

    return pl.pallas_call(
        body,
        grid=(2,),
        in_specs=[comp_spec(velocity.shape, lambda c: c)]
        + [whole(a.shape) for a in (*z_halo, mats)]
        + [pl.BlockSpec(memory_space=pl.ANY)],
        out_specs=comp_spec(velocity.shape, lambda c: c),
        out_shape=jax.ShapeDtypeStruct(velocity.shape, F32),
        scratch_shapes=[pltpu.VMEM((chunks, LANES, LANES), F32)],
        input_output_aliases={6: 0},
        compiler_params=params(),
        name="slopes_z",
        cost_estimate=cost(2, nx * ny * nz),
    )(velocity, *z_halo, mats, gz)


def divergence(velocity, x_halo, z_halo, mats):
    _, nx, ny, nz = velocity.shape
    sub = LANES // ny
    chunks = nx // sub

    def body(f_ref, u_ref, w_ref, xl, xr, zl, zr, zown_l, zown_r, m_ref, out, scratch, rim):
        c = pl.program_id(0)

        @pl.when(c == 0)
        def _():
            rim[...] = jnp.zeros_like(rim)

        rim_rows(
            rim,
            zl[2 + c],
            zl[7] * zl[5 + c],
            zown_l[7] * zown_l[5 + c],
            zown_r[7] * zown_r[5 + c],
            zr[2 + c],
            zr[7] * zr[5 + c],
        )

        def read(k):
            at = pl.ds(k * sub, sub)
            return (w_ref[at] * f_ref[at]).reshape(LANES, nz)

        def write(k, g):
            out[pl.ds(k * sub, sub)] = g.reshape(sub, ny, nz)

        z_derivative(read, write, rim, m_ref, chunks)

        def write_x(i, g):
            out[i] = out[i] + g

        x_derivative(
            lambda i: u_ref[i] * f_ref[i],
            write_x,
            scratch,
            nx,
            xl[2 + c],
            xl[5] * xl[5 + c],
            xr[2 + c],
            xr[5] * xr[5 + c],
        )

    return pl.pallas_call(
        body,
        grid=(3,),
        in_specs=[
            comp_spec(velocity.shape, lambda c: c),
            comp_spec(velocity.shape, lambda c: 0),
            comp_spec(velocity.shape, lambda c: 2),
        ]
        + [whole(a.shape) for a in (*x_halo, *z_halo, mats)],
        out_specs=comp_spec(velocity.shape, lambda c: c),
        out_shape=jax.ShapeDtypeStruct(velocity.shape, F32),
        scratch_shapes=[pltpu.VMEM((nx, ny, nz), F32), pltpu.VMEM((chunks, LANES, LANES), F32)],
        compiler_params=params(),
        name="divergence",
        cost_estimate=cost(6, nx * ny * nz),
    )(velocity, velocity, velocity, *x_halo, *z_halo, mats)


def rebuild(gx, gz, x_terms, z_terms, mats, total_x, total_z):
    _, nx, ny, nz = gx.shape
    sub = LANES // ny
    chunks = nx // sub
    scale_x = -1.0 / math.sqrt(total_x)
    scale_z = -1.0 / math.sqrt(total_z)

    def body(u_ref, w_ref, xt, zt, m_ref, out, rim):
        rim[...] = jnp.zeros_like(rim)
        for q in range(2):
            for p, part in enumerate(split3(zt[q])):
                rim[:, 3 * q + p, :] = part.astype(F32)

        mean = xt[1]

        def along_x(b, acc):
            for k in range(8):
                i = b * 8 + k
                g = w_ref[i]
                out[0, i] = scale_x * (acc + 0.5 * g)
                acc = acc + (g - mean)
            return acc

        lax.fori_loop(0, nx // 8, along_x, xt[0])

        def along_z(b, _):
            for k in range(2):
                c = b * 2 + k
                at = pl.ds(c * sub, sub)
                hi, mid, lo = split3(u_ref[at].reshape(LANES, nz))
                st = rim[c].T.astype(BF16)
                g = dot(jnp.concatenate([hi, mid], 1), m_ref[0]) + dot(
                    jnp.concatenate([lo, st], 1), m_ref[1]
                )
                out[1, at] = (scale_z * g).reshape(sub, ny, nz)
            return 0

        lax.fori_loop(0, chunks // 2, along_z, 0)

    small = (x_terms, z_terms, mats)
    shape = (2,) + gx.shape[1:]
    return pl.pallas_call(
        body,
        grid=(1,),
        in_specs=[comp_spec(gx.shape, lambda i: 0), comp_spec(gx.shape, lambda i: 2)]
        + [whole(a.shape) for a in small],
        out_specs=whole(shape),
        out_shape=jax.ShapeDtypeStruct(shape, F32),
        scratch_shapes=[pltpu.VMEM((chunks, LANES, LANES), F32)],
        compiler_params=params(),
        name="rebuild",
        cost_estimate=cost(2, nx * ny * nz),
    )(gx, gz, *small)


def swap(array, axis, up, down):
    n = lax.axis_size(axis)
    before = lax.ppermute(up, axis, [(i, (i + 1) % n) for i in range(n)])
    after = lax.ppermute(down, axis, [((i + 1) % n, i) for i in range(n)])
    return before, after


def level(axis, terms, count, stride):
    n = lax.axis_size(axis)
    mine = (lax.axis_index(axis) // stride) % count
    parts = []
    for k in range(1, count):
        pairs = []
        for i in range(n):
            own = (i // stride) % count
            pairs.append((i, i + ((own + k) % count - own) * stride))
        parts.append(((mine - k) % count < mine, lax.ppermute(terms, axis, pairs)))
    return parts


def combine(terms, before, parts):
    for lower, part in parts:
        before = before + jnp.where(lower, part[0], 0.0)
        terms = terms + part
    return terms, before


def line_terms(terms, before, start, total_len):
    mean = terms[0] / total_len
    offset = before - (start + 0.5) * mean + terms[1] / total_len
    return jnp.stack([offset, mean])


def body(velocity):
    _, nx, ny, nz = velocity.shape
    size_x = lax.axis_size("gx")
    size_z = lax.axis_size("gz")
    total_x = nx * size_x
    total_z = nz * size_z
    mats = jnp.asarray(z_matrices())
    sums = jnp.asarray(sum_matrices())

    xu, xd, zu, zd = edges_call(velocity, ["u"], ["u"], ["w"], ["w"])
    x_first = swap(None, "gx", xu, xd)
    z_first = swap(None, "gz", zu, zd)
    xu2, xd2, zu2, zd2 = edges_call(
        velocity,
        ["v", "w", "uu", "uv", "uw"],
        ["u", "v", "w"],
        ["u", "v", "wu", "wv", "ww"],
        ["u", "v", "w"],
    )
    x_rest = swap(None, "gx", xu2, xd2)
    z_rest = (*swap(None, "gz", zu2, zd2), zd2, zu2)

    gx, gz, sx, sz = slopes_first(velocity, x_first, (*z_first, zd, zu), mats)

    x0 = (lax.axis_index("gx") * nx).astype(F32)
    z0 = (lax.axis_index("gz") * nz).astype(F32)
    centre_x = x0 + (0.5 * (nx - 1) - 0.5 * (total_x - 1))
    centre_z = z0 + (0.5 * (nz - 1) - 0.5 * (total_z - 1))
    tx = jnp.stack([sx[0], sx[1] + centre_x * sx[0]])
    tz = jnp.stack([sz[0], sz[1] + centre_z * sz[0]])

    px = level("gx", tx, 2, 1)
    pz = level("gz", tz, 4, 1)
    gx = slopes_x(velocity, x_rest, gx)
    gz = slopes_z(velocity, z_rest, mats, gz)
    tx, bx = combine(tx, 0.0, px)
    tz, bz = combine(tz, 0.0, pz)
    px = level("gx", tx, size_x // 2, 2)
    pz = level("gz", tz, size_z // 4, 4)
    convect = divergence(velocity, x_rest, z_rest, mats)
    tx, bx = combine(tx, bx, px)
    tz, bz = combine(tz, bz, pz)
    rebuilt = rebuild(
        gx,
        gz,
        line_terms(tx, bx, x0, total_x),
        line_terms(tz, bz, z0, total_z),
        sums,
        total_x,
        total_z,
    )
    return (gx, gz, convect, rebuilt)


def solution(mesh):
    spec = P(None, "gx", None, "gz")
    return jax.shard_map(
        body, mesh=mesh, in_specs=(spec,), out_specs=(spec,) * 4, check_vma=False
    )
```

time: 597 us -> 76.9 us (0.13); the launches traced: 585 us -> 76.6 us
  local copies, waits for them, and re-layouts: 215 us -> 3.37 us
  blocking collectives: 187 us -> 0 us
  other arithmetic: 67.4 us -> 0.08 us
  waiting for transfers between devices: 65.5 us -> 5.78 us
  Pallas kernels: 0 us -> 42.6 us
  matrix products: 20.7 us -> 0 us
    psum x2 -> x0, blocking collectives: 154 us -> none  [the longest x1 139 us: body(): line_sum_z, centred_z = lax.psum((sum_z, moment_z), 'gz')]
    unnamed x28 -> x22, local copies, waits for them, and re-layouts: 91.9 us -> 1.94 us
    all_to_all x2 -> x0, waiting for transfers between devices: 64.8 us -> none  [the longest x1 64.8 us: body(): lax.all_to_all(fields_z, 'gz', split_axis=1, concat_axis=3, tiled=True)]
    slice x15 -> x0, local copies, waits for them, and re-layouts: 46.1 us -> none  [the longest x3 14 us: couple(): lax.slice_in_dim(last_cells, 0, count - 1, axis=axis_at)]
    pallas_call x0 -> x7, Pallas kernels: none -> 42.6 us  [the longest x1 12.2 us: divergence(): pl.pallas_call(body, grid=(3,), in_specs=[comp_spec(velocity.shape, lambd...]
    all_to_all x4 -> x0, local copies, waits for them, and re-layouts: 42.1 us -> none  [the longest x2 25.8 us: body(): lax.all_to_all(solved_lines_z, 'gz', split_axis=3, concat_axis=1, tiled=T...]
    all_gather x2 -> x0, blocking collectives: 33.7 us -> none  [entering(): everything = lax.all_gather(array, axis)]
    reshape x1 -> x0, local copies, waits for them, and re-layouts: 22.5 us -> none  [whole_lines(): couple(solved, inverse, axis_at, edge_before, edge_after)]
  transfers between devices with their start and end apart: 6 -> 18, of which waited for: 2 -> 6; matrix products, arithmetic and copies ran while one was open for 8% -> 0% of each run, Pallas kernels for 0% -> 19%
where the time goes in v1:
time: 76.9 us; the launch traced here: 76.6 us
  Pallas kernels  42.6 us (55%)
  starting transfers between devices  23.9 us (31%)
  waiting for transfers between devices  5.78 us (8%)
  local copies, waits for them, and re-layouts  3.37 us (4%)
  between operations  0.8 us (1%)
    pallas_call x1, Pallas kernels, divergence(): pl.pallas_call(body, grid=(3,), in_specs=[comp_spec(velocity.shape, lambd...  12.2 us
    pallas_call x2, Pallas kernels, edges_call(): pl.pallas_call(body, grid=(steps,), in_specs=[pl.BlockSpec((comps, step,...  11.8 us
    ppermute x4, starting transfers between devices, swap(): after = lax.ppermute(down, axis, [((i + 1) % n, i) for i in range(n)])  9.19 us
    ppermute x10, starting transfers between devices, level(): parts.append(((mine - k) % count < mine, lax.ppermute(terms, axis, pairs)))  9.12 us
    pallas_call x1, Pallas kernels, slopes_z(): pl.pallas_call(body, grid=(2,), in_specs=[comp_spec(velocity.shape, lambd...  5.93 us
    ppermute x4, starting transfers between devices, swap(): before = lax.ppermute(up, axis, [(i, (i + 1) % n) for i in range(n)])  5.58 us
    pallas_call x1, Pallas kernels, slopes_first(): pl.pallas_call(body, grid=(1,), in_specs=[comp_spec(velocity.shape, lambd...  5.41 us
    pallas_call x1, Pallas kernels, rebuild(): pl.pallas_call(body, grid=(1,), in_specs=[comp_spec(gx.shape, lambda i: 0...  3.93 us
  transfers between devices with their start and end apart: 18, of which 6 were waited for; matrix products, arithmetic and copies ran while one was open for 0% of the time, Pallas kernels for 19%

profile of v1, /device:TPU:0, one launch (start us, length us, event | category | flops | bytes accessed | tf_op | source)
XLA Modules:
  0.0 76.6 jit_solution(3586759237373478507)
XLA Ops:
  0.6 1.4 %jit_solution_.6.w_ref = f32[2,128,128]{2,1,0:T(8,128)} broadcast(f32[2,128]{1,0:T(2,128)} %constant.155.clone), dimensions={0,1} | broadcast | bytes 132096 | tf_op jit(solution)
  2.1 5.7 %edges.3 = (f32[2,8,128]{2,1,0:T(8,128)}, f32[2,8,128]{2,1,0:T(8,128)}, f32[2,16,128]{2,1,0:T(8,128)}, f32[2,16,128]{2,1,0:T(8,128)}) custom-call(f32[3,256,8,128]{3,2,1,0:T(8,128)} %w_ref.5, f32[2,128,128]{2,1,0:T(8,128)} %jit_solution_.6.w_ref), custom_call_target="tpu_custom_call" | custom-call | flops 10485760 | bytes 3145728 | tf_op jit(solution)/shard_map/edges/pallas_call | solution.py:190
  7.8 0.0 copy-start.8
  7.8 2.1 %collective-permute-start.4 = (f32[2,16,128]{2,1,0:T(8,128)}, f32[2,16,128]{2,1,0:T(8,128)S(1)}, u32[]{:S(2)}, u32[]{:S(2)}) collective-permute-start(f32[2,16,128]{2,1,0:T(8,128)} %get-tuple-element.20.zown_r), channel_id=1, source_target_pairs={{0,1},{1,2},{2,3},{3,4},{4,5},{5,6},{6,7},{7,8},{8,9},{9,10},{10,1... | collective-permute-start | bytes 49160 | tf_op jit(solution)/shard_map/ppermute | solution.py:543
  9.8 4.7 %collective-permute-start.5 = (f32[2,16,128]{2,1,0:T(8,128)}, f32[2,16,128]{2,1,0:T(8,128)S(1)}, u32[]{:S(2)}, u32[]{:S(2)}) collective-permute-start(f32[2,16,128]{2,1,0:T(8,128)} %get-tuple-element.21.zown_l), channel_id=1, source_target_pairs={{1,0},{2,1},{3,2},{4,3},{5,4},{6,5},{7,6},{8,7},{9,8},{10,9},{11,1... | collective-permute-start | bytes 49160 | tf_op jit(solution)/shard_map/ppermute | solution.py:544
  14.5 6.1 %edges.2 = (f32[8,8,128]{2,1,0:T(8,128)}, f32[8,8,128]{2,1,0:T(8,128)}, f32[8,16,128]{2,1,0:T(8,128)}, f32[8,16,128]{2,1,0:T(8,128)}) custom-call(f32[3,256,8,128]{3,2,1,0:T(8,128)} %w_ref.5, f32[2,128,128]{2,1,0:T(8,128)} %jit_solution_.6.w_ref), custom_call_target="tpu_custom_call" | custom-call | flops 52428800 | bytes 3145728 | tf_op jit(solution)/shard_map/edges/pallas_call | solution.py:190
  20.6 1.6 %collective-permute-start.2 = (f32[2,8,128]{2,1,0:T(8,128)S(1)}, f32[2,8,128]{2,1,0:T(8,128)S(1)}, u32[]{:S(2)}, u32[]{:S(2)}) collective-permute-start(f32[2,8,128]{2,1,0:T(8,128)S(1)} %copy-done.10), channel_id=1, source_target_pairs={{0,16},{16,32},{32,48},{48,64},{64,80},{80,96},{96,112},{112,0},{1... | collective-permute-start | bytes 24584 | tf_op jit(solution)/shard_map/ppermute | solution.py:543
  22.2 1.4 %collective-permute-start.3 = (f32[2,8,128]{2,1,0:T(8,128)S(1)}, f32[2,8,128]{2,1,0:T(8,128)S(1)}, u32[]{:S(2)}, u32[]{:S(2)}) collective-permute-start(f32[2,8,128]{2,1,0:T(8,128)S(1)} %copy-done.9), channel_id=1, source_target_pairs={{16,0},{32,16},{48,32},{64,48},{80,64},{96,80},{112,96},{0,112},{1... | collective-permute-start | bytes 24584 | tf_op jit(solution)/shard_map/ppermute | solution.py:544
  23.6 1.9 %collective-permute-done.2.xl = f32[2,8,128]{2,1,0:T(8,128)S(1)} collective-permute-done((f32[2,8,128]{2,1,0:T(8,128)S(1)}, f32[2,8,128]{2,1,0:T(8,128)S(1)}, u32[]{:S(2)}, u32[]{:S(2)}) %collective-permute-start.2) | collective-permute-done | bytes 8224 | tf_op jit(solution)/shard_map/ppermute | solution.py:543
  25.5 5.4 %slopes_first.1 = (f32[3,256,8,128]{3,2,1,0:T(8,128)}, f32[3,256,8,128]{3,2,1,0:T(8,128)}, f32[2,8,128]{2,1,0:T(8,128)S(1)}, f32[2,16,128]{2,1,0:T(8,128)S(1)}) custom-call(f32[3,256,8,128]{3,2,1,0:T(8,128)S(1)} %copy-done, f32[3,256,8,128]{3,2,1,0:T(8,128)S(1)} %copy-done, f32[2,8,128]{2,1,0:T(8,128)S(1)} %collective-permute-done.2.xl, ...), custom_call_target="tpu_custom_call" | custom-call | flops 268435456 | bytes 4194304 | tf_op jit(solution)/shard_map/slopes_first/pallas_call | solution.py:337
  31.0 0.5 collective-permute-start.8
  31.5 0.1 collective-permute-start.13
  31.5 0.7 collective-permute-done.8
  32.3 1.2 %collective-permute-start.12 = (f32[2,16,128]{2,1,0:T(8,128)S(1)}, f32[2,16,128]{2,1,0:T(8,128)S(1)}, u32[]{:S(2)}, u32[]{:S(2)}) collective-permute-start(f32[2,16,128]{2,1,0:T(8,128)S(1)} %pad_maximum_fusion), channel_id=1, source_target_pairs={{0,1},{1,2},{2,3},{3,0},{4,5},{5,6},{6,7},{7,4},{8,9},{9,10},{10,1... | collective-permute-start | bytes 49160 | tf_op jit(solution)/shard_map/ppermute | solution.py:557
  33.5 1.7 %collective-permute-done.14 = f32[2,16,128]{2,1,0:T(8,128)S(1)} collective-permute-done((f32[2,16,128]{2,1,0:T(8,128)S(1)}, f32[2,16,128]{2,1,0:T(8,128)S(1)}, u32[]{:S(2)}, u32[]{:S(2)}) %collective-permute-start.14) | collective-permute-done | bytes 16416 | tf_op jit(solution)/shard_map/ppermute | solution.py:557
  35.2 2.3 %collective-permute-start.11 = (f32[2,8,128]{2,1,0:T(8,128)S(1)}, f32[2,8,128]{2,1,0:T(8,128)S(1)}, u32[]{:S(2)}, u32[]{:S(2)}) collective-permute-start(f32[2,8,128]{2,1,0:T(8,128)S(1)} %fusion.12), channel_id=1, source_target_pairs={{0,96},{16,112},{32,0},{48,16},{64,32},{80,48},{96,64},{112,80},{1... | collective-permute-start | bytes 24584 | tf_op jit(solution)/shard_map/ppermute | solution.py:557
  37.5 1.5 %collective-permute-start.10 = (f32[2,8,128]{2,1,0:T(8,128)S(1)}, f32[2,8,128]{2,1,0:T(8,128)S(1)}, u32[]{:S(2)}, u32[]{:S(2)}) collective-permute-start(f32[2,8,128]{2,1,0:T(8,128)S(1)} %fusion.12), channel_id=1, source_target_pairs={{0,64},{16,80},{32,96},{48,112},{64,0},{80,16},{96,32},{112,48},{1... | collective-permute-start | bytes 24584 | tf_op jit(solution)/shard_map/ppermute | solution.py:557
  39.0 1.1 %collective-permute-start.9 = (f32[2,8,128]{2,1,0:T(8,128)S(1)}, f32[2,8,128]{2,1,0:T(8,128)S(1)}, u32[]{:S(2)}, u32[]{:S(2)}) collective-permute-start(f32[2,8,128]{2,1,0:T(8,128)S(1)} %fusion.12), channel_id=1, source_target_pairs={{0,32},{16,48},{32,64},{48,80},{64,96},{80,112},{96,0},{112,16},{1... | collective-permute-start | bytes 24584 | tf_op jit(solution)/shard_map/ppermute | solution.py:557
  40.1 1.9 %collective-permute-start.6 = (f32[8,16,128]{2,1,0:T(8,128)S(1)}, f32[8,16,128]{2,1,0:T(8,128)S(1)}, u32[]{:S(2)}, u32[]{:S(2)}) collective-permute-start(f32[8,16,128]{2,1,0:T(8,128)S(1)} %copy-done.4), channel_id=1, source_target_pairs={{0,1},{1,2},{2,3},{3,4},{4,5},{5,6},{6,7},{7,8},{8,9},{9,10},{10,1... | collective-permute-start | bytes 196616 | tf_op jit(solution)/shard_map/ppermute | solution.py:543
  42.0 0.7 collective-permute-done.10
  42.7 3.2 %collective-permute-start.7 = (f32[8,16,128]{2,1,0:T(8,128)S(1)}, f32[8,16,128]{2,1,0:T(8,128)S(1)}, u32[]{:S(2)}, u32[]{:S(2)}) collective-permute-start(f32[8,16,128]{2,1,0:T(8,128)S(1)} %copy-done.5), channel_id=1, source_target_pairs={{1,0},{2,1},{3,2},{4,3},{5,4},{6,5},{7,6},{8,7},{9,8},{10,9},{11,1... | collective-permute-start | bytes 196616 | tf_op jit(solution)/shard_map/ppermute | solution.py:544
  45.8 0.8 %collective-permute-start.17 = (f32[2,16,128]{2,1,0:T(8,128)S(1)}, f32[2,16,128]{2,1,0:T(8,128)S(1)}, u32[]{:S(2)}, u32[]{:S(2)}) collective-permute-start(f32[2,16,128]{2,1,0:T(8,128)S(1)} %add_add_fusion.1), channel_id=1, source_target_pairs={{0,12},{1,13},{2,14},{3,15},{4,0},{5,1},{6,2},{7,3},{8,4},{9,5},{1... | collective-permute-start | bytes 49160 | tf_op jit(solution)/shard_map/ppermute | solution.py:557
  46.7 0.9 %collective-permute-start.16 = (f32[2,16,128]{2,1,0:T(8,128)S(1)}, f32[2,16,128]{2,1,0:T(8,128)S(1)}, u32[]{:S(2)}, u32[]{:S(2)}) collective-permute-start(f32[2,16,128]{2,1,0:T(8,128)S(1)} %add_add_fusion.1), channel_id=1, source_target_pairs={{0,8},{1,9},{2,10},{3,11},{4,12},{5,13},{6,14},{7,15},{8,0},{9,1},... | collective-permute-start | bytes 49160 | tf_op jit(solution)/shard_map/ppermute | solution.py:557
  47.5 0.8 %collective-permute-start.15 = (f32[2,16,128]{2,1,0:T(8,128)S(1)}, f32[2,16,128]{2,1,0:T(8,128)S(1)}, u32[]{:S(2)}, u32[]{:S(2)}) collective-permute-start(f32[2,16,128]{2,1,0:T(8,128)S(1)} %add_add_fusion.1), channel_id=1, source_target_pairs={{0,4},{1,5},{2,6},{3,7},{4,8},{5,9},{6,10},{7,11},{8,12},{9,13},{1... | collective-permute-start | bytes 49160 | tf_op jit(solution)/shard_map/ppermute | solution.py:557
  48.3 3.3 %slopes_x.1.u_ref = f32[3,256,8,128]{3,2,1,0:T(8,128)} custom-call(f32[3,256,8,128]{3,2,1,0:T(8,128)S(1)} %copy-done, f32[8,8,128]{2,1,0:T(8,128)S(1)} %collective-permute-done.xl, f32[8,8,128]{2,1,0:T(8,128)S(1)} %collective-permute-done.1.xr, f32[3,256,8,128]{3,2,1,0:T(8,128)} %get-tuple-element.22._), custom_call_target="tpu_custom_call", output_to_operand_aliasing={{}: (3, {})} | custom-call | flops 268435456 | bytes 4194304 | tf_op jit(solution)/shard_map/slopes_x/pallas_call | solution.py:369
  51.7 0.3 collective-permute-done.16
  52.0 0.5 collective-permute-done.15
  52.6 0.0 copy-start.6
  52.6 5.9 %slopes_z.1.w_ref = f32[3,256,8,128]{3,2,1,0:T(8,128)} custom-call(f32[3,256,8,128]{3,2,1,0:T(8,128)S(1)} %copy-done, f32[8,16,128]{2,1,0:T(8,128)S(1)} %collective-permute-done.6.zl, f32[8,16,128]{2,1,0:T(8,128)S(1)} %collective-permute-done.7.zr, f32[8,16,128]{2,1,0:T(8,128)S(1)} %copy-done.5, ...), custom_call_target="tpu_custom_call", output_to_operand_aliasing={{}: (6, {})} | custom-call | flops 268435456 | bytes 4194304 | tf_op jit(solution)/shard_map/slopes_z/pallas_call | solution.py:407
  58.5 1.9 %copy-done.1 = f32[3,256,8,128]{3,2,1,0:T(8,128)S(1)} copy-done((f32[3,256,8,128]{3,2,1,0:T(8,128)S(1)}, f32[3,256,8,128]{3,2,1,0:T(8,128)}, u32[]{:S(2)}) %copy-start.1) | copy-done | bytes 3145752
  60.4 3.9 %rebuild.1 = f32[2,256,8,128]{3,2,1,0:T(8,128)} custom-call(f32[3,256,8,128]{3,2,1,0:T(8,128)S(1)} %copy-done.2, f32[3,256,8,128]{3,2,1,0:T(8,128)S(1)} %copy-done.1, f32[2,8,128]{2,1,0:T(8,128)S(1)} %pad_maximum_fusion.3.xt, f32[2,16,128]{2,1,0:T(8,128)S(1)} %pad_maximum_fusion.1.zt, bf16[2,256,128]{2,1,0:T(8,128)(2,1)S(1)} %copy-done.6), custom_call_target="tpu_custom_call" | custom-call | flops 268435456 | bytes 4194304 | tf_op jit(solution)/shard_map/rebuild/pallas_call | solution.py:527
  64.3 12.2 %divergence.1 = f32[3,256,8,128]{3,2,1,0:T(8,128)} custom-call(f32[3,256,8,128]{3,2,1,0:T(8,128)S(1)} %copy-done, f32[3,256,8,128]{3,2,1,0:T(8,128)S(1)} %copy-done, f32[3,256,8,128]{3,2,1,0:T(8,128)S(1)} %copy-done, f32[8,8,128]{2,1,0:T(8,128)S(1)} %collective-permute-done.xl, f32[8,8,128]{2,1,0:T(8,128)S(1)} %collective-permute-done.1.xr, ...), custom_call_target="tpu_custom_call" | custom-call | flops 805306368 | bytes 12582912 | tf_op jit(solution)/shard_map/divergence/pallas_call | solution.py:468
  (46 shorter events, 0.2 us)
Async XLA Ops:
  2.1 23.4 %copy-start = (f32[3,256,8,128]{3,2,1,0:T(8,128)S(1)}, f32[3,256,8,128]{3,2,1,0:T(8,128)}, u32[]{:S(2)}) copy-start(f32[3,256,8,128]{3,2,1,0:T(8,128)} %w_ref.5) | copy-start | bytes 9437188
  2.1 23.4 %copy-start.3 = (bf16[2,256,128]{2,1,0:T(8,128)(2,1)S(1)}, bf16[2,256,128]{2,1,0:T(8,128)(2,1)}, u32[]{:S(2)}) copy-start(bf16[2,256,128]{2,1,0:T(8,128)(2,1)} %constant.153.clone.m_ref) | copy-start | bytes 393220
  7.7 12.9 %copy-start.10 = (f32[2,8,128]{2,1,0:T(8,128)S(1)}, f32[2,8,128]{2,1,0:T(8,128)}, u32[]{:S(2)}) copy-start(f32[2,8,128]{2,1,0:T(8,128)} %get-tuple-element.18) | copy-start | bytes 24580
  7.7 14.5 %copy-start.9 = (f32[2,8,128]{2,1,0:T(8,128)S(1)}, f32[2,8,128]{2,1,0:T(8,128)}, u32[]{:S(2)}) copy-start(f32[2,8,128]{2,1,0:T(8,128)} %get-tuple-element.19) | copy-start | bytes 24580
  7.7 17.8 %copy-start.7 = (f32[2,16,128]{2,1,0:T(8,128)S(1)}, f32[2,16,128]{2,1,0:T(8,128)}, u32[]{:S(2)}) copy-start(f32[2,16,128]{2,1,0:T(8,128)} %get-tuple-element.20.zown_r) | copy-start | bytes 49156
  7.8 17.8 %copy-start.8 = (f32[2,16,128]{2,1,0:T(8,128)S(1)}, f32[2,16,128]{2,1,0:T(8,128)}, u32[]{:S(2)}) copy-start(f32[2,16,128]{2,1,0:T(8,128)} %get-tuple-element.21.zown_l) | copy-start | bytes 49156
  7.8 17.7 %collective-permute-start.4 = (f32[2,16,128]{2,1,0:T(8,128)}, f32[2,16,128]{2,1,0:T(8,128)S(1)}, u32[]{:S(2)}, u32[]{:S(2)}) collective-permute-start(f32[2,16,128]{2,1,0:T(8,128)} %get-tuple-element.20.zown_r), channel_id=1, source_target_pairs={{0,1},{1,2},{2,3},{3,4},{4,5},{5,6},{6,7},{7,8},{8,9},{9,10},{10,1... | collective-permute-start | bytes 49160 | tf_op jit(solution)/shard_map/ppermute | solution.py:543
  9.8 15.6 %collective-permute-start.5 = (f32[2,16,128]{2,1,0:T(8,128)}, f32[2,16,128]{2,1,0:T(8,128)S(1)}, u32[]{:S(2)}, u32[]{:S(2)}) collective-permute-start(f32[2,16,128]{2,1,0:T(8,128)} %get-tuple-element.21.zown_l), channel_id=1, source_target_pairs={{1,0},{2,1},{3,2},{4,3},{5,4},{6,5},{7,6},{8,7},{9,8},{10,9},{11,1... | collective-permute-start | bytes 49160 | tf_op jit(solution)/shard_map/ppermute | solution.py:544
  20.6 26.0 %collective-permute-start = (f32[8,8,128]{2,1,0:T(8,128)}, f32[8,8,128]{2,1,0:T(8,128)S(1)}, u32[]{:S(2)}, u32[]{:S(2)}) collective-permute-start(f32[8,8,128]{2,1,0:T(8,128)} %get-tuple-element.16), channel_id=1, source_target_pairs={{0,16},{16,32},{32,48},{48,64},{64,80},{80,96},{96,112},{112,0},{1... | collective-permute-start | bytes 98312 | tf_op jit(solution)/shard_map/ppermute | solution.py:543
  20.6 4.8 %collective-permute-start.2 = (f32[2,8,128]{2,1,0:T(8,128)S(1)}, f32[2,8,128]{2,1,0:T(8,128)S(1)}, u32[]{:S(2)}, u32[]{:S(2)}) collective-permute-start(f32[2,8,128]{2,1,0:T(8,128)S(1)} %copy-done.10), channel_id=1, source_target_pairs={{0,16},{16,32},{32,48},{48,64},{64,80},{80,96},{96,112},{112,0},{1... | collective-permute-start | bytes 24584 | tf_op jit(solution)/shard_map/ppermute | solution.py:543
  22.2 3.2 %collective-permute-start.3 = (f32[2,8,128]{2,1,0:T(8,128)S(1)}, f32[2,8,128]{2,1,0:T(8,128)S(1)}, u32[]{:S(2)}, u32[]{:S(2)}) collective-permute-start(f32[2,8,128]{2,1,0:T(8,128)S(1)} %copy-done.9), channel_id=1, source_target_pairs={{16,0},{32,16},{48,32},{64,48},{80,64},{96,80},{112,96},{0,112},{1... | collective-permute-start | bytes 24584 | tf_op jit(solution)/shard_map/ppermute | solution.py:544
  25.5 14.6 %copy-start.4 = (f32[8,16,128]{2,1,0:T(8,128)S(1)}, f32[8,16,128]{2,1,0:T(8,128)}, u32[]{:S(2)}) copy-start(f32[8,16,128]{2,1,0:T(8,128)} %get-tuple-element.23.zown_r) | copy-start | bytes 196612
  25.5 17.2 %copy-start.5 = (f32[8,16,128]{2,1,0:T(8,128)S(1)}, f32[8,16,128]{2,1,0:T(8,128)}, u32[]{:S(2)}) copy-start(f32[8,16,128]{2,1,0:T(8,128)} %get-tuple-element.24.zown_l) | copy-start | bytes 196612
  25.5 22.1 %collective-permute-start.1 = (f32[8,8,128]{2,1,0:T(8,128)}, f32[8,8,128]{2,1,0:T(8,128)S(1)}, u32[]{:S(2)}, u32[]{:S(2)}) collective-permute-start(f32[8,8,128]{2,1,0:T(8,128)} %get-tuple-element.17), channel_id=1, source_target_pairs={{16,0},{32,16},{48,32},{64,48},{80,64},{96,80},{112,96},{0,112},{1... | collective-permute-start | bytes 98312 | tf_op jit(solution)/shard_map/ppermute | solution.py:544
  31.0 1.3 %collective-permute-start.8 = (f32[2,8,128]{2,1,0:T(8,128)S(1)}, f32[2,8,128]{2,1,0:T(8,128)S(1)}, u32[]{:S(2)}, u32[]{:S(2)}) collective-permute-start(f32[2,8,128]{2,1,0:T(8,128)S(1)} %pad_maximum_fusion.2), channel_id=1, source_target_pairs={{0,16},{16,0},{32,48},{48,32},{64,80},{80,64},{96,112},{112,96},{1... | collective-permute-start | bytes 24584 | tf_op jit(solution)/shard_map/ppermute | solution.py:557
  31.5 3.7 %collective-permute-start.14 = (f32[2,16,128]{2,1,0:T(8,128)S(1)}, f32[2,16,128]{2,1,0:T(8,128)S(1)}, u32[]{:S(2)}, u32[]{:S(2)}) collective-permute-start(f32[2,16,128]{2,1,0:T(8,128)S(1)} %pad_maximum_fusion), channel_id=1, source_target_pairs={{0,3},{1,0},{2,1},{3,2},{4,7},{5,4},{6,5},{7,6},{8,11},{9,8},{10,9... | collective-permute-start | bytes 49160 | tf_op jit(solution)/shard_map/ppermute | solution.py:557
  31.5 6.0 %collective-permute-start.13 = (f32[2,16,128]{2,1,0:T(8,128)S(1)}, f32[2,16,128]{2,1,0:T(8,128)S(1)}, u32[]{:S(2)}, u32[]{:S(2)}) collective-permute-start(f32[2,16,128]{2,1,0:T(8,128)S(1)} %pad_maximum_fusion), channel_id=1, source_target_pairs={{0,2},{1,3},{2,0},{3,1},{4,6},{5,7},{6,4},{7,5},{8,10},{9,11},{10,... | collective-permute-start | bytes 49160 | tf_op jit(solution)/shard_map/ppermute | solution.py:557
  32.3 6.7 %collective-permute-start.12 = (f32[2,16,128]{2,1,0:T(8,128)S(1)}, f32[2,16,128]{2,1,0:T(8,128)S(1)}, u32[]{:S(2)}, u32[]{:S(2)}) collective-permute-start(f32[2,16,128]{2,1,0:T(8,128)S(1)} %pad_maximum_fusion), channel_id=1, source_target_pairs={{0,1},{1,2},{2,3},{3,0},{4,5},{5,6},{6,7},{7,4},{8,9},{9,10},{10,1... | collective-permute-start | bytes 49160 | tf_op jit(solution)/shard_map/ppermute | solution.py:557
  35.2 4.9 %collective-permute-start.11 = (f32[2,8,128]{2,1,0:T(8,128)S(1)}, f32[2,8,128]{2,1,0:T(8,128)S(1)}, u32[]{:S(2)}, u32[]{:S(2)}) collective-permute-start(f32[2,8,128]{2,1,0:T(8,128)S(1)} %fusion.12), channel_id=1, source_target_pairs={{0,96},{16,112},{32,0},{48,16},{64,32},{80,48},{96,64},{112,80},{1... | collective-permute-start | bytes 24584 | tf_op jit(solution)/shard_map/ppermute | solution.py:557
  37.5 5.2 %collective-permute-start.10 = (f32[2,8,128]{2,1,0:T(8,128)S(1)}, f32[2,8,128]{2,1,0:T(8,128)S(1)}, u32[]{:S(2)}, u32[]{:S(2)}) collective-permute-start(f32[2,8,128]{2,1,0:T(8,128)S(1)} %fusion.12), channel_id=1, source_target_pairs={{0,64},{16,80},{32,96},{48,112},{64,0},{80,16},{96,32},{112,48},{1... | collective-permute-start | bytes 24584 | tf_op jit(solution)/shard_map/ppermute | solution.py:557
  39.0 6.9 %collective-permute-start.9 = (f32[2,8,128]{2,1,0:T(8,128)S(1)}, f32[2,8,128]{2,1,0:T(8,128)S(1)}, u32[]{:S(2)}, u32[]{:S(2)}) collective-permute-start(f32[2,8,128]{2,1,0:T(8,128)S(1)} %fusion.12), channel_id=1, source_target_pairs={{0,32},{16,48},{32,64},{48,80},{64,96},{80,112},{96,0},{112,16},{1... | collective-permute-start | bytes 24584 | tf_op jit(solution)/shard_map/ppermute | solution.py:557
  40.1 12.4 %collective-permute-start.6 = (f32[8,16,128]{2,1,0:T(8,128)S(1)}, f32[8,16,128]{2,1,0:T(8,128)S(1)}, u32[]{:S(2)}, u32[]{:S(2)}) collective-permute-start(f32[8,16,128]{2,1,0:T(8,128)S(1)} %copy-done.4), channel_id=1, source_target_pairs={{0,1},{1,2},{2,3},{3,4},{4,5},{5,6},{6,7},{7,8},{8,9},{9,10},{10,1... | collective-permute-start | bytes 196616 | tf_op jit(solution)/shard_map/ppermute | solution.py:543
  42.7 9.9 %collective-permute-start.7 = (f32[8,16,128]{2,1,0:T(8,128)S(1)}, f32[8,16,128]{2,1,0:T(8,128)S(1)}, u32[]{:S(2)}, u32[]{:S(2)}) collective-permute-start(f32[8,16,128]{2,1,0:T(8,128)S(1)} %copy-done.5), channel_id=1, source_target_pairs={{1,0},{2,1},{3,2},{4,3},{5,4},{6,5},{7,6},{8,7},{9,8},{10,9},{11,1... | collective-permute-start | bytes 196616 | tf_op jit(solution)/shard_map/ppermute | solution.py:544
  45.8 5.9 %collective-permute-start.17 = (f32[2,16,128]{2,1,0:T(8,128)S(1)}, f32[2,16,128]{2,1,0:T(8,128)S(1)}, u32[]{:S(2)}, u32[]{:S(2)}) collective-permute-start(f32[2,16,128]{2,1,0:T(8,128)S(1)} %add_add_fusion.1), channel_id=1, source_target_pairs={{0,12},{1,13},{2,14},{3,15},{4,0},{5,1},{6,2},{7,3},{8,4},{9,5},{1... | collective-permute-start | bytes 49160 | tf_op jit(solution)/shard_map/ppermute | solution.py:557
  46.7 5.3 %collective-permute-start.16 = (f32[2,16,128]{2,1,0:T(8,128)S(1)}, f32[2,16,128]{2,1,0:T(8,128)S(1)}, u32[]{:S(2)}, u32[]{:S(2)}) collective-permute-start(f32[2,16,128]{2,1,0:T(8,128)S(1)} %add_add_fusion.1), channel_id=1, source_target_pairs={{0,8},{1,9},{2,10},{3,11},{4,12},{5,13},{6,14},{7,15},{8,0},{9,1},... | collective-permute-start | bytes 49160 | tf_op jit(solution)/shard_map/ppermute | solution.py:557
  47.5 5.0 %collective-permute-start.15 = (f32[2,16,128]{2,1,0:T(8,128)S(1)}, f32[2,16,128]{2,1,0:T(8,128)S(1)}, u32[]{:S(2)}, u32[]{:S(2)}) collective-permute-start(f32[2,16,128]{2,1,0:T(8,128)S(1)} %add_add_fusion.1), channel_id=1, source_target_pairs={{0,4},{1,5},{2,6},{3,7},{4,8},{5,9},{6,10},{7,11},{8,12},{9,13},{1... | collective-permute-start | bytes 49160 | tf_op jit(solution)/shard_map/ppermute | solution.py:557
  52.5 6.0 %copy-start.2 = (f32[3,256,8,128]{3,2,1,0:T(8,128)S(1)}, f32[3,256,8,128]{3,2,1,0:T(8,128)}, u32[]{:S(2)}) copy-start(f32[3,256,8,128]{3,2,1,0:T(8,128)} %slopes_x.1.u_ref) | copy-start | bytes 9437188
  52.6 5.9 %copy-start.6 = (bf16[2,256,128]{2,1,0:T(8,128)(2,1)S(1)}, bf16[2,256,128]{2,1,0:T(8,128)(2,1)}, u32[]{:S(2)}) copy-start(bf16[2,256,128]{2,1,0:T(8,128)(2,1)} %constant.154.clone.m_ref) | copy-start | bytes 393220
  58.5 1.9 %copy-start.1 = (f32[3,256,8,128]{3,2,1,0:T(8,128)S(1)}, f32[3,256,8,128]{3,2,1,0:T(8,128)}, u32[]{:S(2)}) copy-start(f32[3,256,8,128]{3,2,1,0:T(8,128)} %slopes_z.1.w_ref) | copy-start | bytes 9437188

commit v2 on v0

v2 whole, which is shorter than its diff:
```python
import math

import jax
import jax.numpy as jnp
import numpy as np
from jax import lax
from jax.experimental import pallas as pl
from jax.experimental.pallas import tpu as pltpu
from jax.sharding import PartitionSpec as P

ALPHA = 1.0 / 3.0
COEF_A = 14.0 / 9.0
COEF_B = 1.0 / 9.0
LANES = 128
F32 = jnp.float32
VMEM = pl.BlockSpec(memory_space=pltpu.VMEM)
HBM = pl.BlockSpec(memory_space=pltpu.HBM)
ANY = pl.BlockSpec(memory_space=pl.ANY)
BF16 = jnp.bfloat16

RHO = (-1.0 + math.sqrt(1.0 - 4.0 * ALPHA * ALPHA)) / (2.0 * ALPHA)


def kernel_weights():
    reach = 400
    k = np.arange(-reach, reach + 1)
    green = RHO ** np.abs(k).astype(np.float64) / math.sqrt(1.0 - 4.0 * ALPHA * ALPHA)

    def shifted(s):
        out = np.zeros_like(green)
        if s >= 0:
            out[s:] = green[: len(green) - s]
        else:
            out[:s] = green[-s:]
        return out

    direct = 0.5 * COEF_A * (shifted(-1) - shifted(1)) + 0.25 * COEF_B * (shifted(-2) - shifted(2))
    total = np.concatenate([[0.0], np.cumsum(direct)])
    return {m: total[m + reach] for m in range(-2, 4)}


_W = kernel_weights()
NEAR = _W[1]
TAIL = _W[2] / RHO**2
KAPPA = TAIL * RHO * RHO
TOGETHER = 16
REACH = 96


def h_of(m):
    m = np.asarray(m)
    m = np.where(m <= 0, 1 - m, m)
    return np.where(m == 1, NEAR, TAIL * RHO ** m.astype(np.float64))


def split_np(x):
    hi = x.astype(BF16)
    lo = (x - hi.astype(np.float64)).astype(BF16)
    return hi, lo


def going_up(length):
    j = np.arange(length)
    w = (RHO - 1.0) * RHO ** (length - j).astype(np.float64)
    w[-1] = RHO**2
    return w


def going_down(length):
    return going_up(length)[::-1] * -1.0


def z_inner():
    j = np.arange(LANES)
    inner = h_of(j[None, :] - j[:, None])
    inner[LANES - 1] = 0.0
    hi, lo = split_np(inner)
    return np.stack([hi, lo])


def z_rims(fields):
    j = np.arange(LANES)
    rim = np.stack(
        [
            h_of(j + 1),
            TAIL * RHO ** j.astype(np.float64),
            h_of(LANES - j),
            TAIL * RHO ** (LANES - 1 - j).astype(np.float64),
        ]
    )
    hi, lo = split_np(rim)
    out = np.zeros((fields, LANES, LANES), BF16)
    for f in range(fields):
        out[f, 12 * f : 12 * f + 12] = np.concatenate([hi, hi, lo], 0)
    return out


def sum_matrices():
    j = np.arange(LANES)
    lower = (j[:, None] < j[None, :]) + 0.5 * (j[:, None] == j[None, :])
    ones = np.ones((3, LANES))
    slope = -np.broadcast_to(j, (3, LANES))
    pad = np.zeros((LANES - 6, LANES))
    first = np.concatenate([lower, lower], 0)
    second = np.concatenate([lower, ones, slope, pad], 0)
    return np.stack([first, second]).astype(BF16)


def split2(x):
    hi = x.astype(BF16)
    return hi, (x - hi.astype(F32)).astype(BF16)


def split3(x):
    hi = x.astype(BF16)
    rest = x - hi.astype(F32)
    mid = rest.astype(BF16)
    return hi, mid, (rest - mid.astype(F32)).astype(BF16)


def dot(a, b):
    return lax.dot_general(a, b, (((1,), (0,)), ((), ())), preferred_element_type=F32)


def product(values, name):
    out = values[name[0]]
    for c in name[1:]:
        out = out * values[c]
    return out


COMP = {"u": 0, "v": 1, "w": 2}


X_SUMS = ["u", "v", "w", "uu", "uv", "uw"]
Z_SUMS = ["u", "v", "w", "wu", "wv", "ww"]
CELLS = ["u", "v", "w"]


def edges_call(velocity):
    comps, nx, ny, nz = velocity.shape
    sub = LANES // ny
    chunks = nx // sub
    nq = len(X_SUMS) + len(CELLS)
    up_x = going_up(nx)
    down_x = going_down(nx)
    cut_x = min(REACH, nx)
    cut = min(REACH, nz)
    group = 8
    parts = 4
    part = nx // parts
    first_up = nx - cut_x

    def ramp(powers, factor):
        row = lax.broadcasted_iota(jnp.int32, (8, LANES), 0)
        tile = jnp.zeros((8, LANES), F32)
        for k in range(8):
            tile = jnp.where(row == k, np.float32(powers[k]), tile)
        return [tile * np.float32(f) for f in factor]

    def z_weights():
        up = going_up(nz)[nz - cut :]
        down = going_down(nz)[:cut]
        tiles = cut // 8
        ups = ramp(up[:8] / up[0], up[::8])
        downs = ramp(down[-8:] / down[-8], down[::8])
        row = lax.broadcasted_iota(jnp.int32, (8, LANES), 0)
        ups[-1] = jnp.where(row == 7, np.float32(up[-1]), ups[-1])
        downs[0] = ramp(down[8:16] / down[8], [down[8] / RHO**8])[0]
        downs[0] = jnp.where(row == 0, np.float32(down[0]), downs[0])
        return jnp.concatenate(ups, 0), jnp.concatenate(downs, 0)

    def body(v_hbm, xu_ref, xd_ref, zu_ref, zd_ref, v_ref, sems):
        copies = [
            pltpu.make_async_copy(
                v_hbm.at[:, pl.ds(p * part, part)], v_ref.at[:, pl.ds(p * part, part)], sems.at[p]
            )
            for p in range(parts)
        ]
        for copy in copies:
            copy.start()
        weight_up, weight_down = z_weights()

        def x_rows(acc, weights, rows):
            for i in rows:
                vals = {c: v_ref[COMP[c], i] for c in CELLS}
                for q, name in enumerate(X_SUMS):
                    term = product(vals, name) * np.float32(weights[i])
                    acc[q] = term if acc[q] is None else acc[q] + term

        ups = [None] * len(X_SUMS)
        downs = [None] * len(X_SUMS)
        rows_z = {}
        for p in range(parts):
            copies[p].wait()
            for s in range(p * part // sub, (p + 1) * part // sub):
                t = {c: v_ref[COMP[c], s * sub : (s + 1) * sub].reshape(LANES, nz).T for c in CELLS}
                for q, name in enumerate(Z_SUMS):
                    f = product(t, name)
                    up = jnp.sum(f[nz - cut :] * weight_up, axis=0, keepdims=True)
                    down = jnp.sum(f[:cut] * weight_down, axis=0, keepdims=True)
                    rows_z.setdefault(q, []).append((up, down))
                for q, name in enumerate(CELLS):
                    rows_z.setdefault(len(Z_SUMS) + q, []).append((t[name][nz - 1 : nz], t[name][0:1]))
                if (s + 1) % group == 0:
                    at = s + 1 - group
                    for q, pairs in rows_z.items():
                        zu_ref[q, at : at + group] = jnp.concatenate([r[0] for r in pairs], 0)
                        zd_ref[q, at : at + group] = jnp.concatenate([r[1] for r in pairs], 0)
                    rows_z = {}
            here = range(p * part, (p + 1) * part)
            x_rows(downs, down_x, [i for i in here if i < cut_x])
            x_rows(ups, up_x, [i for i in here if i >= first_up])
        for q in range(len(X_SUMS)):
            xu_ref[q] = ups[q]
            xd_ref[q] = downs[q]
        for q in range(len(CELLS)):
            xu_ref[len(X_SUMS) + q] = v_ref[q, nx - 1]
            xd_ref[len(X_SUMS) + q] = v_ref[q, 0]

    xs = jax.ShapeDtypeStruct((nq, ny, nz), F32)
    zs = jax.ShapeDtypeStruct((nq, chunks, LANES), F32)
    return pl.pallas_call(
        body,
        in_specs=[HBM],
        out_specs=[VMEM] * 5,
        out_shape=[xs, xs, zs, zs, jax.ShapeDtypeStruct(velocity.shape, F32)],
        scratch_shapes=[pltpu.SemaphoreType.DMA((parts,))],
        compiler_params=params(),
        name="edges",
        cost_estimate=cost(6, nx * ny * nz),
    )(pltpu.with_memory_space_constraint(velocity, pltpu.HBM))


def x_derivative(read, write, scratch, nx, sum_before, cell_before, sum_after, cell_after, done=None):
    unroll = 8
    half = nx // 2
    blocks = half // unroll
    grown = [KAPPA * RHO ** -(k + 1) for k in range(unroll)]
    power = [RHO**k for k in range(unroll + 1)]

    def sweep(first):
        def step(b, carry):
            low, before, here, high, after, there = carry
            lows = (0 if first else half) + b * unroll
            highs = (nx if first else half) - 1 - b * unroll
            for k in range(unroll):
                i = lows + k
                part = low if k == 0 else power[k] * low
                edge = here - before
                if first:
                    nxt = read(i + 1)
                    scratch[i] = part
                else:
                    if k == unroll - 1:
                        nxt = jnp.where(b == blocks - 1, cell_after, read(jnp.minimum(i + 1, nx - 1)))
                    else:
                        nxt = read(i + 1)
                    write(i, scratch[i] + (part + NEAR * (nxt - before)))
                low = low + grown[k] * edge
                before, here = here, nxt

                i = highs - k
                part = high if k == 0 else power[k] * high
                edge = after - there
                if first:
                    nxt = read(i - 1)
                    scratch[i] = part
                else:
                    if k == unroll - 1:
                        nxt = jnp.where(b == blocks - 1, cell_before, read(jnp.maximum(i - 1, 0)))
                    else:
                        nxt = read(i - 1)
                    write(i, scratch[i] + (part + NEAR * (after - nxt)))
                high = high + grown[k] * edge
                after, there = there, nxt
            return power[unroll] * low, before, here, power[unroll] * high, after, there

        return step

    carry = (TAIL * sum_before, cell_before, read(0), TAIL * sum_after, cell_after, read(nx - 1))
    carry = lax.fori_loop(0, blocks, sweep(True), carry)
    pieces = 2
    for p in range(pieces):
        lo, hi = p * blocks // pieces, (p + 1) * blocks // pieces
        carry = lax.fori_loop(lo, hi, sweep(False), carry)
        if done is not None:
            done(half + lo * unroll, (hi - lo) * unroll)
            done(half - hi * unroll, (hi - lo) * unroll)


class Outbox:
    def __init__(self, sems):
        self.sems, self.copies = sems, []

    def send(self, src, dst):
        copy = pltpu.make_async_copy(src, dst, self.sems.at[len(self.copies)])
        copy.start()
        self.copies.append(copy)

    def wait(self):
        for copy in self.copies:
            copy.wait()


def params(mib=8):
    return pltpu.CompilerParams(vmem_limit_bytes=mib * 2**20)


def cost(fields, size):
    return pl.CostEstimate(flops=fields * size * 512, transcendentals=0, bytes_accessed=fields * size * 8)


def inner_z(velocity, inner):
    _, nx, ny, nz = velocity.shape
    rows = nx * ny

    def body(v_ref, m_ref, w_out, u_out, v_out, *c_outs):
        outs = (u_out, v_out, w_out) + c_outs
        keep = lax.broadcasted_iota(jnp.int32, (rows, LANES), 1) < LANES - 1
        both = jnp.concatenate([m_ref[0], m_ref[0]], 0)
        w = v_ref[2].reshape(rows, nz)
        for c in range(6):
            f = v_ref[c % 3].reshape(rows, nz)
            if c >= 3:
                f = f * w
            e = jnp.where(keep, pltpu.roll(f, LANES - 1, 1) - f, 0.0)
            hi, lo = split2(e)
            g = dot(jnp.concatenate([hi, lo], 1), both) + dot(hi, m_ref[1])
            outs[c][...] = g.reshape(nx, ny, nz)

    return pl.pallas_call(
        body,
        in_specs=[VMEM, VMEM],
        out_specs=[VMEM] * 6,
        out_shape=[jax.ShapeDtypeStruct(velocity.shape[1:], F32)] * 6,
        compiler_params=params(),
        name="inner_z",
        cost_estimate=cost(6, nx * ny * nz),
    )(velocity, inner)


def slopes_first(velocity, inner, x_halo, z_halo, rims):
    _, nx, ny, nz = velocity.shape
    sub = LANES // ny
    chunks = nx // sub
    rows = nx * ny

    def body(v_ref, i_ref, xl, xr, zl, zr, own_l, own_r, m_ref, gu, gw, sx, sz, st, scratch, rim):
        used = 12 * len(Z_SUMS)
        rim[:, used:, :] = jnp.zeros((chunks, LANES - used, LANES), F32)
        for f in range(6):
            cells = [r[6 + f % 3] for r in (zl, own_l, own_r, zr)]
            if f >= 3:
                cells = [c * r[8] for c, r in zip(cells, (zl, own_l, own_r, zr))]
            terms = [cells[1] - cells[0], zl[f], cells[3] - cells[2], zr[f]]
            for q, term in enumerate(terms):
                hi = term.astype(BF16).astype(F32)
                lo = (term - hi).astype(BF16).astype(F32)
                rim[:, 12 * f + q, :] = hi
                rim[:, 12 * f + 4 + q, :] = lo
                rim[:, 12 * f + 8 + q, :] = hi
        for c in range(chunks):
            st[c * LANES : (c + 1) * LANES] = rim[c].T.astype(BF16)

        g = i_ref[...].reshape(rows, nz) + dot(st[...], m_ref[2])
        gw[...] = g.reshape(nx, ny, nz)

        def write_x(i, g):
            gu[i] = g

        x_derivative(lambda i: v_ref[0, i], write_x, scratch, nx, xl[0], xl[6], xr[0], xr[6])

        zero = jnp.zeros((ny, nz), F32)
        ways = 4

        def add(b, carry):
            out = []
            for k, (total, moment) in enumerate(carry):
                for n in range(2):
                    i = b * 2 * ways + 2 * k + n
                    g = gw[i]
                    total = total + g
                    moment = moment + (i.astype(F32) - 0.5 * (nx - 1)) * g
                out.append((total, moment))
            return tuple(out)

        got = lax.fori_loop(0, nx // (2 * ways), add, ((zero, zero),) * ways)
        sx[0] = (got[0][0] + got[1][0]) + (got[2][0] + got[3][0])
        sx[1] = (got[0][1] + got[1][1]) + (got[2][1] + got[3][1])

        at = lax.broadcasted_iota(jnp.int32, (nz, LANES), 0).astype(F32) - 0.5 * (nz - 1)
        totals, moments = [], []
        for c in range(chunks):
            t = gu[c * sub : (c + 1) * sub].reshape(LANES, nz).T
            totals.append(jnp.sum(t, axis=0, keepdims=True))
            moments.append(jnp.sum(t * at, axis=0, keepdims=True))
        sz[0] = jnp.concatenate(totals, 0)
        sz[1] = jnp.concatenate(moments, 0)

    one = jax.ShapeDtypeStruct(velocity.shape[1:], F32)
    sx = jax.ShapeDtypeStruct((2, ny, nz), F32)
    sz = jax.ShapeDtypeStruct((2, chunks, LANES), F32)
    st = jax.ShapeDtypeStruct((rows, LANES), BF16)
    small = [*x_halo, *z_halo, rims]
    outs = [one, one, sx, sz, st]
    return pl.pallas_call(
        body,
        in_specs=[VMEM] * (2 + len(small)),
        out_specs=[VMEM] * len(outs),
        out_shape=outs,
        scratch_shapes=[pltpu.VMEM((nx, ny, nz), F32), pltpu.VMEM((chunks, LANES, LANES), F32)],
        compiler_params=params(),
        name="slopes_first",
        cost_estimate=cost(2, nx * ny * nz),
    )(velocity, inner, *small)


def slopes_x(velocity, x_halo, gu):
    _, nx, ny, nz = velocity.shape

    def body(v_ref, gu_ref, xl, xr, out, scratch, made, sems):
        box = Outbox(sems)
        box.send(gu_ref, out.at[0])
        for c in (1, 2):

            def write(i, g):
                made[c - 1, i] = g

            def done(start, size):
                rows = pl.ds(start, size)
                box.send(made.at[c - 1, rows], out.at[c, rows])

            x_derivative(
                lambda i: v_ref[c, i], write, scratch, nx, xl[c], xl[6 + c], xr[c], xr[6 + c], done
            )
        box.wait()

    return pl.pallas_call(
        body,
        in_specs=[VMEM] * 4,
        out_specs=ANY,
        out_shape=jax.ShapeDtypeStruct(velocity.shape, F32),
        scratch_shapes=[
            pltpu.VMEM((nx, ny, nz), F32),
            pltpu.VMEM((2, nx, ny, nz), F32),
            pltpu.SemaphoreType.DMA((16,)),
        ],
        compiler_params=params(),
        name="slopes_x",
        cost_estimate=cost(2, nx * ny * nz),
    )(velocity, gu, *x_halo)


def slopes_z(inner_u, inner_v, st, rims, gw):
    nx, ny, nz = gw.shape
    rows = nx * ny
    parts = 2

    def body(iu_ref, iv_ref, gw_ref, st_ref, m_ref, out, made, sems):
        box = Outbox(sems)
        box.send(gw_ref, out.at[2])
        for c, i_ref in enumerate((iu_ref, iv_ref)):
            for p in range(parts):
                at = pl.ds(p * nx // parts, nx // parts)
                local = i_ref[at].reshape(rows // parts, nz)
                g = local + dot(st_ref[pl.ds(p * rows // parts, rows // parts)], m_ref[c])
                made[c, at] = g.reshape(nx // parts, ny, nz)
                box.send(made.at[c, at], out.at[c, at])
        box.wait()

    return pl.pallas_call(
        body,
        in_specs=[VMEM] * 5,
        out_specs=ANY,
        out_shape=jax.ShapeDtypeStruct((3, nx, ny, nz), F32),
        scratch_shapes=[pltpu.VMEM((2, nx, ny, nz), F32), pltpu.SemaphoreType.DMA((16,))],
        compiler_params=params(),
        name="slopes_z",
        cost_estimate=cost(2, nx * ny * nz),
    )(inner_u, inner_v, gw, st, rims)


def divergence(velocity, inner, x_halo, st, rims, comps, into=None):
    _, nx, ny, nz = velocity.shape
    rows = nx * ny

    def body(v_ref, xl, xr, st_ref, m_ref, *rest):
        i_refs = rest[: len(comps)]
        out, scratch, flux, made, sems = rest[-5:]
        box = Outbox(sems)
        for n, c in enumerate(comps):
            flux[...] = v_ref[0] * v_ref[c]
            g = i_refs[n][...].reshape(rows, nz) + dot(st_ref[...], m_ref[3 + c])
            made[n] = g.reshape(nx, ny, nz)

            def write(i, g):
                made[n, i] = made[n, i] + g

            def done(start, size):
                at = pl.ds(start, size)
                box.send(made.at[n, at], out.at[c, at])

            x_derivative(
                lambda i: flux[i],
                write,
                scratch,
                nx,
                xl[3 + c],
                xl[6] * xl[6 + c],
                xr[3 + c],
                xr[6] * xr[6 + c],
                done,
            )
        box.wait()

    extra = [] if into is None else [into]
    return pl.pallas_call(
        body,
        in_specs=[VMEM] * (5 + len(comps)) + [ANY] * len(extra),
        out_specs=ANY,
        out_shape=jax.ShapeDtypeStruct(velocity.shape, F32),
        scratch_shapes=[
            pltpu.VMEM((nx, ny, nz), F32),
            pltpu.VMEM((nx, ny, nz), F32),
            pltpu.VMEM((len(comps), nx, ny, nz), F32),
            pltpu.SemaphoreType.DMA((16,)),
        ],
        input_output_aliases={5 + len(comps): 0} if extra else {},
        compiler_params=params(),
        name="divergence",
        cost_estimate=cost(2 * len(comps), nx * ny * nz),
    )(velocity, *x_halo, st, rims, *inner, *extra)


def rebuild(gu, gw, x_terms, z_terms, mats, total_x, total_z):
    nx, ny, nz = gu.shape
    sub = LANES // ny
    chunks = nx // sub
    rows = nx * ny
    parts = 4
    scale_x = -1.0 / math.sqrt(total_x)
    scale_z = -1.0 / math.sqrt(total_z)

    def body(u_ref, w_ref, xt, zt, m_ref, out, rim, made, sems):
        box = Outbox(sems)
        rim[:, 6:, :] = jnp.zeros((chunks, LANES - 6, LANES), F32)
        for q in range(2):
            for p, part in enumerate(split3(zt[q])):
                rim[:, 3 * q + p, :] = part.astype(F32)
        for p in range(parts):
            at = pl.ds(p * nx // parts, nx // parts)
            hi, mid, lo = split3(u_ref[at].reshape(rows // parts, nz))
            here = range(p * chunks // parts, (p + 1) * chunks // parts)
            st = jnp.concatenate([rim[c].T.astype(BF16) for c in here], 0)
            g = dot(jnp.concatenate([hi, mid], 1), m_ref[0]) + dot(
                jnp.concatenate([lo, st], 1), m_ref[1]
            )
            made[1, at] = (scale_z * g).reshape(nx // parts, ny, nz)
            box.send(made.at[1, at], out.at[1, at])

        mean = xt[1]

        def along_x(b, acc):
            for k in range(8):
                i = b * 8 + k
                g = w_ref[i]
                made[0, i] = scale_x * (acc + 0.5 * g)
                acc = acc + (g - mean)
            return acc

        acc = xt[0]
        for p in range(parts):
            acc = lax.fori_loop(p * nx // parts // 8, (p + 1) * nx // parts // 8, along_x, acc)
            at = pl.ds(p * nx // parts, nx // parts)
            box.send(made.at[0, at], out.at[0, at])
        box.wait()

    shape = (2,) + gu.shape
    return pl.pallas_call(
        body,
        in_specs=[VMEM] * 5,
        out_specs=ANY,
        out_shape=jax.ShapeDtypeStruct(shape, F32),
        scratch_shapes=[
            pltpu.VMEM((chunks, LANES, LANES), F32),
            pltpu.VMEM(shape, F32),
            pltpu.SemaphoreType.DMA((16,)),
        ],
        compiler_params=params(),
        name="rebuild",
        cost_estimate=cost(2, nx * ny * nz),
    )(gu, gw, x_terms, z_terms, mats)


def swap(axis, up, down):
    n = lax.axis_size(axis)
    before = lax.ppermute(up, axis, [(i, (i + 1) % n) for i in range(n)])
    after = lax.ppermute(down, axis, [((i + 1) % n, i) for i in range(n)])
    return before, after


def exchange(axis, terms, bit):
    n = lax.axis_size(axis)
    return lax.ppermute(terms, axis, [(i, i ^ bit) for i in range(n)])


def combine(terms, before, part, upper):
    return terms + part, before + upper * part[0]


def place(axis, cells):
    n = lax.axis_size(axis)
    mine = lax.axis_index(axis)
    bits = {}
    bit = 1
    while bit < n:
        bits[bit] = jnp.where((mine & bit) != 0, 1.0, 0.0).astype(F32)
        bit *= 2
    start = (mine * cells).astype(F32)
    centre = start + (0.5 * (cells - 1) - 0.5 * (n * cells - 1))
    return bits, centre, (start + 0.5) * (1.0 / (n * cells))


def line_terms(terms, before, start, total_len):
    mean = terms[0] / total_len
    offset = before - start * terms[0] + terms[1] / total_len
    return jnp.stack([offset, mean])


def body(velocity):
    _, nx, ny, nz = velocity.shape
    size_x = lax.axis_size("gx")
    size_z = lax.axis_size("gz")
    total_x = nx * size_x
    total_z = nz * size_z
    inner_mats = jnp.asarray(z_inner())
    rims = jnp.asarray(z_rims(len(Z_SUMS)))
    sums = jnp.asarray(sum_matrices())

    spot_x, spot_z = place("gx", nx), place("gz", nz)
    velocity, (spot_x, spot_z) = lax.optimization_barrier((velocity, (spot_x, spot_z)))
    bits_x, centre_x, x0 = spot_x
    bits_z, centre_z, z0 = spot_z
    xu, xd, zu, zd, vel = edges_call(velocity)
    z_halo = (*swap("gz", zu, zd), zd, zu)
    x_halo = swap("gx", xu, xd)
    in_w, in_u, in_v, *in_c = inner_z(vel, inner_mats)
    gu, gw, sx, sz, st = slopes_first(vel, in_w, x_halo, z_halo, rims)

    tx = jnp.stack([sx[0], sx[1] + centre_x * sx[0]])
    tz = jnp.stack([sz[0], sz[1] + centre_z * sz[0]])
    bx = jnp.zeros_like(sx[0])
    bz = jnp.zeros_like(sz[0])

    results = {}
    fillers = [
        ("gx", lambda: slopes_x(vel, x_halo, gu)),
        ("gz", lambda: slopes_z(in_u, in_v, st, rims, gw)),
        ("c0", lambda: divergence(vel, in_c[:1], x_halo, st, rims, [0])),
        ("c1", lambda: divergence(vel, in_c[1:], x_halo, st, rims, [1, 2], results["c0"])),
    ]
    bit = 1
    while bit < max(size_x, size_z) or fillers:
        px = exchange("gx", tx, bit) if bit < size_x else None
        pz = exchange("gz", tz, bit) if bit < size_z else None
        if fillers:
            name, make = fillers.pop(0)
            results[name] = make()
            px, pz, results[name] = lax.optimization_barrier((px, pz, results[name]))
        if px is not None:
            tx, bx = combine(tx, bx, px, bits_x[bit])
        if pz is not None:
            tz, bz = combine(tz, bz, pz, bits_z[bit])
        bit *= 2
    rebuilt = rebuild(
        gu,
        gw,
        line_terms(tx, bx, x0, total_x),
        line_terms(tz, bz, z0, total_z),
        sums,
        total_x,
        total_z,
    )
    return (results["gx"], results["gz"], results["c1"], rebuilt)


def solution(mesh):
    spec = P(None, "gx", None, "gz")
    return jax.shard_map(
        body, mesh=mesh, in_specs=(spec,), out_specs=(spec,) * 4, check_vma=False
    )
```

time: 597 us -> 43.1 us (0.07); the launches traced: 585 us -> 43 us
  local copies, waits for them, and re-layouts: 215 us -> 0.02 us
  blocking collectives: 187 us -> 0 us
  other arithmetic: 67.4 us -> 0.09 us
  waiting for transfers between devices: 65.5 us -> 5.13 us
  Pallas kernels: 0 us -> 20.9 us
  matrix products: 20.7 us -> 0 us
  starting transfers between devices: 24.3 us -> 15.9 us
    psum x2 -> x0, blocking collectives: 154 us -> none  [the longest x1 139 us: body(): line_sum_z, centred_z = lax.psum((sum_z, moment_z), 'gz')]
    unnamed x28 -> x6, local copies, waits for them, and re-layouts: 91.9 us -> 0.02 us
    all_to_all x2 -> x0, waiting for transfers between devices: 64.8 us -> none  [the longest x1 64.8 us: body(): lax.all_to_all(fields_z, 'gz', split_axis=1, concat_axis=3, tiled=True)]
    slice x15 -> x0, local copies, waits for them, and re-layouts: 46.1 us -> none  [the longest x3 14 us: couple(): lax.slice_in_dim(last_cells, 0, count - 1, axis=axis_at)]
    all_to_all x4 -> x0, local copies, waits for them, and re-layouts: 42.1 us -> none  [the longest x2 25.8 us: body(): lax.all_to_all(solved_lines_z, 'gz', split_axis=3, concat_axis=1, tiled=T...]
    all_gather x2 -> x0, blocking collectives: 33.7 us -> none  [entering(): everything = lax.all_gather(array, axis)]
    reshape x1 -> x0, local copies, waits for them, and re-layouts: 22.5 us -> none  [whole_lines(): couple(solved, inverse, axis_at, edge_before, edge_after)]
    pallas_call x0 -> x8, Pallas kernels: none -> 20.9 us  [the longest x2 6.55 us: divergence(): pl.pallas_call(body, in_specs=[VMEM] * (5 + len(comps)) + [ANY] * len(ext...]
  transfers between devices with their start and end apart: 6 -> 11, of which waited for: 2 -> 5; matrix products, arithmetic and copies ran while one was open for 8% -> 0% of each run, Pallas kernels for 0% -> 32%
where the time goes in v2:
time: 43.1 us; the launch traced here: 43 us
  Pallas kernels  20.9 us (48%)
  starting transfers between devices  15.9 us (37%)
  waiting for transfers between devices  5.13 us (12%)
  between operations  0.91 us (2%)
    ppermute x2, starting transfers between devices, swap(): after = lax.ppermute(down, axis, [((i + 1) % n, i) for i in range(n)])  7.52 us
    pallas_call x2, Pallas kernels, divergence(): pl.pallas_call(body, in_specs=[VMEM] * (5 + len(comps)) + [ANY] * len(ext...  6.55 us
    ppermute x7, starting transfers between devices, exchange(): return lax.ppermute(terms, axis, [(i, i ^ bit) for i in range(n)])  6.42 us
    ppermute x7, waiting for transfers between devices, exchange(): return lax.ppermute(terms, axis, [(i, i ^ bit) for i in range(n)])  5.12 us
    pallas_call x1, Pallas kernels, inner_z(): pl.pallas_call(body, in_specs=[VMEM, VMEM], out_specs=[VMEM] * 6, out_sha...  3.05 us
    pallas_call x1, Pallas kernels, edges_call(): pl.pallas_call(body, in_specs=[HBM], out_specs=[VMEM] * 5, out_shape=[xs,...  2.85 us
    pallas_call x1, Pallas kernels, slopes_x(): pl.pallas_call(body, in_specs=[VMEM] * 4, out_specs=ANY, out_shape=jax.Sh...  2.27 us
    pallas_call x1, Pallas kernels, slopes_first(): pl.pallas_call(body, in_specs=[VMEM] * (2 + len(small)), out_specs=[VMEM]...  2.21 us
  transfers between devices with their start and end apart: 11, of which 5 were waited for; matrix products, arithmetic and copies ran while one was open for 0% of the time, Pallas kernels for 32%

profile of v2, /device:TPU:0, one launch (start us, length us, event | category | flops | bytes accessed | tf_op | source)
XLA Modules:
  0.0 43.0 jit_solution(13365299379678871518)
XLA Ops:
  0.6 0.0 copy-start.2
  0.7 0.0 copy-start
  0.7 2.9 %edges.1 = (f32[9,8,128]{2,1,0:T(8,128)S(1)}, f32[9,8,128]{2,1,0:T(8,128)S(1)}, f32[9,16,128]{2,1,0:T(8,128)S(1)}, f32[9,16,128]{2,1,0:T(8,128)S(1)}, f32[3,256,8,128]{3,2,1,0:T(8,128)S(1)}) custom-call(f32[3,256,8,128]{3,2,1,0:T(8,128)} %v_hbm), custom_call_target="tpu_custom_call" | custom-call | flops 805306368 | bytes 12582912 | tf_op jit(solution)/shard_map/edges/pallas_call | solution.py:223
  3.6 0.0 collective-permute-start
  3.6 2.9 %collective-permute-start.1 = (f32[9,8,128]{2,1,0:T(8,128)S(1)}, f32[9,8,128]{2,1,0:T(8,128)S(1)}, u32[]{:S(2)}, u32[]{:S(2)}) collective-permute-start(f32[9,8,128]{2,1,0:T(8,128)S(1)} %get-tuple-element.47), channel_id=1, source_target_pairs={{16,0},{32,16},{48,32},{64,48},{80,64},{96,80},{112,96},{0,112},{1... | collective-permute-start | bytes 110600 | tf_op jit(solution)/shard_map/ppermute | solution.py:599
  6.5 2.0 %collective-permute-start.2 = (f32[9,16,128]{2,1,0:T(8,128)S(1)}, f32[9,16,128]{2,1,0:T(8,128)S(1)}, u32[]{:S(2)}, u32[]{:S(2)}) collective-permute-start(f32[9,16,128]{2,1,0:T(8,128)S(1)} %get-tuple-element.48.own_r), channel_id=1, source_target_pairs={{0,1},{1,2},{2,3},{3,4},{4,5},{5,6},{6,7},{7,8},{8,9},{9,10},{10,1... | collective-permute-start | bytes 221192 | tf_op jit(solution)/shard_map/ppermute | solution.py:598
  8.5 4.6 %collective-permute-start.3 = (f32[9,16,128]{2,1,0:T(8,128)S(1)}, f32[9,16,128]{2,1,0:T(8,128)S(1)}, u32[]{:S(2)}, u32[]{:S(2)}) collective-permute-start(f32[9,16,128]{2,1,0:T(8,128)S(1)} %get-tuple-element.49.own_l), channel_id=1, source_target_pairs={{1,0},{2,1},{3,2},{4,3},{5,4},{6,5},{7,6},{8,7},{9,8},{10,9},{11,1... | collective-permute-start | bytes 221192 | tf_op jit(solution)/shard_map/ppermute | solution.py:599
  13.1 3.1 %inner_z.1 = (f32[256,8,128]{2,1,0:T(8,128)S(1)}, f32[256,8,128]{2,1,0:T(8,128)S(1)}, f32[256,8,128]{2,1,0:T(8,128)S(1)}, f32[256,8,128]{2,1,0:T(8,128)S(1)}, f3...) custom-call(f32[3,256,8,128]{3,2,1,0:T(8,128)S(1)} %get-tuple-element.44.v_ref, bf16[2,128,128]{2,1,0:T(8,128)(2,1)S(1)} %copy-done.2), custom_call_target="tpu_custom_call" | custom-call | flops 805306368 | bytes 12582912 | tf_op jit(solution)/shard_map/inner_z/pallas_call | solution.py:332
  16.2 0.0 collective-permute-done.xl
  16.2 0.0 collective-permute-done.1.xr
  16.2 0.0 collective-permute-done.2.zl
  16.2 0.0 collective-permute-done.3.zr
  16.2 2.2 %slopes_first.1 = (f32[256,8,128]{2,1,0:T(8,128)S(1)}, f32[256,8,128]{2,1,0:T(8,128)S(1)}, f32[2,8,128]{2,1,0:T(8,128)S(1)}, f32[2,16,128]{2,1,0:T(8,128)S(1)}, bf16[2048,128]{1,0:T(8,128)(2,1)S(1)}) custom-call(f32[3,256,8,128]{3,2,1,0:T(8,128)S(1)} %get-tuple-element.44.v_ref, f32[256,8,128]{2,1,0:T(8,128)S(1)} %get-tuple-element.45.i_ref, ...), custom_call_target="tpu_custom_call" | custom-call | flops 268435456 | bytes 4194304 | tf_op jit(solution)/shard_map/slopes_first/pallas_call | solution.py:407
  18.5 0.1 collective-permute-start.4
  18.6 0.1 collective-permute-start.5
  18.7 2.3 %slopes_x.1 = f32[3,256,8,128]{3,2,1,0:T(8,128)} custom-call(f32[3,256,8,128]{3,2,1,0:T(8,128)S(1)} %get-tuple-element.44.v_ref, f32[256,8,128]{2,1,0:T(8,128)S(1)} %get-tuple-element.54.gu_ref.u_ref, f32[9,8,128]{2,1,0:T(8,128)S(1)} %collective-permute-done.xl, f32[9,8,128]{2,1,0:T(8,128)S(1)} %collective-permute-done.1.xr), custom_call_target="tpu_custom_call" | custom-call | flops 268435456 | bytes 4194304 | tf_op jit(solution)/shard_map/slopes_x/pallas_call | solution.py:439
  21.0 0.0 collective-permute-done.4
  21.0 1.4 %collective-permute-done.5 = f32[2,16,128]{2,1,0:T(8,128)S(1)} collective-permute-done((f32[2,16,128]{2,1,0:T(8,128)S(1)}, f32[2,16,128]{2,1,0:T(8,128)S(1)}, u32[]{:S(2)}, u32[]{:S(2)}) %collective-permute-start.5) | collective-permute-done | bytes 16416 | tf_op jit(solution)/shard_map/ppermute | solution.py:605
  22.4 0.4 collective-permute-start.6
  22.8 1.1 %collective-permute-start.7 = (f32[2,16,128]{2,1,0:T(8,128)S(1)}, f32[2,16,128]{2,1,0:T(8,128)S(1)}, u32[]{:S(2)}, u32[]{:S(2)}) collective-permute-start(f32[2,16,128]{2,1,0:T(8,128)S(1)} %fusion.3), channel_id=1, source_target_pairs={{0,2},{1,3},{2,0},{3,1},{4,6},{5,7},{6,4},{7,5},{8,10},{9,11},{10,... | collective-permute-start | bytes 49160 | tf_op jit(solution)/shard_map/ppermute | solution.py:605
  23.9 1.8 %slopes_z.1 = f32[3,256,8,128]{3,2,1,0:T(8,128)} custom-call(f32[256,8,128]{2,1,0:T(8,128)S(1)} %get-tuple-element.58.iu_ref, f32[256,8,128]{2,1,0:T(8,128)S(1)} %get-tuple-element.59.iv_ref, f32[256,8,128]{2,1,0:T(8,128)S(1)} %get-tuple-element.60.gw_ref.w_ref, bf16[2048,128]{1,0:T(8,128)(2,1)S(1)} %get-tuple-element.61.st_ref, bf16[6,128,128]{2,1,0:T(8,128)(2,1)S(1)} %copy-done), custom_call_target="tpu_custom_call" | custom-call | flops 268435456 | bytes 4194304 | tf_op jit(solution)/shard_map/slopes_z/pallas_call | solution.py:472
  25.7 0.4 collective-permute-done.6
  26.1 1.9 %collective-permute-done.7 = f32[2,16,128]{2,1,0:T(8,128)S(1)} collective-permute-done((f32[2,16,128]{2,1,0:T(8,128)S(1)}, f32[2,16,128]{2,1,0:T(8,128)S(1)}, u32[]{:S(2)}, u32[]{:S(2)}) %collective-permute-start.7) | collective-permute-done | bytes 16416 | tf_op jit(solution)/shard_map/ppermute | solution.py:605
  28.0 2.8 %collective-permute-start.8 = (f32[2,8,128]{2,1,0:T(8,128)S(1)}, f32[2,8,128]{2,1,0:T(8,128)S(1)}, u32[]{:S(2)}, u32[]{:S(2)}) collective-permute-start(f32[2,8,128]{2,1,0:T(8,128)S(1)} %fusion.6), channel_id=1, source_target_pairs={{0,64},{16,80},{32,96},{48,112},{64,0},{80,16},{96,32},{112,48},{1... | collective-permute-start | bytes 24584 | tf_op jit(solution)/shard_map/ppermute | solution.py:605
  30.8 0.0 collective-permute-start.9
  30.8 2.3 %divergence.2.rest_2_ = f32[3,256,8,128]{3,2,1,0:T(8,128)} custom-call(f32[3,256,8,128]{3,2,1,0:T(8,128)S(1)} %get-tuple-element.44.v_ref, f32[9,8,128]{2,1,0:T(8,128)S(1)} %collective-permute-done.xl, f32[9,8,128]{2,1,0:T(8,128)S(1)} %collective-permute-done.1.xr, bf16[2048,128]{1,0:T(8,128)(2,1)S(1)} %get-tuple-element.61.st_ref, ...), custom_call_target="tpu_custom_call" | custom-call | flops 268435456 | bytes 4194304 | tf_op jit(solution)/shard_map/divergence/pallas_call | solution.py:518
  33.2 0.1 collective-permute-done.8
  33.3 1.3 %collective-permute-done.9 = f32[2,16,128]{2,1,0:T(8,128)S(1)} collective-permute-done((f32[2,16,128]{2,1,0:T(8,128)S(1)}, f32[2,16,128]{2,1,0:T(8,128)S(1)}, u32[]{:S(2)}, u32[]{:S(2)}) %collective-permute-start.9) | collective-permute-done | bytes 16416 | tf_op jit(solution)/shard_map/ppermute | solution.py:605
  34.6 1.9 %collective-permute-start.10 = (f32[2,16,128]{2,1,0:T(8,128)S(1)}, f32[2,16,128]{2,1,0:T(8,128)S(1)}, u32[]{:S(2)}, u32[]{:S(2)}) collective-permute-start(f32[2,16,128]{2,1,0:T(8,128)S(1)} %add.79), channel_id=1, source_target_pairs={{0,8},{1,9},{2,10},{3,11},{4,12},{5,13},{6,14},{7,15},{8,0},{9,1},... | collective-permute-start | bytes 49160 | tf_op jit(solution)/shard_map/ppermute | solution.py:605
  36.6 4.2 %divergence.3 = f32[3,256,8,128]{3,2,1,0:T(8,128)} custom-call(f32[3,256,8,128]{3,2,1,0:T(8,128)S(1)} %get-tuple-element.44.v_ref, f32[9,8,128]{2,1,0:T(8,128)S(1)} %collective-permute-done.xl, f32[9,8,128]{2,1,0:T(8,128)S(1)} %collective-permute-done.1.xr, bf16[2048,128]{1,0:T(8,128)(2,1)S(1)} %get-tuple-element.61.st_ref, ...), custom_call_target="tpu_custom_call", output_to_operand_aliasing={{}: (7, {})} | custom-call | flops 536870912 | bytes 8388608 | tf_op jit(solution)/shard_map/divergence/pallas_call | solution.py:518
  40.8 0.0 collective-permute-done.10
  40.8 2.2 %rebuild.1 = f32[2,256,8,128]{3,2,1,0:T(8,128)} custom-call(f32[256,8,128]{2,1,0:T(8,128)S(1)} %get-tuple-element.54.gu_ref.u_ref, f32[256,8,128]{2,1,0:T(8,128)S(1)} %get-tuple-element.60.gw_ref.w_ref, f32[2,8,128]{2,1,0:T(8,128)S(1)} %pad_maximum_fusion.3.xt, f32[2,16,128]{2,1,0:T(8,128)S(1)} %pad_maximum_fusion.1.zt, bf16[2,256,128]{2,1,0:T(8,128)(2,1)S(1)} %copy-done.1), custom_call_target="tpu_custom_call" | custom-call | flops 268435456 | bytes 4194304 | tf_op jit(solution)/shard_map/rebuild/pallas_call | solution.py:580
  (19 shorter events, 0.1 us)
Async XLA Ops:
  0.6 12.5 %copy-start.2 = (bf16[2,128,128]{2,1,0:T(8,128)(2,1)S(1)}, bf16[2,128,128]{2,1,0:T(8,128)(2,1)}, u32[]{:S(2)}) copy-start(bf16[2,128,128]{2,1,0:T(8,128)(2,1)} %constant.47.clone.m_ref) | copy-start | bytes 196612
  0.7 15.5 %copy-start = (bf16[6,128,128]{2,1,0:T(8,128)(2,1)S(1)}, bf16[6,128,128]{2,1,0:T(8,128)(2,1)}, u32[]{:S(2)}) copy-start(bf16[6,128,128]{2,1,0:T(8,128)(2,1)} %constant.48.clone.m_ref) | copy-start | bytes 589828
  3.6 12.6 %collective-permute-start = (f32[9,8,128]{2,1,0:T(8,128)S(1)}, f32[9,8,128]{2,1,0:T(8,128)S(1)}, u32[]{:S(2)}, u32[]{:S(2)}) collective-permute-start(f32[9,8,128]{2,1,0:T(8,128)S(1)} %get-tuple-element.46), channel_id=1, source_target_pairs={{0,16},{16,32},{32,48},{48,64},{64,80},{80,96},{96,112},{112,0},{1... | collective-permute-start | bytes 110600 | tf_op jit(solution)/shard_map/ppermute | solution.py:598
  3.6 12.6 %collective-permute-start.1 = (f32[9,8,128]{2,1,0:T(8,128)S(1)}, f32[9,8,128]{2,1,0:T(8,128)S(1)}, u32[]{:S(2)}, u32[]{:S(2)}) collective-permute-start(f32[9,8,128]{2,1,0:T(8,128)S(1)} %get-tuple-element.47), channel_id=1, source_target_pairs={{16,0},{32,16},{48,32},{64,48},{80,64},{96,80},{112,96},{0,112},{1... | collective-permute-start | bytes 110600 | tf_op jit(solution)/shard_map/ppermute | solution.py:599
  6.5 9.7 %collective-permute-start.2 = (f32[9,16,128]{2,1,0:T(8,128)S(1)}, f32[9,16,128]{2,1,0:T(8,128)S(1)}, u32[]{:S(2)}, u32[]{:S(2)}) collective-permute-start(f32[9,16,128]{2,1,0:T(8,128)S(1)} %get-tuple-element.48.own_r), channel_id=1, source_target_pairs={{0,1},{1,2},{2,3},{3,4},{4,5},{5,6},{6,7},{7,8},{8,9},{9,10},{10,1... | collective-permute-start | bytes 221192 | tf_op jit(solution)/shard_map/ppermute | solution.py:598
  8.5 7.7 %collective-permute-start.3 = (f32[9,16,128]{2,1,0:T(8,128)S(1)}, f32[9,16,128]{2,1,0:T(8,128)S(1)}, u32[]{:S(2)}, u32[]{:S(2)}) collective-permute-start(f32[9,16,128]{2,1,0:T(8,128)S(1)} %get-tuple-element.49.own_l), channel_id=1, source_target_pairs={{1,0},{2,1},{3,2},{4,3},{5,4},{6,5},{7,6},{8,7},{9,8},{10,9},{11,1... | collective-permute-start | bytes 221192 | tf_op jit(solution)/shard_map/ppermute | solution.py:599
  18.5 2.5 %collective-permute-start.4 = (f32[2,8,128]{2,1,0:T(8,128)S(1)}, f32[2,8,128]{2,1,0:T(8,128)S(1)}, u32[]{:S(2)}, u32[]{:S(2)}) collective-permute-start(f32[2,8,128]{2,1,0:T(8,128)S(1)} %pad_maximum_fusion.2), channel_id=1, source_target_pairs={{0,16},{16,0},{32,48},{48,32},{64,80},{80,64},{96,112},{112,96},{1... | collective-permute-start | bytes 24584 | tf_op jit(solution)/shard_map/ppermute | solution.py:605
  18.6 3.8 %collective-permute-start.5 = (f32[2,16,128]{2,1,0:T(8,128)S(1)}, f32[2,16,128]{2,1,0:T(8,128)S(1)}, u32[]{:S(2)}, u32[]{:S(2)}) collective-permute-start(f32[2,16,128]{2,1,0:T(8,128)S(1)} %pad_maximum_fusion), channel_id=1, source_target_pairs={{0,1},{1,0},{2,3},{3,2},{4,5},{5,4},{6,7},{7,6},{8,9},{9,8},{10,11... | collective-permute-start | bytes 49160 | tf_op jit(solution)/shard_map/ppermute | solution.py:605
  22.4 3.7 %collective-permute-start.6 = (f32[2,8,128]{2,1,0:T(8,128)S(1)}, f32[2,8,128]{2,1,0:T(8,128)S(1)}, u32[]{:S(2)}, u32[]{:S(2)}) collective-permute-start(f32[2,8,128]{2,1,0:T(8,128)S(1)} %fusion.2), channel_id=1, source_target_pairs={{0,32},{16,48},{32,0},{48,16},{64,96},{80,112},{96,64},{112,80},{1... | collective-permute-start | bytes 24584 | tf_op jit(solution)/shard_map/ppermute | solution.py:605
  22.8 5.2 %collective-permute-start.7 = (f32[2,16,128]{2,1,0:T(8,128)S(1)}, f32[2,16,128]{2,1,0:T(8,128)S(1)}, u32[]{:S(2)}, u32[]{:S(2)}) collective-permute-start(f32[2,16,128]{2,1,0:T(8,128)S(1)} %fusion.3), channel_id=1, source_target_pairs={{0,2},{1,3},{2,0},{3,1},{4,6},{5,7},{6,4},{7,5},{8,10},{9,11},{10,... | collective-permute-start | bytes 49160 | tf_op jit(solution)/shard_map/ppermute | solution.py:605
  28.0 5.2 %collective-permute-start.8 = (f32[2,8,128]{2,1,0:T(8,128)S(1)}, f32[2,8,128]{2,1,0:T(8,128)S(1)}, u32[]{:S(2)}, u32[]{:S(2)}) collective-permute-start(f32[2,8,128]{2,1,0:T(8,128)S(1)} %fusion.6), channel_id=1, source_target_pairs={{0,64},{16,80},{32,96},{48,112},{64,0},{80,16},{96,32},{112,48},{1... | collective-permute-start | bytes 24584 | tf_op jit(solution)/shard_map/ppermute | solution.py:605
  30.8 3.7 %collective-permute-start.9 = (f32[2,16,128]{2,1,0:T(8,128)S(1)}, f32[2,16,128]{2,1,0:T(8,128)S(1)}, u32[]{:S(2)}, u32[]{:S(2)}) collective-permute-start(f32[2,16,128]{2,1,0:T(8,128)S(1)} %fusion.7), channel_id=1, source_target_pairs={{0,4},{1,5},{2,6},{3,7},{4,0},{5,1},{6,2},{7,3},{8,12},{9,13},{10,... | collective-permute-start | bytes 49160 | tf_op jit(solution)/shard_map/ppermute | solution.py:605
  34.6 6.2 %collective-permute-start.10 = (f32[2,16,128]{2,1,0:T(8,128)S(1)}, f32[2,16,128]{2,1,0:T(8,128)S(1)}, u32[]{:S(2)}, u32[]{:S(2)}) collective-permute-start(f32[2,16,128]{2,1,0:T(8,128)S(1)} %add.79), channel_id=1, source_target_pairs={{0,8},{1,9},{2,10},{3,11},{4,12},{5,13},{6,14},{7,15},{8,0},{9,1},... | collective-permute-start | bytes 49160 | tf_op jit(solution)/shard_map/ppermute | solution.py:605
  36.5 4.3 %copy-start.1 = (bf16[2,256,128]{2,1,0:T(8,128)(2,1)S(1)}, bf16[2,256,128]{2,1,0:T(8,128)(2,1)}, u32[]{:S(2)}) copy-start(bf16[2,256,128]{2,1,0:T(8,128)(2,1)} %constant.49.clone.m_ref) | copy-start | bytes 393220

commit v3 on v2

v3 whole, which is shorter than its diff:
```python
import math

import jax
import jax.numpy as jnp
import numpy as np
from jax import lax
from jax.experimental import pallas as pl
from jax.experimental.pallas import tpu as pltpu
from jax.sharding import PartitionSpec as P

ALPHA = 1.0 / 3.0
COEF_A = 14.0 / 9.0
COEF_B = 1.0 / 9.0
LANES = 128
F32 = jnp.float32
VMEM = pl.BlockSpec(memory_space=pltpu.VMEM)
HBM = pl.BlockSpec(memory_space=pltpu.HBM)
ANY = pl.BlockSpec(memory_space=pl.ANY)
BF16 = jnp.bfloat16

RHO = (-1.0 + math.sqrt(1.0 - 4.0 * ALPHA * ALPHA)) / (2.0 * ALPHA)


def kernel_weights():
    reach = 400
    k = np.arange(-reach, reach + 1)
    green = RHO ** np.abs(k).astype(np.float64) / math.sqrt(1.0 - 4.0 * ALPHA * ALPHA)

    def shifted(s):
        out = np.zeros_like(green)
        if s >= 0:
            out[s:] = green[: len(green) - s]
        else:
            out[:s] = green[-s:]
        return out

    direct = 0.5 * COEF_A * (shifted(-1) - shifted(1)) + 0.25 * COEF_B * (shifted(-2) - shifted(2))
    total = np.concatenate([[0.0], np.cumsum(direct)])
    return {m: total[m + reach] for m in range(-2, 4)}


_W = kernel_weights()
NEAR = _W[1]
TAIL = _W[2] / RHO**2
KAPPA = TAIL * RHO * RHO
TOGETHER = 16
REACH = 96


def h_of(m):
    m = np.asarray(m)
    m = np.where(m <= 0, 1 - m, m)
    return np.where(m == 1, NEAR, TAIL * RHO ** m.astype(np.float64))


def split_np(x):
    hi = x.astype(BF16)
    lo = (x - hi.astype(np.float64)).astype(BF16)
    return hi, lo


def going_up(length):
    j = np.arange(length)
    w = (RHO - 1.0) * RHO ** (length - j).astype(np.float64)
    w[-1] = RHO**2
    return w


def going_down(length):
    return going_up(length)[::-1] * -1.0


def z_inner():
    j = np.arange(LANES)
    inner = h_of(j[None, :] - j[:, None])
    inner[LANES - 1] = 0.0
    hi, lo = split_np(inner)
    return np.stack([hi, lo])


def z_rims(fields):
    j = np.arange(LANES)
    rim = np.stack(
        [
            h_of(j + 1),
            TAIL * RHO ** j.astype(np.float64),
            h_of(LANES - j),
            TAIL * RHO ** (LANES - 1 - j).astype(np.float64),
        ]
    )
    hi, lo = split_np(rim)
    out = np.zeros((fields, LANES, LANES), BF16)
    for f in range(fields):
        out[f, 12 * f : 12 * f + 12] = np.concatenate([hi, hi, lo], 0)
    return out


def sum_matrices():
    j = np.arange(LANES)
    lower = (j[:, None] < j[None, :]) + 0.5 * (j[:, None] == j[None, :])
    ones = np.ones((3, LANES))
    slope = -np.broadcast_to(j, (3, LANES))
    pad = np.zeros((LANES - 6, LANES))
    first = np.concatenate([lower, lower], 0)
    second = np.concatenate([lower, ones, slope, pad], 0)
    return np.stack([first, second]).astype(BF16)


def split2(x):
    hi = x.astype(BF16)
    return hi, (x - hi.astype(F32)).astype(BF16)


def split3(x):
    hi = x.astype(BF16)
    rest = x - hi.astype(F32)
    mid = rest.astype(BF16)
    return hi, mid, (rest - mid.astype(F32)).astype(BF16)


def dot(a, b):
    return lax.dot_general(a, b, (((1,), (0,)), ((), ())), preferred_element_type=F32)


def product(values, name):
    out = values[name[0]]
    for c in name[1:]:
        out = out * values[c]
    return out


COMP = {"u": 0, "v": 1, "w": 2}


X_SUMS = ["u", "v", "w", "uu", "uv", "uw"]
Z_SUMS = ["u", "v", "w", "wu", "wv", "ww"]
CELLS = ["u", "v", "w"]


def z_weights(nz, cut):
    row = lax.broadcasted_iota(jnp.int32, (8, LANES), 0)

    def tiles(powers, factors):
        tile = jnp.zeros((8, LANES), F32)
        for k in range(8):
            tile = jnp.where(row == k, np.float32(powers[k]), tile)
        return [tile * np.float32(f) for f in factors]

    up = going_up(nz)[nz - cut :]
    down = going_down(nz)[:cut]
    ups = tiles(up[:8] / up[0], up[::8])
    ups[-1] = jnp.where(row == 7, np.float32(up[-1]), ups[-1])
    steady = down[8:16] / down[8]
    downs = tiles(steady, [down[8] / RHO**8] + list(down[8::8]))
    downs[0] = jnp.where(row == 0, np.float32(down[0]), downs[0])
    return jnp.concatenate(ups, 0), jnp.concatenate(downs, 0)


def edges_call(velocity):
    _, nx, ny, nz = velocity.shape
    sub = LANES // ny
    chunks = nx // sub
    nq = len(Z_SUMS) + len(CELLS)
    cut_x = min(REACH, nx)
    cut = min(REACH, nz)
    group = 8
    parts = 8
    part = nx // parts

    def body(v_hbm, xu_ref, xd_ref, zu_ref, zd_ref, v_ref, sems):
        copies = [
            pltpu.make_async_copy(
                v_hbm.at[:, pl.ds(p * part, part)], v_ref.at[:, pl.ds(p * part, part)], sems.at[p]
            )
            for p in range(parts)
        ]
        for copy in copies:
            copy.start()
        weight_up, weight_down = z_weights(nz, cut)

        def x_rows(acc, weights, rows):
            for i in rows:
                vals = {c: v_ref[COMP[c], i] for c in CELLS}
                for q, name in enumerate(X_SUMS):
                    term = product(vals, name) * np.float32(weights[i])
                    acc[q] = term if acc[q] is None else acc[q] + term

        ups = [None] * len(X_SUMS)
        downs = [None] * len(X_SUMS)
        rows = {}
        for p in range(parts):
            copies[p].wait()
            for s in range(p * part // sub, (p + 1) * part // sub):
                t = {c: v_ref[COMP[c], s * sub : (s + 1) * sub].reshape(LANES, nz).T for c in CELLS}
                for q, name in enumerate(Z_SUMS):
                    f = product(t, name)
                    up = jnp.sum(f[nz - cut :] * weight_up, axis=0, keepdims=True)
                    down = jnp.sum(f[:cut] * weight_down, axis=0, keepdims=True)
                    rows.setdefault(q, []).append((up, down))
                for q, name in enumerate(CELLS):
                    rows.setdefault(len(Z_SUMS) + q, []).append((t[name][nz - 1 : nz], t[name][0:1]))
                if (s + 1) % group == 0:
                    at = s + 1 - group
                    for q, pairs in rows.items():
                        zu_ref[q, at : at + group] = jnp.concatenate([r[0] for r in pairs], 0)
                        zd_ref[q, at : at + group] = jnp.concatenate([r[1] for r in pairs], 0)
                    rows = {}
            here = range(p * part, (p + 1) * part)
            x_rows(downs, going_down(nx), [i for i in here if i < cut_x])
            x_rows(ups, going_up(nx), [i for i in here if i >= nx - cut_x])
        for q in range(len(X_SUMS)):
            xu_ref[q] = ups[q]
            xd_ref[q] = downs[q]
        for q in range(len(CELLS)):
            xu_ref[len(X_SUMS) + q] = v_ref[q, nx - 1]
            xd_ref[len(X_SUMS) + q] = v_ref[q, 0]

    xs = jax.ShapeDtypeStruct((nq, ny, nz), F32)
    zs = jax.ShapeDtypeStruct((nq, chunks, LANES), F32)
    return pl.pallas_call(
        body,
        in_specs=[HBM],
        out_specs=[VMEM] * 5,
        out_shape=[xs, xs, zs, zs, jax.ShapeDtypeStruct(velocity.shape, F32)],
        scratch_shapes=[pltpu.SemaphoreType.DMA((parts,))],
        compiler_params=params(),
        name="edges",
        cost_estimate=cost(6, nx * ny * nz),
    )(pltpu.with_memory_space_constraint(velocity, pltpu.HBM))


def x_derivatives(read, write, scratch, nx, rims, pieces=1, done=None):
    unroll = 8
    half = nx // 2
    blocks = half // unroll
    fields = range(len(rims))
    grown = [KAPPA * RHO ** -(k + 1) for k in range(unroll)]
    power = [RHO**k for k in range(unroll + 1)]

    def sweep(first):
        def step(b, carry):
            out = []
            lows = (0 if first else half) + b * unroll
            highs = (nx if first else half) - 1 - b * unroll
            for f in fields:
                low, before, here, high, after, there = carry[f]
                _, cell_before, _, cell_after = rims[f]
                for k in range(unroll):
                    i = lows + k
                    part = low if k == 0 else power[k] * low
                    edge = here - before
                    if first:
                        nxt = read(f, i + 1)
                        scratch(f)[i] = part
                    else:
                        if k == unroll - 1:
                            inside = read(f, jnp.minimum(i + 1, nx - 1))
                            nxt = jnp.where(b == blocks - 1, cell_after, inside)
                        else:
                            nxt = read(f, i + 1)
                        write(f, i, scratch(f)[i] + (part + NEAR * (nxt - before)))
                    low = low + grown[k] * edge
                    before, here = here, nxt

                    i = highs - k
                    part = high if k == 0 else power[k] * high
                    edge = after - there
                    if first:
                        nxt = read(f, i - 1)
                        scratch(f)[i] = part
                    else:
                        if k == unroll - 1:
                            inside = read(f, jnp.maximum(i - 1, 0))
                            nxt = jnp.where(b == blocks - 1, cell_before, inside)
                        else:
                            nxt = read(f, i - 1)
                        write(f, i, scratch(f)[i] + (part + NEAR * (after - nxt)))
                    high = high + grown[k] * edge
                    after, there = there, nxt
                out.append((power[unroll] * low, before, here, power[unroll] * high, after, there))
            return tuple(out)

        return step

    carry = tuple(
        (TAIL * sum_before, cell_before, read(f, 0), TAIL * sum_after, cell_after, read(f, nx - 1))
        for f, (sum_before, cell_before, sum_after, cell_after) in enumerate(rims)
    )
    carry = lax.fori_loop(0, blocks, sweep(True), carry)
    for p in range(pieces):
        lo, hi = p * blocks // pieces, (p + 1) * blocks // pieces
        carry = lax.fori_loop(lo, hi, sweep(False), carry)
        if done is not None:
            done(half + lo * unroll, (hi - lo) * unroll)
            done(half - hi * unroll, (hi - lo) * unroll)


class Outbox:
    def __init__(self, sems):
        self.sems, self.copies = sems, []

    def send(self, src, dst):
        copy = pltpu.make_async_copy(src, dst, self.sems.at[len(self.copies)])
        copy.start()
        self.copies.append(copy)

    def wait(self):
        for copy in self.copies:
            copy.wait()


def params(mib=8):
    return pltpu.CompilerParams(vmem_limit_bytes=mib * 2**20)


def cost(fields, size):
    return pl.CostEstimate(flops=fields * size * 512, transcendentals=0, bytes_accessed=fields * size * 8)


def inner_z(velocity, inner):
    _, nx, ny, nz = velocity.shape
    rows = nx * ny

    def body(v_ref, m_ref, w_out, u_out, v_out, *c_outs):
        outs = (u_out, v_out, w_out) + c_outs
        keep = lax.broadcasted_iota(jnp.int32, (rows, LANES), 1) < LANES - 1
        both = jnp.concatenate([m_ref[0], m_ref[0]], 0)
        w = v_ref[2].reshape(rows, nz)
        for c in range(6):
            f = v_ref[c % 3].reshape(rows, nz)
            if c >= 3:
                f = f * w
            e = jnp.where(keep, pltpu.roll(f, LANES - 1, 1) - f, 0.0)
            hi, lo = split2(e)
            g = dot(jnp.concatenate([hi, lo], 1), both) + dot(hi, m_ref[1])
            outs[c][...] = g.reshape(nx, ny, nz)

    return pl.pallas_call(
        body,
        in_specs=[VMEM, VMEM],
        out_specs=[VMEM] * 6,
        out_shape=[jax.ShapeDtypeStruct(velocity.shape[1:], F32)] * 6,
        compiler_params=params(),
        name="inner_z",
        cost_estimate=cost(6, nx * ny * nz),
    )(velocity, inner)


def slopes_first(velocity, inner, x_halo, z_halo, rims):
    _, nx, ny, nz = velocity.shape
    sub = LANES // ny
    chunks = nx // sub
    rows = nx * ny

    def body(v_ref, i_ref, xl, xr, zl, zr, own_l, own_r, m_ref, gu, gw, tx, tz, st, px, pz, scratch, rim):
        used = 12 * len(Z_SUMS)
        rim[:, used:, :] = jnp.zeros((chunks, LANES - used, LANES), F32)
        for f in range(6):
            cells = [r[6 + f % 3] for r in (zl, own_l, own_r, zr)]
            if f >= 3:
                cells = [c * r[8] for c, r in zip(cells, (zl, own_l, own_r, zr))]
            terms = [cells[1] - cells[0], zl[f], cells[3] - cells[2], zr[f]]
            for q, term in enumerate(terms):
                hi = term.astype(BF16).astype(F32)
                lo = (term - hi).astype(BF16).astype(F32)
                rim[:, 12 * f + q, :] = hi
                rim[:, 12 * f + 4 + q, :] = lo
                rim[:, 12 * f + 8 + q, :] = hi
        for c in range(chunks):
            st[c * LANES : (c + 1) * LANES] = rim[c].T.astype(BF16)

        g = i_ref[...].reshape(rows, nz) + dot(st[...], m_ref[2])
        gw[...] = g.reshape(nx, ny, nz)

        def write_x(_, i, g):
            gu[i] = g

        rims_x = [(xl[0], xl[6], xr[0], xr[6])]
        x_derivatives(lambda _, i: v_ref[0, i], write_x, lambda _: scratch, nx, rims_x)

        zero = jnp.zeros((ny, nz), F32)
        ways = 4

        def add(b, carry):
            out = []
            for k, (total, moment) in enumerate(carry):
                for n in range(2):
                    i = b * 2 * ways + 2 * k + n
                    g = gw[i]
                    total = total + g
                    moment = moment + (i.astype(F32) - 0.5 * (nx - 1)) * g
                out.append((total, moment))
            return tuple(out)

        got = lax.fori_loop(0, nx // (2 * ways), add, ((zero, zero),) * ways)
        bits, centre, start = place("gx", nx)
        total = (got[0][0] + got[1][0]) + (got[2][0] + got[3][0])
        tx[0] = total
        tx[1] = (got[0][1] + got[1][1]) + (got[2][1] + got[3][1]) + centre * total
        for k, value in enumerate([*bits, start]):
            px[k] = jnp.full((ny, nz), value, F32)

        at = lax.broadcasted_iota(jnp.int32, (nz, LANES), 0).astype(F32) - 0.5 * (nz - 1)
        totals, moments = [], []
        for c in range(chunks):
            t = gu[c * sub : (c + 1) * sub].reshape(LANES, nz).T
            totals.append(jnp.sum(t, axis=0, keepdims=True))
            moments.append(jnp.sum(t * at, axis=0, keepdims=True))
        bits, centre, start = place("gz", nz)
        total = jnp.concatenate(totals, 0)
        tz[0] = total
        tz[1] = jnp.concatenate(moments, 0) + centre * total
        for k, value in enumerate([*bits, start]):
            pz[k] = jnp.full((chunks, LANES), value, F32)

    one = jax.ShapeDtypeStruct(velocity.shape[1:], F32)
    sx = jax.ShapeDtypeStruct((2, ny, nz), F32)
    sz = jax.ShapeDtypeStruct((2, chunks, LANES), F32)
    st = jax.ShapeDtypeStruct((rows, LANES), BF16)
    small = [*x_halo, *z_halo, rims]
    steps_x = sum(count - 1 for count, _ in LEVELS["gx"])
    steps_z = sum(count - 1 for count, _ in LEVELS["gz"])
    px = jax.ShapeDtypeStruct((steps_x + 1, ny, nz), F32)
    pz = jax.ShapeDtypeStruct((steps_z + 1, chunks, LANES), F32)
    outs = [one, one, sx, sz, st, px, pz]
    return pl.pallas_call(
        body,
        in_specs=[VMEM] * (2 + len(small)),
        out_specs=[VMEM] * len(outs),
        out_shape=outs,
        scratch_shapes=[pltpu.VMEM((nx, ny, nz), F32), pltpu.VMEM((chunks, LANES, LANES), F32)],
        compiler_params=params(),
        name="slopes_first",
        cost_estimate=cost(2, nx * ny * nz),
    )(velocity, inner, *small)


def slopes_rest(velocity, inner_u, inner_v, x_halo, st, rims, gw):
    _, nx, ny, nz = velocity.shape
    rows = nx * ny
    parts = 2

    def body(v_ref, iu_ref, iv_ref, xl, xr, st_ref, m_ref, gw_ref, gv, gx, out, s0, s1, made, sems):
        box = Outbox(sems)
        box.send(gw_ref, out.at[2])
        for c, i_ref in enumerate((iu_ref, iv_ref)):
            for p in range(parts):
                at = pl.ds(p * nx // parts, nx // parts)
                local = i_ref[at].reshape(rows // parts, nz)
                g = local + dot(st_ref[pl.ds(p * rows // parts, rows // parts)], m_ref[c])
                made[c, at] = g.reshape(nx // parts, ny, nz)
                box.send(made.at[c, at], out.at[c, at])

        def write(f, i, g):
            (gv, gx)[f][i] = g

        x_derivatives(
            lambda f, i: v_ref[1 + f, i],
            write,
            lambda f: (s0, s1)[f],
            nx,
            [(xl[c], xl[6 + c], xr[c], xr[6 + c]) for c in (1, 2)],
        )
        box.wait()

    one = jax.ShapeDtypeStruct((nx, ny, nz), F32)
    return pl.pallas_call(
        body,
        in_specs=[VMEM] * 8,
        out_specs=[VMEM, VMEM, ANY],
        out_shape=[one, one, jax.ShapeDtypeStruct(velocity.shape, F32)],
        scratch_shapes=[
            pltpu.VMEM((nx, ny, nz), F32),
            pltpu.VMEM((nx, ny, nz), F32),
            pltpu.VMEM((2, nx, ny, nz), F32),
            pltpu.SemaphoreType.DMA((8,)),
        ],
        compiler_params=params(),
        name="slopes_rest",
        cost_estimate=cost(3, nx * ny * nz),
    )(velocity, inner_u, inner_v, *x_halo, st, rims, gw)


def divergence(velocity, inner, x_halo, st, rims, slopes):
    _, nx, ny, nz = velocity.shape
    rows = nx * ny
    comps = range(3)

    def body(v_ref, xl, xr, st_ref, m_ref, *rest):
        i_refs, g_refs = rest[:3], rest[3:6]
        gx, out, s0, s1, s2, m0, m1, m2, sems = rest[6:]
        made = (m0, m1, m2)
        box = Outbox(sems)
        for c in comps:
            box.send(g_refs[c], gx.at[c])
        for c in comps:
            g = i_refs[c][...].reshape(rows, nz) + dot(st_ref[...], m_ref[3 + c])
            made[c][...] = g.reshape(nx, ny, nz)

        def write(c, i, g):
            made[c][i] = made[c][i] + g

        def done(start, size):
            at = pl.ds(start, size)
            for c in comps:
                box.send(made[c].at[at], out.at[c, at])

        x_derivatives(
            lambda c, i: v_ref[0, i] * v_ref[c, i],
            write,
            lambda c: (s0, s1, s2)[c],
            nx,
            [(xl[3 + c], xl[6] * xl[6 + c], xr[3 + c], xr[6] * xr[6 + c]) for c in comps],
            4,
            done,
        )
        box.wait()

    full = jax.ShapeDtypeStruct(velocity.shape, F32)
    return pl.pallas_call(
        body,
        in_specs=[VMEM] * 11,
        out_specs=[ANY, ANY],
        out_shape=[full, full],
        scratch_shapes=[pltpu.VMEM((nx, ny, nz), F32)] * 6 + [pltpu.SemaphoreType.DMA((32,))],
        compiler_params=params(12),
        name="divergence",
        cost_estimate=cost(6, nx * ny * nz),
    )(velocity, *x_halo, st, rims, *inner, *slopes)


def rebuild(gu, gw, x_terms, z_terms, mats, total_x, total_z):
    nx, ny, nz = gu.shape
    sub = LANES // ny
    chunks = nx // sub
    rows = nx * ny
    parts = 4
    scale_x = -1.0 / math.sqrt(total_x)
    scale_z = -1.0 / math.sqrt(total_z)

    def body(u_ref, w_ref, xt, zt, m_ref, out, rim, made, sems):
        box = Outbox(sems)
        mean = xt[1]

        def along_x(b, acc):
            for k in range(8):
                i = b * 8 + k
                g = w_ref[i]
                made[0, i] = scale_x * (acc + 0.5 * g)
                acc = acc + (g - mean)
            return acc

        acc = xt[0]
        for p in range(parts):
            acc = lax.fori_loop(p * nx // parts // 8, (p + 1) * nx // parts // 8, along_x, acc)
            at = pl.ds(p * nx // parts, nx // parts)
            box.send(made.at[0, at], out.at[0, at])
        rim[:, 6:, :] = jnp.zeros((chunks, LANES - 6, LANES), F32)
        for q in range(2):
            for p, part in enumerate(split3(zt[q])):
                rim[:, 3 * q + p, :] = part.astype(F32)
        for p in range(parts):
            at = pl.ds(p * nx // parts, nx // parts)
            hi, mid, lo = split3(u_ref[at].reshape(rows // parts, nz))
            here = range(p * chunks // parts, (p + 1) * chunks // parts)
            st = jnp.concatenate([rim[c].T.astype(BF16) for c in here], 0)
            g = dot(jnp.concatenate([hi, mid], 1), m_ref[0]) + dot(
                jnp.concatenate([lo, st], 1), m_ref[1]
            )
            made[1, at] = (scale_z * g).reshape(nx // parts, ny, nz)
            box.send(made.at[1, at], out.at[1, at])
        box.wait()

    shape = (2,) + gu.shape
    return pl.pallas_call(
        body,
        in_specs=[VMEM] * 5,
        out_specs=ANY,
        out_shape=jax.ShapeDtypeStruct(shape, F32),
        scratch_shapes=[
            pltpu.VMEM((chunks, LANES, LANES), F32),
            pltpu.VMEM(shape, F32),
            pltpu.SemaphoreType.DMA((16,)),
        ],
        compiler_params=params(),
        name="rebuild",
        cost_estimate=cost(2, nx * ny * nz),
    )(gu, gw, x_terms, z_terms, mats)


def swap(axis, up, down):
    n = lax.axis_size(axis)
    before = lax.ppermute(up, axis, [(i, (i + 1) % n) for i in range(n)])
    after = lax.ppermute(down, axis, [((i + 1) % n, i) for i in range(n)])
    return before, after


LEVELS = {"gx": [(2, 1), (4, 2)], "gz": [(4, 1), (4, 4)]}


def exchange(axis, terms, level):
    n = lax.axis_size(axis)
    count, stride = level
    parts = {}
    for k in sorted(range(1, count), key=lambda k: min(k, count - k)):
        pairs = []
        for i in range(n):
            own = (i // stride) % count
            pairs.append((i, i + ((own + k) % count - own) * stride))
        parts[k] = lax.ppermute(terms, axis, pairs)
    return parts


def combine(terms, before, parts, lower):
    for k, part in parts.items():
        before = before + lower[k] * part[0]
        terms = terms + part
    return terms, before


def place(axis, cells):
    n = lax.axis_size(axis)
    mine = lax.axis_index(axis)
    below = []
    for count, stride in LEVELS[axis]:
        own = mine // stride % count
        for k in range(1, count):
            below.append((own >= k).astype(F32))
    start = (mine * cells).astype(F32)
    centre = start + (0.5 * (cells - 1) - 0.5 * (n * cells - 1))
    return below, centre, (start + 0.5) * (1.0 / (n * cells))


def below_of(axis, spot, at):
    skip = sum(count - 1 for count, _ in LEVELS[axis][:at])
    count = LEVELS[axis][at][0]
    return {k: spot[skip + k - 1] for k in range(1, count)}


def line_terms(terms, before, start, total_len):
    mean = terms[0] / total_len
    offset = before - start * terms[0] + terms[1] / total_len
    return jnp.stack([offset, mean])


def body(velocity):
    _, nx, ny, nz = velocity.shape
    size_x = lax.axis_size("gx")
    size_z = lax.axis_size("gz")
    total_x = nx * size_x
    total_z = nz * size_z
    inner_mats = jnp.asarray(z_inner())
    rims = jnp.asarray(z_rims(len(Z_SUMS)))
    sums = jnp.asarray(sum_matrices())

    xu, xd, zu, zd, vel = edges_call(velocity)
    z_halo = (*swap("gz", zu, zd), zd, zu)
    x_halo = swap("gx", xu, xd)
    in_w, in_u, in_v, *in_c = inner_z(vel, inner_mats)
    gu, gw, tx, tz, st, spot_x, spot_z = slopes_first(vel, in_w, x_halo, z_halo, rims)
    bx = jnp.zeros_like(tx[0])
    bz = jnp.zeros_like(tz[0])

    px = exchange("gx", tx, LEVELS["gx"][0])
    pz = exchange("gz", tz, LEVELS["gz"][0])
    gv, gq, grad_z = slopes_rest(vel, in_u, in_v, x_halo, st, rims, gw)
    px, pz, gv, gq, grad_z = lax.optimization_barrier((px, pz, gv, gq, grad_z))
    tx, bx = combine(tx, bx, px, below_of("gx", spot_x, 0))
    tz, bz = combine(tz, bz, pz, below_of("gz", spot_z, 0))
    px = exchange("gx", tx, LEVELS["gx"][1])
    pz = exchange("gz", tz, LEVELS["gz"][1])
    grad_x, convect = divergence(vel, in_c, x_halo, st, rims, (gu, gv, gq))
    px, pz, grad_x, convect = lax.optimization_barrier((px, pz, grad_x, convect))
    tx, bx = combine(tx, bx, px, below_of("gx", spot_x, 1))
    tz, bz = combine(tz, bz, pz, below_of("gz", spot_z, 1))
    rebuilt = rebuild(
        gu,
        gw,
        line_terms(tx, bx, spot_x[-1], total_x),
        line_terms(tz, bz, spot_z[-1], total_z),
        sums,
        total_x,
        total_z,
    )
    return (grad_x, grad_z, convect, rebuilt)


def solution(mesh):
    spec = P(None, "gx", None, "gz")
    return jax.shard_map(
        body, mesh=mesh, in_specs=(spec,), out_specs=(spec,) * 4, check_vma=False
    )
```

time: 43.1 us -> 41.1 us (0.954)
  the two profiles are of different devices: /device:TPU:0 before, /device:TPU:10 now
where the time goes in v3:
time: 41.1 us; the launch traced here: 41 us
  starting transfers between devices  20.9 us (51%)
  Pallas kernels  16.7 us (41%)
  waiting for transfers between devices  2.57 us (6%)
  between operations  0.85 us (2%)
    ppermute x10, starting transfers between devices, exchange(): parts[k] = lax.ppermute(terms, axis, pairs)  15 us
    pallas_call x1, Pallas kernels, divergence(): pl.pallas_call(body, in_specs=[VMEM] * 11, out_specs=[ANY, ANY], out_shap...  4.14 us
    ppermute x2, starting transfers between devices, swap(): after = lax.ppermute(down, axis, [((i + 1) % n, i) for i in range(n)])  3.95 us
    pallas_call x1, Pallas kernels, inner_z(): pl.pallas_call(body, in_specs=[VMEM, VMEM], out_specs=[VMEM] * 6, out_sha...  3.24 us
    pallas_call x1, Pallas kernels, edges_call(): pl.pallas_call(body, in_specs=[HBM], out_specs=[VMEM] * 5, out_shape=[xs,...  3.13 us
    ppermute x10, waiting for transfers between devices, exchange(): parts[k] = lax.ppermute(terms, axis, pairs)  2.56 us
    pallas_call x1, Pallas kernels, slopes_first(): pl.pallas_call(body, in_specs=[VMEM] * (2 + len(small)), out_specs=[VMEM]...  2.24 us
    pallas_call x1, Pallas kernels, rebuild(): pl.pallas_call(body, in_specs=[VMEM] * 5, out_specs=ANY, out_shape=jax.Sh...  2.2 us
  transfers between devices with their start and end apart: 14, of which 1 were waited for; matrix products, arithmetic and copies ran while one was open for 0% of the time, Pallas kernels for 22%

profile of v3, /device:TPU:10, one launch (start us, length us, event | category | flops | bytes accessed | tf_op | source)
XLA Modules:
  0.0 41.0 jit_solution(11354183895080067292)
XLA Ops:
  0.6 0.0 copy-start.2
  0.6 0.0 copy-start
  0.7 3.1 %edges.1 = (f32[9,8,128]{2,1,0:T(8,128)S(1)}, f32[9,8,128]{2,1,0:T(8,128)S(1)}, f32[9,16,128]{2,1,0:T(8,128)S(1)}, f32[9,16,128]{2,1,0:T(8,128)S(1)}, f32[3,256,8,128]{3,2,1,0:T(8,128)S(1)}) custom-call(f32[3,256,8,128]{3,2,1,0:T(8,128)} %v_hbm.1), custom_call_target="tpu_custom_call" | custom-call | flops 805306368 | bytes 12582912 | tf_op jit(solution)/shard_map/edges/pallas_call | solution.py:220
  3.8 0.0 collective-permute-start
  3.8 1.7 %collective-permute-start.1 = (f32[9,8,128]{2,1,0:T(8,128)S(1)}, f32[9,8,128]{2,1,0:T(8,128)S(1)}, u32[]{:S(2)}, u32[]{:S(2)}) collective-permute-start(f32[9,8,128]{2,1,0:T(8,128)S(1)} %get-tuple-element.45), channel_id=1, source_target_pairs={{16,0},{32,16},{48,32},{64,48},{80,64},{96,80},{112,96},{0,112},{1... | collective-permute-start | bytes 110600 | tf_op jit(solution)/shard_map/ppermute | solution.py:594
  5.6 1.9 %collective-permute-start.2 = (f32[9,16,128]{2,1,0:T(8,128)S(1)}, f32[9,16,128]{2,1,0:T(8,128)S(1)}, u32[]{:S(2)}, u32[]{:S(2)}) collective-permute-start(f32[9,16,128]{2,1,0:T(8,128)S(1)} %get-tuple-element.46.own_r), channel_id=1, source_target_pairs={{0,1},{1,2},{2,3},{3,4},{4,5},{5,6},{6,7},{7,8},{8,9},{9,10},{10,1... | collective-permute-start | bytes 221192 | tf_op jit(solution)/shard_map/ppermute | solution.py:593
  7.5 2.2 %collective-permute-start.3 = (f32[9,16,128]{2,1,0:T(8,128)S(1)}, f32[9,16,128]{2,1,0:T(8,128)S(1)}, u32[]{:S(2)}, u32[]{:S(2)}) collective-permute-start(f32[9,16,128]{2,1,0:T(8,128)S(1)} %get-tuple-element.47.own_l), channel_id=1, source_target_pairs={{1,0},{2,1},{3,2},{4,3},{5,4},{6,5},{7,6},{8,7},{9,8},{10,9},{11,1... | collective-permute-start | bytes 221192 | tf_op jit(solution)/shard_map/ppermute | solution.py:594
  9.7 3.2 %inner_z.1 = (f32[256,8,128]{2,1,0:T(8,128)S(1)}, f32[256,8,128]{2,1,0:T(8,128)S(1)}, f32[256,8,128]{2,1,0:T(8,128)S(1)}, f32[256,8,128]{2,1,0:T(8,128)S(1)}, f3...) custom-call(f32[3,256,8,128]{3,2,1,0:T(8,128)S(1)} %get-tuple-element.42.v_ref, bf16[2,128,128]{2,1,0:T(8,128)(2,1)S(1)} %copy-done.2), custom_call_target="tpu_custom_call" | custom-call | flops 805306368 | bytes 12582912 | tf_op jit(solution)/shard_map/inner_z/pallas_call | solution.py:338
  12.9 0.0 collective-permute-done.xl
  13.0 0.0 collective-permute-done.1.xr
  13.0 0.0 collective-permute-done.2.zl
  13.0 0.0 collective-permute-done.3.zr
  13.0 2.2 %slopes_first.1 = (f32[256,8,128]{2,1,0:T(8,128)S(1)}, f32[256,8,128]{2,1,0:T(8,128)S(1)}, f32[2,8,128]{2,1,0:T(8,128)S(1)}, f32[2,16,128]{2,1,0:T(8,128)S(1)}, ...) custom-call(f32[3,256,8,128]{3,2,1,0:T(8,128)S(1)} %get-tuple-element.42.v_ref, ...), custom_call_target="tpu_custom_call" | custom-call | flops 268435456 | bytes 4194304 | tf_op jit(solution)/shard_map/slopes_first/pallas_call | solution.py:426
  15.2 3.3 %collective-permute-start.7 = (f32[2,16,128]{2,1,0:T(8,128)S(1)}, f32[2,16,128]{2,1,0:T(8,128)S(1)}, u32[]{:S(2)}, u32[]{:S(2)}) collective-permute-start(f32[2,16,128]{2,1,0:T(8,128)S(1)} %get-tuple-element.49), channel_id=1, source_target_pairs={{0,3},{1,0},{2,1},{3,2},{4,7},{5,4},{6,5},{7,6},{8,11},{9,8},{10,9... | collective-permute-start | bytes 49160 | tf_op jit(solution)/shard_map/ppermute | solution.py:610
  18.6 0.0 collective-permute-start.6
  18.6 0.9 %collective-permute-start.5 = (f32[2,16,128]{2,1,0:T(8,128)S(1)}, f32[2,16,128]{2,1,0:T(8,128)S(1)}, u32[]{:S(2)}, u32[]{:S(2)}) collective-permute-start(f32[2,16,128]{2,1,0:T(8,128)S(1)} %get-tuple-element.49), channel_id=1, source_target_pairs={{0,1},{1,2},{2,3},{3,0},{4,5},{5,6},{6,7},{7,4},{8,9},{9,10},{10,1... | collective-permute-start | bytes 49160 | tf_op jit(solution)/shard_map/ppermute | solution.py:610
  19.5 0.0 collective-permute-start.4
  19.5 1.7 %slopes_rest.1 = (f32[256,8,128]{2,1,0:T(8,128)S(1)}, f32[256,8,128]{2,1,0:T(8,128)S(1)}, f32[3,256,8,128]{3,2,1,0:T(8,128)}) custom-call(f32[3,256,8,128]{3,2,1,0:T(8,128)S(1)} %get-tuple-element.42.v_ref, f32[256,8,128]{2,1,0:T(8,128)S(1)} %get-tuple-element.50.iu_ref, f32[256,8,128]{2,1,0:T(8,128)S(1)} %get-tuple-element.51.iv_ref, ...), custom_call_target="tpu_custom_call" | custom-call | flops 402653184 | bytes 6291456 | tf_op jit(solution)/shard_map/slopes_rest/pallas_call | solution.py:467
  21.3 0.0 collective-permute-done.4
  21.3 0.0 collective-permute-done.7
  21.3 2.5 %collective-permute-done.6 = f32[2,16,128]{2,1,0:T(8,128)S(1)} collective-permute-done((f32[2,16,128]{2,1,0:T(8,128)S(1)}, f32[2,16,128]{2,1,0:T(8,128)S(1)}, u32[]{:S(2)}, u32[]{:S(2)}) %collective-permute-start.6) | collective-permute-done | bytes 16416 | tf_op jit(solution)/shard_map/ppermute | solution.py:610
  23.8 1.7 %collective-permute-start.10 = (f32[2,8,128]{2,1,0:T(8,128)S(1)}, f32[2,8,128]{2,1,0:T(8,128)S(1)}, u32[]{:S(2)}, u32[]{:S(2)}) collective-permute-start(f32[2,8,128]{2,1,0:T(8,128)S(1)} %add.70), channel_id=1, source_target_pairs={{0,96},{16,112},{32,0},{48,16},{64,32},{80,48},{96,64},{112,80},{1... | collective-permute-start | bytes 24584 | tf_op jit(solution)/shard_map/ppermute | solution.py:610
  25.6 1.2 %collective-permute-start.9 = (f32[2,8,128]{2,1,0:T(8,128)S(1)}, f32[2,8,128]{2,1,0:T(8,128)S(1)}, u32[]{:S(2)}, u32[]{:S(2)}) collective-permute-start(f32[2,8,128]{2,1,0:T(8,128)S(1)} %add.70), channel_id=1, source_target_pairs={{0,64},{16,80},{32,96},{48,112},{64,0},{80,16},{96,32},{112,48},{1... | collective-permute-start | bytes 24584 | tf_op jit(solution)/shard_map/ppermute | solution.py:610
  26.8 1.8 %collective-permute-start.8 = (f32[2,8,128]{2,1,0:T(8,128)S(1)}, f32[2,8,128]{2,1,0:T(8,128)S(1)}, u32[]{:S(2)}, u32[]{:S(2)}) collective-permute-start(f32[2,8,128]{2,1,0:T(8,128)S(1)} %add.70), channel_id=1, source_target_pairs={{0,32},{16,48},{32,64},{48,80},{64,96},{80,112},{96,0},{112,16},{1... | collective-permute-start | bytes 24584 | tf_op jit(solution)/shard_map/ppermute | solution.py:610
  28.6 0.7 %collective-permute-start.13 = (f32[2,16,128]{2,1,0:T(8,128)S(1)}, f32[2,16,128]{2,1,0:T(8,128)S(1)}, u32[]{:S(2)}, u32[]{:S(2)}) collective-permute-start(f32[2,16,128]{2,1,0:T(8,128)S(1)} %add_add_fusion.1), channel_id=1, source_target_pairs={{0,12},{1,13},{2,14},{3,15},{4,0},{5,1},{6,2},{7,3},{8,4},{9,5},{1... | collective-permute-start | bytes 49160 | tf_op jit(solution)/shard_map/ppermute | solution.py:610
  29.3 2.7 %collective-permute-start.12 = (f32[2,16,128]{2,1,0:T(8,128)S(1)}, f32[2,16,128]{2,1,0:T(8,128)S(1)}, u32[]{:S(2)}, u32[]{:S(2)}) collective-permute-start(f32[2,16,128]{2,1,0:T(8,128)S(1)} %add_add_fusion.1), channel_id=1, source_target_pairs={{0,8},{1,9},{2,10},{3,11},{4,12},{5,13},{6,14},{7,15},{8,0},{9,1},... | collective-permute-start | bytes 49160 | tf_op jit(solution)/shard_map/ppermute | solution.py:610
  32.0 2.5 %collective-permute-start.11 = (f32[2,16,128]{2,1,0:T(8,128)S(1)}, f32[2,16,128]{2,1,0:T(8,128)S(1)}, u32[]{:S(2)}, u32[]{:S(2)}) collective-permute-start(f32[2,16,128]{2,1,0:T(8,128)S(1)} %add_add_fusion.1), channel_id=1, source_target_pairs={{0,4},{1,5},{2,6},{3,7},{4,8},{5,9},{6,10},{7,11},{8,12},{9,13},{1... | collective-permute-start | bytes 49160 | tf_op jit(solution)/shard_map/ppermute | solution.py:610
  34.5 4.1 %divergence.1 = (f32[3,256,8,128]{3,2,1,0:T(8,128)}, f32[3,256,8,128]{3,2,1,0:T(8,128)}) custom-call(f32[3,256,8,128]{3,2,1,0:T(8,128)S(1)} %get-tuple-element.42.v_ref, f32[9,8,128]{2,1,0:T(8,128)S(1)} %collective-permute-done.xl, f32[9,8,128]{2,1,0:T(8,128)S(1)} %collective-permute-done.1.xr, bf16[2048,128]{1,0:T(8,128)(2,1)S(1)} %get-tuple-element.52.st_ref, ...), custom_call_target="tpu_custom_call" | custom-call | flops 805306368 | bytes 12582912 | tf_op jit(solution)/shard_map/divergence/pallas_call | solution.py:520
  38.7 0.0 collective-permute-done.9
  38.7 0.0 collective-permute-done.13
  38.7 0.0 collective-permute-done.12
  38.8 2.2 %rebuild.1 = f32[2,256,8,128]{3,2,1,0:T(8,128)} custom-call(f32[256,8,128]{2,1,0:T(8,128)S(1)} %get-tuple-element.64.rest_3_.u_ref, f32[256,8,128]{2,1,0:T(8,128)S(1)} %get-tuple-element.53.gw_ref.w_ref, f32[2,8,128]{2,1,0:T(8,128)S(1)} %pad_maximum_fusion.1.xt, f32[2,16,128]{2,1,0:T(8,128)S(1)} %pad_maximum_fusion.zt, bf16[2,256,128]{2,1,0:T(8,128)(2,1)S(1)} %copy-done.1), custom_call_target="tpu_custom_call" | custom-call | flops 268435456 | bytes 4194304 | tf_op jit(solution)/shard_map/rebuild/pallas_call | solution.py:575
  (16 shorter events, 0.1 us)
Async XLA Ops:
  0.6 9.1 %copy-start.2 = (bf16[2,128,128]{2,1,0:T(8,128)(2,1)S(1)}, bf16[2,128,128]{2,1,0:T(8,128)(2,1)}, u32[]{:S(2)}) copy-start(bf16[2,128,128]{2,1,0:T(8,128)(2,1)} %constant.13.clone.m_ref) | copy-start | bytes 196612
  0.6 12.3 %copy-start = (bf16[6,128,128]{2,1,0:T(8,128)(2,1)S(1)}, bf16[6,128,128]{2,1,0:T(8,128)(2,1)}, u32[]{:S(2)}) copy-start(bf16[6,128,128]{2,1,0:T(8,128)(2,1)} %constant.14.clone.m_ref) | copy-start | bytes 589828
  3.8 9.1 %collective-permute-start = (f32[9,8,128]{2,1,0:T(8,128)S(1)}, f32[9,8,128]{2,1,0:T(8,128)S(1)}, u32[]{:S(2)}, u32[]{:S(2)}) collective-permute-start(f32[9,8,128]{2,1,0:T(8,128)S(1)} %get-tuple-element.44), channel_id=1, source_target_pairs={{0,16},{16,32},{32,48},{48,64},{64,80},{80,96},{96,112},{112,0},{1... | collective-permute-start | bytes 110600 | tf_op jit(solution)/shard_map/ppermute | solution.py:593
  3.8 9.1 %collective-permute-start.1 = (f32[9,8,128]{2,1,0:T(8,128)S(1)}, f32[9,8,128]{2,1,0:T(8,128)S(1)}, u32[]{:S(2)}, u32[]{:S(2)}) collective-permute-start(f32[9,8,128]{2,1,0:T(8,128)S(1)} %get-tuple-element.45), channel_id=1, source_target_pairs={{16,0},{32,16},{48,32},{64,48},{80,64},{96,80},{112,96},{0,112},{1... | collective-permute-start | bytes 110600 | tf_op jit(solution)/shard_map/ppermute | solution.py:594
  5.6 7.4 %collective-permute-start.2 = (f32[9,16,128]{2,1,0:T(8,128)S(1)}, f32[9,16,128]{2,1,0:T(8,128)S(1)}, u32[]{:S(2)}, u32[]{:S(2)}) collective-permute-start(f32[9,16,128]{2,1,0:T(8,128)S(1)} %get-tuple-element.46.own_r), channel_id=1, source_target_pairs={{0,1},{1,2},{2,3},{3,4},{4,5},{5,6},{6,7},{7,8},{8,9},{9,10},{10,1... | collective-permute-start | bytes 221192 | tf_op jit(solution)/shard_map/ppermute | solution.py:593
  7.5 5.5 %collective-permute-start.3 = (f32[9,16,128]{2,1,0:T(8,128)S(1)}, f32[9,16,128]{2,1,0:T(8,128)S(1)}, u32[]{:S(2)}, u32[]{:S(2)}) collective-permute-start(f32[9,16,128]{2,1,0:T(8,128)S(1)} %get-tuple-element.47.own_l), channel_id=1, source_target_pairs={{1,0},{2,1},{3,2},{4,3},{5,4},{6,5},{7,6},{8,7},{9,8},{10,9},{11,1... | collective-permute-start | bytes 221192 | tf_op jit(solution)/shard_map/ppermute | solution.py:594
  15.2 6.0 %collective-permute-start.7 = (f32[2,16,128]{2,1,0:T(8,128)S(1)}, f32[2,16,128]{2,1,0:T(8,128)S(1)}, u32[]{:S(2)}, u32[]{:S(2)}) collective-permute-start(f32[2,16,128]{2,1,0:T(8,128)S(1)} %get-tuple-element.49), channel_id=1, source_target_pairs={{0,3},{1,0},{2,1},{3,2},{4,7},{5,4},{6,5},{7,6},{8,11},{9,8},{10,9... | collective-permute-start | bytes 49160 | tf_op jit(solution)/shard_map/ppermute | solution.py:610
  18.6 5.2 %collective-permute-start.6 = (f32[2,16,128]{2,1,0:T(8,128)S(1)}, f32[2,16,128]{2,1,0:T(8,128)S(1)}, u32[]{:S(2)}, u32[]{:S(2)}) collective-permute-start(f32[2,16,128]{2,1,0:T(8,128)S(1)} %get-tuple-element.49), channel_id=1, source_target_pairs={{0,2},{1,3},{2,0},{3,1},{4,6},{5,7},{6,4},{7,5},{8,10},{9,11},{10,... | collective-permute-start | bytes 49160 | tf_op jit(solution)/shard_map/ppermute | solution.py:610
  18.6 5.2 %collective-permute-start.5 = (f32[2,16,128]{2,1,0:T(8,128)S(1)}, f32[2,16,128]{2,1,0:T(8,128)S(1)}, u32[]{:S(2)}, u32[]{:S(2)}) collective-permute-start(f32[2,16,128]{2,1,0:T(8,128)S(1)} %get-tuple-element.49), channel_id=1, source_target_pairs={{0,1},{1,2},{2,3},{3,0},{4,5},{5,6},{6,7},{7,4},{8,9},{9,10},{10,1... | collective-permute-start | bytes 49160 | tf_op jit(solution)/shard_map/ppermute | solution.py:610
  19.5 1.7 %collective-permute-start.4 = (f32[2,8,128]{2,1,0:T(8,128)S(1)}, f32[2,8,128]{2,1,0:T(8,128)S(1)}, u32[]{:S(2)}, u32[]{:S(2)}) collective-permute-start(f32[2,8,128]{2,1,0:T(8,128)S(1)} %get-tuple-element.48), channel_id=1, source_target_pairs={{0,16},{16,0},{32,48},{48,32},{64,80},{80,64},{96,112},{112,96},{1... | collective-permute-start | bytes 24584 | tf_op jit(solution)/shard_map/ppermute | solution.py:610
  23.8 8.1 %collective-permute-start.10 = (f32[2,8,128]{2,1,0:T(8,128)S(1)}, f32[2,8,128]{2,1,0:T(8,128)S(1)}, u32[]{:S(2)}, u32[]{:S(2)}) collective-permute-start(f32[2,8,128]{2,1,0:T(8,128)S(1)} %add.70), channel_id=1, source_target_pairs={{0,96},{16,112},{32,0},{48,16},{64,32},{80,48},{96,64},{112,80},{1... | collective-permute-start | bytes 24584 | tf_op jit(solution)/shard_map/ppermute | solution.py:610
  25.6 13.1 %collective-permute-start.9 = (f32[2,8,128]{2,1,0:T(8,128)S(1)}, f32[2,8,128]{2,1,0:T(8,128)S(1)}, u32[]{:S(2)}, u32[]{:S(2)}) collective-permute-start(f32[2,8,128]{2,1,0:T(8,128)S(1)} %add.70), channel_id=1, source_target_pairs={{0,64},{16,80},{32,96},{48,112},{64,0},{80,16},{96,32},{112,48},{1... | collective-permute-start | bytes 24584 | tf_op jit(solution)/shard_map/ppermute | solution.py:610
  26.8 11.9 %collective-permute-start.8 = (f32[2,8,128]{2,1,0:T(8,128)S(1)}, f32[2,8,128]{2,1,0:T(8,128)S(1)}, u32[]{:S(2)}, u32[]{:S(2)}) collective-permute-start(f32[2,8,128]{2,1,0:T(8,128)S(1)} %add.70), channel_id=1, source_target_pairs={{0,32},{16,48},{32,64},{48,80},{64,96},{80,112},{96,0},{112,16},{1... | collective-permute-start | bytes 24584 | tf_op jit(solution)/shard_map/ppermute | solution.py:610
  28.6 10.1 %collective-permute-start.13 = (f32[2,16,128]{2,1,0:T(8,128)S(1)}, f32[2,16,128]{2,1,0:T(8,128)S(1)}, u32[]{:S(2)}, u32[]{:S(2)}) collective-permute-start(f32[2,16,128]{2,1,0:T(8,128)S(1)} %add_add_fusion.1), channel_id=1, source_target_pairs={{0,12},{1,13},{2,14},{3,15},{4,0},{5,1},{6,2},{7,3},{8,4},{9,5},{1... | collective-permute-start | bytes 49160 | tf_op jit(solution)/shard_map/ppermute | solution.py:610
  29.3 9.4 %collective-permute-start.12 = (f32[2,16,128]{2,1,0:T(8,128)S(1)}, f32[2,16,128]{2,1,0:T(8,128)S(1)}, u32[]{:S(2)}, u32[]{:S(2)}) collective-permute-start(f32[2,16,128]{2,1,0:T(8,128)S(1)} %add_add_fusion.1), channel_id=1, source_target_pairs={{0,8},{1,9},{2,10},{3,11},{4,12},{5,13},{6,14},{7,15},{8,0},{9,1},... | collective-permute-start | bytes 49160 | tf_op jit(solution)/shard_map/ppermute | solution.py:610
  32.0 6.7 %collective-permute-start.11 = (f32[2,16,128]{2,1,0:T(8,128)S(1)}, f32[2,16,128]{2,1,0:T(8,128)S(1)}, u32[]{:S(2)}, u32[]{:S(2)}) collective-permute-start(f32[2,16,128]{2,1,0:T(8,128)S(1)} %add_add_fusion.1), channel_id=1, source_target_pairs={{0,4},{1,5},{2,6},{3,7},{4,8},{5,9},{6,10},{7,11},{8,12},{9,13},{1... | collective-permute-start | bytes 49160 | tf_op jit(solution)/shard_map/ppermute | solution.py:610
  34.5 4.3 %copy-start.1 = (bf16[2,256,128]{2,1,0:T(8,128)(2,1)S(1)}, bf16[2,256,128]{2,1,0:T(8,128)(2,1)}, u32[]{:S(2)}) copy-start(bf16[2,256,128]{2,1,0:T(8,128)(2,1)} %constant.15.clone.m_ref) | copy-start | bytes 393220

commit v4 on v3

--- a/solution.py
+++ b/solution.py
@@ -418,8 +418,8 @@
     sz = jax.ShapeDtypeStruct((2, chunks, LANES), F32)
     st = jax.ShapeDtypeStruct((rows, LANES), BF16)
     small = [*x_halo, *z_halo, rims]
-    steps_x = sum(count - 1 for count, _ in LEVELS["gx"])
-    steps_z = sum(count - 1 for count, _ in LEVELS["gz"])
+    steps_x = sum(len(below_tests(level)) for level in LEVELS["gx"])
+    steps_z = sum(len(below_tests(level)) for level in LEVELS["gz"])
     px = jax.ShapeDtypeStruct((steps_x + 1, ny, nz), F32)
     pz = jax.ShapeDtypeStruct((steps_z + 1, chunks, LANES), F32)
     outs = [one, one, sx, sz, st, px, pz]
@@ -481,24 +481,50 @@
     )(velocity, inner_u, inner_v, *x_halo, st, rims, gw)
 
 
-def divergence(velocity, inner, x_halo, st, rims, slopes):
+def prepare(inner, st, rims, slopes, sums):
+    nx, ny, nz = slopes[0].shape
+    rows = nx * ny
+
+    def body(*refs):
+        i_refs, g_refs, st_ref, m_ref, t_ref = refs[:3], refs[3:6], *refs[6:9]
+        *c_refs, local, gx, sems = refs[9:]
+        box = Outbox(sems)
+        for c in range(3):
+            box.send(g_refs[c], gx.at[c])
+        hi, mid, lo = split3(g_refs[0][...].reshape(rows, nz))
+        g = dot(jnp.concatenate([hi, mid], 1), t_ref[0]) + dot(lo, t_ref[1, :LANES])
+        local[...] = g.reshape(nx, ny, nz)
+        for c in range(3):
+            g = i_refs[c][...].reshape(rows, nz) + dot(st_ref[...], m_ref[3 + c])
+            c_refs[c][...] = g.reshape(nx, ny, nz)
+        box.wait()
+
+    one = jax.ShapeDtypeStruct((nx, ny, nz), F32)
+    *parts, local, gx = pl.pallas_call(
+        body,
+        in_specs=[VMEM] * 9,
+        out_specs=[VMEM] * 4 + [ANY],
+        out_shape=[one] * 4 + [jax.ShapeDtypeStruct((3, nx, ny, nz), F32)],
+        scratch_shapes=[pltpu.SemaphoreType.DMA((4,))],
+        compiler_params=params(),
+        name="prepare",
+        cost_estimate=cost(3, nx * ny * nz),
+    )(*inner, *slopes, st, rims, sums)
+    return parts, local, gx
+
+
+def divergence(velocity, along_z, x_halo):
     _, nx, ny, nz = velocity.shape
-    rows = nx * ny
     comps = range(3)
 
-    def body(v_ref, xl, xr, st_ref, m_ref, *rest):
-        i_refs, g_refs = rest[:3], rest[3:6]
-        gx, out, s0, s1, s2, m0, m1, m2, sems = rest[6:]
+    def body(v_ref, xl, xr, *rest):
+        z_refs = rest[:3]
+        out, s0, s1, s2, m0, m1, m2, sems = rest[3:]
         made = (m0, m1, m2)
         box = Outbox(sems)
-        for c in comps:
-            box.send(g_refs[c], gx.at[c])
-        for c in comps:
-            g = i_refs[c][...].reshape(rows, nz) + dot(st_ref[...], m_ref[3 + c])
-            made[c][...] = g.reshape(nx, ny, nz)
 
         def write(c, i, g):
-            made[c][i] = made[c][i] + g
+            made[c][i] = z_refs[c][i] + g
 
         def done(start, size):
             at = pl.ds(start, size)
@@ -516,21 +542,20 @@
         )
         box.wait()
 
-    full = jax.ShapeDtypeStruct(velocity.shape, F32)
     return pl.pallas_call(
         body,
-        in_specs=[VMEM] * 11,
-        out_specs=[ANY, ANY],
-        out_shape=[full, full],
+        in_specs=[VMEM] * 6,
+        out_specs=ANY,
+        out_shape=jax.ShapeDtypeStruct(velocity.shape, F32),
         scratch_shapes=[pltpu.VMEM((nx, ny, nz), F32)] * 6 + [pltpu.SemaphoreType.DMA((32,))],
         compiler_params=params(12),
         name="divergence",
         cost_estimate=cost(6, nx * ny * nz),
-    )(velocity, *x_halo, st, rims, *inner, *slopes)
-
-
-def rebuild(gu, gw, x_terms, z_terms, mats, total_x, total_z):
-    nx, ny, nz = gu.shape
+    )(velocity, *x_halo, *along_z)
+
+
+def rebuild(local, gw, x_terms, z_terms, mats, total_x, total_z):
+    nx, ny, nz = gw.shape
     sub = LANES // ny
     chunks = nx // sub
     rows = nx * ny
@@ -538,7 +563,7 @@
     scale_x = -1.0 / math.sqrt(total_x)
     scale_z = -1.0 / math.sqrt(total_z)
 
-    def body(u_ref, w_ref, xt, zt, m_ref, out, rim, made, sems):
+    def body(l_ref, w_ref, xt, zt, m_ref, out, rim, made, sems):
         box = Outbox(sems)
         mean = xt[1]
 
@@ -561,17 +586,14 @@
                 rim[:, 3 * q + p, :] = part.astype(F32)
         for p in range(parts):
             at = pl.ds(p * nx // parts, nx // parts)
-            hi, mid, lo = split3(u_ref[at].reshape(rows // parts, nz))
             here = range(p * chunks // parts, (p + 1) * chunks // parts)
             st = jnp.concatenate([rim[c].T.astype(BF16) for c in here], 0)
-            g = dot(jnp.concatenate([hi, mid], 1), m_ref[0]) + dot(
-                jnp.concatenate([lo, st], 1), m_ref[1]
-            )
+            g = l_ref[at].reshape(rows // parts, nz) + dot(st, m_ref[1, LANES:])
             made[1, at] = (scale_z * g).reshape(nx // parts, ny, nz)
             box.send(made.at[1, at], out.at[1, at])
         box.wait()
 
-    shape = (2,) + gu.shape
+    shape = (2,) + gw.shape
     return pl.pallas_call(
         body,
         in_specs=[VMEM] * 5,
@@ -585,7 +607,7 @@
         compiler_params=params(),
         name="rebuild",
         cost_estimate=cost(2, nx * ny * nz),
-    )(gu, gw, x_terms, z_terms, mats)
+    )(local, gw, x_terms, z_terms, mats)
 
 
 def swap(axis, up, down):
@@ -595,25 +617,41 @@
     return before, after
 
 
-LEVELS = {"gx": [(2, 1), (4, 2)], "gz": [(4, 1), (4, 4)]}
+LEVELS = {
+    "gx": [(2, 1, False), (2, 2, False), (4, 2, True)],
+    "gz": [(4, 1, False), (2, 4, False), (4, 4, True)],
+}
+ROUNDS = [(("gx", "gz"), "rest"), (("gx", "gz"), "prepare"), (("gx", "gz"), "flux")]
+
+
+def shifts(level):
+    count, _, mirror = level
+    if mirror:
+        return [lambda own: count - 1 - 2 * own]
+    order = sorted(range(1, count), key=lambda k: min(k, count - k))
+    return [lambda own, k=k: (own + k) % count - own for k in order]
+
+
+def below_tests(level):
+    count, _, mirror = level
+    if mirror:
+        return [count // 2]
+    return sorted(range(1, count), key=lambda k: min(k, count - k))
 
 
 def exchange(axis, terms, level):
     n = lax.axis_size(axis)
-    count, stride = level
-    parts = {}
-    for k in sorted(range(1, count), key=lambda k: min(k, count - k)):
-        pairs = []
-        for i in range(n):
-            own = (i // stride) % count
-            pairs.append((i, i + ((own + k) % count - own) * stride))
-        parts[k] = lax.ppermute(terms, axis, pairs)
+    count, stride, _ = level
+    parts = []
+    for shift in shifts(level):
+        pairs = [(i, i + shift((i // stride) % count) * stride) for i in range(n)]
+        parts.append(lax.ppermute(terms, axis, pairs))
     return parts
 
 
-def combine(terms, before, parts, lower):
-    for k, part in parts.items():
-        before = before + lower[k] * part[0]
+def combine(terms, before, parts, below):
+    for mask, part in zip(below, parts):
+        before = before + mask * part[0]
         terms = terms + part
     return terms, before
 
@@ -622,19 +660,17 @@
     n = lax.axis_size(axis)
     mine = lax.axis_index(axis)
     below = []
-    for count, stride in LEVELS[axis]:
-        own = mine // stride % count
-        for k in range(1, count):
-            below.append((own >= k).astype(F32))
+    for level in LEVELS[axis]:
+        own = mine // level[1] % level[0]
+        below += [(own >= least).astype(F32) for least in below_tests(level)]
     start = (mine * cells).astype(F32)
     centre = start + (0.5 * (cells - 1) - 0.5 * (n * cells - 1))
     return below, centre, (start + 0.5) * (1.0 / (n * cells))
 
 
 def below_of(axis, spot, at):
-    skip = sum(count - 1 for count, _ in LEVELS[axis][:at])
-    count = LEVELS[axis][at][0]
-    return {k: spot[skip + k - 1] for k in range(1, count)}
+    skip = sum(len(below_tests(level)) for level in LEVELS[axis][:at])
+    return [spot[skip + k] for k in range(len(below_tests(LEVELS[axis][at])))]
 
 
 def line_terms(terms, before, start, total_len):
@@ -661,20 +697,33 @@
     bx = jnp.zeros_like(tx[0])
     bz = jnp.zeros_like(tz[0])
 
-    px = exchange("gx", tx, LEVELS["gx"][0])
-    pz = exchange("gz", tz, LEVELS["gz"][0])
-    gv, gq, grad_z = slopes_rest(vel, in_u, in_v, x_halo, st, rims, gw)
-    px, pz, gv, gq, grad_z = lax.optimization_barrier((px, pz, gv, gq, grad_z))
-    tx, bx = combine(tx, bx, px, below_of("gx", spot_x, 0))
-    tz, bz = combine(tz, bz, pz, below_of("gz", spot_z, 0))
-    px = exchange("gx", tx, LEVELS["gx"][1])
-    pz = exchange("gz", tz, LEVELS["gz"][1])
-    grad_x, convect = divergence(vel, in_c, x_halo, st, rims, (gu, gv, gq))
-    px, pz, grad_x, convect = lax.optimization_barrier((px, pz, grad_x, convect))
-    tx, bx = combine(tx, bx, px, below_of("gx", spot_x, 1))
-    tz, bz = combine(tz, bz, pz, below_of("gz", spot_z, 1))
+    terms = {"gx": (tx, bx), "gz": (tz, bz)}
+    spots = {"gx": spot_x, "gz": spot_z}
+    done = {"gx": 0, "gz": 0}
+    for axes, filler in ROUNDS:
+        parts = {axis: exchange(axis, terms[axis][0], LEVELS[axis][done[axis]]) for axis in axes}
+        made = ()
+        if filler == "rest":
+            made = slopes_rest(vel, in_u, in_v, x_halo, st, rims, gw)
+        elif filler == "flux":
+            made = divergence(vel, in_c, x_halo)
+        elif filler == "prepare":
+            made = prepare(in_c, st, rims, (gu, gv, gq), sums)
+        if filler:
+            parts, made = lax.optimization_barrier((parts, made))
+        if filler == "rest":
+            gv, gq, grad_z = made
+        elif filler == "prepare":
+            in_c, local, grad_x = made
+        elif filler == "flux":
+            convect = made
+        for axis in axes:
+            below = below_of(axis, spots[axis], done[axis])
+            terms[axis] = combine(*terms[axis], parts[axis], below)
+            done[axis] += 1
+    (tx, bx), (tz, bz) = terms["gx"], terms["gz"]
     rebuilt = rebuild(
-        gu,
+        local,
         gw,
         line_terms(tx, bx, spot_x[-1], total_x),
         line_terms(tz, bz, spot_z[-1], total_z),

time: 41.1 us -> 40 us (0.973)
  the two profiles are of different devices: /device:TPU:10 before, /device:TPU:0 now
where the time goes in v4:
time: 40 us; the launch traced here: 39.9 us
  Pallas kernels  17.3 us (43%)
  starting transfers between devices  16.8 us (42%)
  waiting for transfers between devices  4.92 us (12%)
  between operations  0.84 us (2%)
    ppermute x2, starting transfers between devices, swap(): after = lax.ppermute(down, axis, [((i + 1) % n, i) for i in range(n)])  7.52 us
    ppermute x8, starting transfers between devices, exchange(): parts.append(lax.ppermute(terms, axis, pairs))  7.26 us
    ppermute x8, waiting for transfers between devices, exchange(): parts.append(lax.ppermute(terms, axis, pairs))  4.91 us
    pallas_call x1, Pallas kernels, divergence(): pl.pallas_call(body, in_specs=[VMEM] * 6, out_specs=ANY, out_shape=jax.Sh...  3.19 us
    pallas_call x1, Pallas kernels, edges_call(): pl.pallas_call(body, in_specs=[HBM], out_specs=[VMEM] * 5, out_shape=[xs,...  3.13 us
    pallas_call x1, Pallas kernels, inner_z(): pl.pallas_call(body, in_specs=[VMEM, VMEM], out_specs=[VMEM] * 6, out_sha...  3.05 us
    pallas_call x1, Pallas kernels, slopes_first(): pl.pallas_call(body, in_specs=[VMEM] * (2 + len(small)), out_specs=[VMEM]...  2.24 us
    pallas_call x1, Pallas kernels, prepare(): pl.pallas_call(body, in_specs=[VMEM] * 9, out_specs=[VMEM] * 4 + [ANY], o...  2.04 us
  transfers between devices with their start and end apart: 12, of which 3 were waited for; matrix products, arithmetic and copies ran while one was open for 0% of the time, Pallas kernels for 25%

profile of v4, /device:TPU:0, one launch (start us, length us, event | category | flops | bytes accessed | tf_op | source)
XLA Modules:
  0.0 39.9 jit_solution(8974461374541820640)
XLA Ops:
  0.6 0.0 copy-start.2
  0.6 0.0 copy-start
  0.7 3.1 %edges.1 = (f32[9,8,128]{2,1,0:T(8,128)S(1)}, f32[9,8,128]{2,1,0:T(8,128)S(1)}, f32[9,16,128]{2,1,0:T(8,128)S(1)}, f32[9,16,128]{2,1,0:T(8,128)S(1)}, f32[3,256,8,128]{3,2,1,0:T(8,128)S(1)}) custom-call(f32[3,256,8,128]{3,2,1,0:T(8,128)} %v_hbm.1), custom_call_target="tpu_custom_call" | custom-call | flops 805306368 | bytes 12582912 | tf_op jit(solution)/shard_map/edges/pallas_call | solution.py:220
  3.8 0.0 collective-permute-start
  3.8 2.9 %collective-permute-start.1 = (f32[9,8,128]{2,1,0:T(8,128)S(1)}, f32[9,8,128]{2,1,0:T(8,128)S(1)}, u32[]{:S(2)}, u32[]{:S(2)}) collective-permute-start(f32[9,8,128]{2,1,0:T(8,128)S(1)} %get-tuple-element.50), channel_id=1, source_target_pairs={{16,0},{32,16},{48,32},{64,48},{80,64},{96,80},{112,96},{0,112},{1... | collective-permute-start | bytes 110600 | tf_op jit(solution)/shard_map/ppermute | solution.py:616
  6.8 2.0 %collective-permute-start.2 = (f32[9,16,128]{2,1,0:T(8,128)S(1)}, f32[9,16,128]{2,1,0:T(8,128)S(1)}, u32[]{:S(2)}, u32[]{:S(2)}) collective-permute-start(f32[9,16,128]{2,1,0:T(8,128)S(1)} %get-tuple-element.51.own_r), channel_id=1, source_target_pairs={{0,1},{1,2},{2,3},{3,4},{4,5},{5,6},{6,7},{7,8},{8,9},{9,10},{10,1... | collective-permute-start | bytes 221192 | tf_op jit(solution)/shard_map/ppermute | solution.py:615
  8.8 4.6 %collective-permute-start.3 = (f32[9,16,128]{2,1,0:T(8,128)S(1)}, f32[9,16,128]{2,1,0:T(8,128)S(1)}, u32[]{:S(2)}, u32[]{:S(2)}) collective-permute-start(f32[9,16,128]{2,1,0:T(8,128)S(1)} %get-tuple-element.52.own_l), channel_id=1, source_target_pairs={{1,0},{2,1},{3,2},{4,3},{5,4},{6,5},{7,6},{8,7},{9,8},{10,9},{11,1... | collective-permute-start | bytes 221192 | tf_op jit(solution)/shard_map/ppermute | solution.py:616
  13.3 3.1 %inner_z.1 = (f32[256,8,128]{2,1,0:T(8,128)S(1)}, f32[256,8,128]{2,1,0:T(8,128)S(1)}, f32[256,8,128]{2,1,0:T(8,128)S(1)}, f32[256,8,128]{2,1,0:T(8,128)S(1)}, f3...) custom-call(f32[3,256,8,128]{3,2,1,0:T(8,128)S(1)} %get-tuple-element.47.v_ref, bf16[2,128,128]{2,1,0:T(8,128)(2,1)S(1)} %copy-done.2), custom_call_target="tpu_custom_call" | custom-call | flops 805306368 | bytes 12582912 | tf_op jit(solution)/shard_map/inner_z/pallas_call | solution.py:338
  16.4 0.0 collective-permute-done.xl
  16.4 0.0 collective-permute-done.1.xr
  16.4 0.0 collective-permute-done.2.zl
  16.4 0.0 collective-permute-done.3.zr
  16.4 2.2 %slopes_first.1 = (f32[256,8,128]{2,1,0:T(8,128)S(1)}, f32[256,8,128]{2,1,0:T(8,128)S(1)}, f32[2,8,128]{2,1,0:T(8,128)S(1)}, f32[2,16,128]{2,1,0:T(8,128)S(1)}, ...) custom-call(f32[3,256,8,128]{3,2,1,0:T(8,128)S(1)} %get-tuple-element.47.v_ref, ...), custom_call_target="tpu_custom_call" | custom-call | flops 268435456 | bytes 4194304 | tf_op jit(solution)/shard_map/slopes_first/pallas_call | solution.py:426
  18.7 0.1 collective-permute-start.5
  18.8 3.2 %collective-permute-start.6 = (f32[2,16,128]{2,1,0:T(8,128)S(1)}, f32[2,16,128]{2,1,0:T(8,128)S(1)}, u32[]{:S(2)}, u32[]{:S(2)}) collective-permute-start(f32[2,16,128]{2,1,0:T(8,128)S(1)} %get-tuple-element.54), channel_id=1, source_target_pairs={{0,3},{1,0},{2,1},{3,2},{4,7},{5,4},{6,5},{7,6},{8,11},{9,8},{10,9... | collective-permute-start | bytes 49160 | tf_op jit(solution)/shard_map/ppermute | solution.py:648
  22.0 0.0 collective-permute-start.7
  22.0 0.0 collective-permute-start.4
  22.0 1.7 %slopes_rest.1 = (f32[256,8,128]{2,1,0:T(8,128)S(1)}, f32[256,8,128]{2,1,0:T(8,128)S(1)}, f32[3,256,8,128]{3,2,1,0:T(8,128)}) custom-call(f32[3,256,8,128]{3,2,1,0:T(8,128)S(1)} %get-tuple-element.47.v_ref, f32[256,8,128]{2,1,0:T(8,128)S(1)} %get-tuple-element.55.iu_ref, f32[256,8,128]{2,1,0:T(8,128)S(1)} %get-tuple-element.56.iv_ref, ...), custom_call_target="tpu_custom_call" | custom-call | flops 402653184 | bytes 6291456 | tf_op jit(solution)/shard_map/slopes_rest/pallas_call | solution.py:467
  23.8 0.0 collective-permute-done.5
  23.8 0.0 collective-permute-done.6
  23.8 3.5 %collective-permute-done.7 = f32[2,16,128]{2,1,0:T(8,128)S(1)} collective-permute-done((f32[2,16,128]{2,1,0:T(8,128)S(1)}, f32[2,16,128]{2,1,0:T(8,128)S(1)}, u32[]{:S(2)}, u32[]{:S(2)}) %collective-permute-start.7) | collective-permute-done | bytes 16416 | tf_op jit(solution)/shard_map/ppermute | solution.py:648
  27.2 0.0 collective-permute-start.9
  27.3 0.4 collective-permute-start.8
  27.6 2.0 %prepare.1 = (f32[256,8,128]{2,1,0:T(8,128)S(1)}, f32[256,8,128]{2,1,0:T(8,128)S(1)}, f32[256,8,128]{2,1,0:T(8,128)S(1)}, f32[256,8,128]{2,1,0:T(8,128)S(1)}, f32[3,256,8,128]{3,2,1,0:T(8,128)}) custom-call(f32[256,8,128]{2,1,0:T(8,128)S(1)} %get-tuple-element.66.refs_0_, f32[256,8,128]{2,1,0:T(8,128)S(1)} %get-tuple-element.67.refs_1_, ...), custom_call_target="tpu_custom_call" | custom-call | flops 402653184 | bytes 6291456 | tf_op jit(solution)/shard_map/prepare/pallas_call | solution.py:503
  29.7 1.3 %collective-permute-done.8 = f32[2,8,128]{2,1,0:T(8,128)S(1)} collective-permute-done((f32[2,8,128]{2,1,0:T(8,128)S(1)}, f32[2,8,128]{2,1,0:T(8,128)S(1)}, u32[]{:S(2)}, u32[]{:S(2)}) %collective-permute-start.8) | collective-permute-done | bytes 8224 | tf_op jit(solution)/shard_map/ppermute | solution.py:648
  31.0 0.0 collective-permute-done.9
  31.0 2.0 %collective-permute-start.11 = (f32[2,16,128]{2,1,0:T(8,128)S(1)}, f32[2,16,128]{2,1,0:T(8,128)S(1)}, u32[]{:S(2)}, u32[]{:S(2)}) collective-permute-start(f32[2,16,128]{2,1,0:T(8,128)S(1)} %add.61), channel_id=1, source_target_pairs={{0,12},{1,13},{2,14},{3,15},{4,8},{5,9},{6,10},{7,11},{8,4},{9,5},... | collective-permute-start | bytes 49160 | tf_op jit(solution)/shard_map/ppermute | solution.py:648
  33.1 1.5 %collective-permute-start.10 = (f32[2,8,128]{2,1,0:T(8,128)S(1)}, f32[2,8,128]{2,1,0:T(8,128)S(1)}, u32[]{:S(2)}, u32[]{:S(2)}) collective-permute-start(f32[2,8,128]{2,1,0:T(8,128)S(1)} %add.60), channel_id=1, source_target_pairs={{0,96},{16,112},{32,64},{48,80},{64,32},{80,48},{96,0},{112,16},{1... | collective-permute-start | bytes 24584 | tf_op jit(solution)/shard_map/ppermute | solution.py:648
  34.6 3.2 %divergence.1 = f32[3,256,8,128]{3,2,1,0:T(8,128)} custom-call(f32[3,256,8,128]{3,2,1,0:T(8,128)S(1)} %get-tuple-element.47.v_ref, f32[9,8,128]{2,1,0:T(8,128)S(1)} %collective-permute-done.xl, f32[9,8,128]{2,1,0:T(8,128)S(1)} %collective-permute-done.1.xr, f32[256,8,128]{2,1,0:T(8,128)S(1)} %get-tuple-element.81.rest_0_, ...), custom_call_target="tpu_custom_call" | custom-call | flops 805306368 | bytes 12582912 | tf_op jit(solution)/shard_map/divergence/pallas_call | solution.py:545
  37.8 0.1 collective-permute-done.10
  37.9 0.0 collective-permute-done.11
  38.0 1.9 %rebuild.1 = f32[2,256,8,128]{3,2,1,0:T(8,128)} custom-call(f32[256,8,128]{2,1,0:T(8,128)S(1)} %get-tuple-element.85.l_ref, f32[256,8,128]{2,1,0:T(8,128)S(1)} %get-tuple-element.58.gw_ref.w_ref, f32[2,8,128]{2,1,0:T(8,128)S(1)} %pad_maximum_fusion.1.xt, f32[2,16,128]{2,1,0:T(8,128)S(1)} %pad_maximum_fusion.zt, bf16[2,256,128]{2,1,0:T(8,128)(2,1)S(1)} %copy-done.1), custom_call_target="tpu_custom_call" | custom-call | flops 268435456 | bytes 4194304 | tf_op jit(solution)/shard_map/rebuild/pallas_call | solution.py:597
  (15 shorter events, 0.1 us)
Async XLA Ops:
  0.6 12.7 %copy-start.2 = (bf16[2,128,128]{2,1,0:T(8,128)(2,1)S(1)}, bf16[2,128,128]{2,1,0:T(8,128)(2,1)}, u32[]{:S(2)}) copy-start(bf16[2,128,128]{2,1,0:T(8,128)(2,1)} %constant.13.clone.m_ref) | copy-start | bytes 196612
  0.6 15.8 %copy-start = (bf16[6,128,128]{2,1,0:T(8,128)(2,1)S(1)}, bf16[6,128,128]{2,1,0:T(8,128)(2,1)}, u32[]{:S(2)}) copy-start(bf16[6,128,128]{2,1,0:T(8,128)(2,1)} %constant.14.clone.m_ref.refs_7_) | copy-start | bytes 589828
  3.8 12.6 %collective-permute-start = (f32[9,8,128]{2,1,0:T(8,128)S(1)}, f32[9,8,128]{2,1,0:T(8,128)S(1)}, u32[]{:S(2)}, u32[]{:S(2)}) collective-permute-start(f32[9,8,128]{2,1,0:T(8,128)S(1)} %get-tuple-element.49), channel_id=1, source_target_pairs={{0,16},{16,32},{32,48},{48,64},{64,80},{80,96},{96,112},{112,0},{1... | collective-permute-start | bytes 110600 | tf_op jit(solution)/shard_map/ppermute | solution.py:615
  3.8 12.6 %collective-permute-start.1 = (f32[9,8,128]{2,1,0:T(8,128)S(1)}, f32[9,8,128]{2,1,0:T(8,128)S(1)}, u32[]{:S(2)}, u32[]{:S(2)}) collective-permute-start(f32[9,8,128]{2,1,0:T(8,128)S(1)} %get-tuple-element.50), channel_id=1, source_target_pairs={{16,0},{32,16},{48,32},{64,48},{80,64},{96,80},{112,96},{0,112},{1... | collective-permute-start | bytes 110600 | tf_op jit(solution)/shard_map/ppermute | solution.py:616
  6.8 9.7 %collective-permute-start.2 = (f32[9,16,128]{2,1,0:T(8,128)S(1)}, f32[9,16,128]{2,1,0:T(8,128)S(1)}, u32[]{:S(2)}, u32[]{:S(2)}) collective-permute-start(f32[9,16,128]{2,1,0:T(8,128)S(1)} %get-tuple-element.51.own_r), channel_id=1, source_target_pairs={{0,1},{1,2},{2,3},{3,4},{4,5},{5,6},{6,7},{7,8},{8,9},{9,10},{10,1... | collective-permute-start | bytes 221192 | tf_op jit(solution)/shard_map/ppermute | solution.py:615
  8.8 7.7 %collective-permute-start.3 = (f32[9,16,128]{2,1,0:T(8,128)S(1)}, f32[9,16,128]{2,1,0:T(8,128)S(1)}, u32[]{:S(2)}, u32[]{:S(2)}) collective-permute-start(f32[9,16,128]{2,1,0:T(8,128)S(1)} %get-tuple-element.52.own_l), channel_id=1, source_target_pairs={{1,0},{2,1},{3,2},{4,3},{5,4},{6,5},{7,6},{8,7},{9,8},{10,9},{11,1... | collective-permute-start | bytes 221192 | tf_op jit(solution)/shard_map/ppermute | solution.py:616
  18.7 5.1 %collective-permute-start.5 = (f32[2,16,128]{2,1,0:T(8,128)S(1)}, f32[2,16,128]{2,1,0:T(8,128)S(1)}, u32[]{:S(2)}, u32[]{:S(2)}) collective-permute-start(f32[2,16,128]{2,1,0:T(8,128)S(1)} %get-tuple-element.54), channel_id=1, source_target_pairs={{0,1},{1,2},{2,3},{3,0},{4,5},{5,6},{6,7},{7,4},{8,9},{9,10},{10,1... | collective-permute-start | bytes 49160 | tf_op jit(solution)/shard_map/ppermute | solution.py:648
  18.8 5.0 %collective-permute-start.6 = (f32[2,16,128]{2,1,0:T(8,128)S(1)}, f32[2,16,128]{2,1,0:T(8,128)S(1)}, u32[]{:S(2)}, u32[]{:S(2)}) collective-permute-start(f32[2,16,128]{2,1,0:T(8,128)S(1)} %get-tuple-element.54), channel_id=1, source_target_pairs={{0,3},{1,0},{2,1},{3,2},{4,7},{5,4},{6,5},{7,6},{8,11},{9,8},{10,9... | collective-permute-start | bytes 49160 | tf_op jit(solution)/shard_map/ppermute | solution.py:648
  22.0 5.2 %collective-permute-start.7 = (f32[2,16,128]{2,1,0:T(8,128)S(1)}, f32[2,16,128]{2,1,0:T(8,128)S(1)}, u32[]{:S(2)}, u32[]{:S(2)}) collective-permute-start(f32[2,16,128]{2,1,0:T(8,128)S(1)} %get-tuple-element.54), channel_id=1, source_target_pairs={{0,2},{1,3},{2,0},{3,1},{4,6},{5,7},{6,4},{7,5},{8,10},{9,11},{10,... | collective-permute-start | bytes 49160 | tf_op jit(solution)/shard_map/ppermute | solution.py:648
  22.0 1.7 %collective-permute-start.4 = (f32[2,8,128]{2,1,0:T(8,128)S(1)}, f32[2,8,128]{2,1,0:T(8,128)S(1)}, u32[]{:S(2)}, u32[]{:S(2)}) collective-permute-start(f32[2,8,128]{2,1,0:T(8,128)S(1)} %get-tuple-element.53), channel_id=1, source_target_pairs={{0,16},{16,0},{32,48},{48,32},{64,80},{80,64},{96,112},{112,96},{1... | collective-permute-start | bytes 24584 | tf_op jit(solution)/shard_map/ppermute | solution.py:648
  22.0 5.6 %copy-start.1 = (bf16[2,256,128]{2,1,0:T(8,128)(2,1)S(1)}, bf16[2,256,128]{2,1,0:T(8,128)(2,1)}, u32[]{:S(2)}) copy-start(bf16[2,256,128]{2,1,0:T(8,128)(2,1)} %constant.15.clone.refs_8_.m_ref) | copy-start | bytes 393220
  27.2 3.8 %collective-permute-start.9 = (f32[2,16,128]{2,1,0:T(8,128)S(1)}, f32[2,16,128]{2,1,0:T(8,128)S(1)}, u32[]{:S(2)}, u32[]{:S(2)}) collective-permute-start(f32[2,16,128]{2,1,0:T(8,128)S(1)} %add_add_fusion), channel_id=1, source_target_pairs={{0,4},{1,5},{2,6},{3,7},{4,0},{5,1},{6,2},{7,3},{8,12},{9,13},{10,... | collective-permute-start | bytes 49160 | tf_op jit(solution)/shard_map/ppermute | solution.py:648
  27.3 3.7 %collective-permute-start.8 = (f32[2,8,128]{2,1,0:T(8,128)S(1)}, f32[2,8,128]{2,1,0:T(8,128)S(1)}, u32[]{:S(2)}, u32[]{:S(2)}) collective-permute-start(f32[2,8,128]{2,1,0:T(8,128)S(1)} %add.56), channel_id=1, source_target_pairs={{0,32},{16,48},{32,0},{48,16},{64,96},{80,112},{96,64},{112,80},{1... | collective-permute-start | bytes 24584 | tf_op jit(solution)/shard_map/ppermute | solution.py:648
  31.0 6.9 %collective-permute-start.11 = (f32[2,16,128]{2,1,0:T(8,128)S(1)}, f32[2,16,128]{2,1,0:T(8,128)S(1)}, u32[]{:S(2)}, u32[]{:S(2)}) collective-permute-start(f32[2,16,128]{2,1,0:T(8,128)S(1)} %add.61), channel_id=1, source_target_pairs={{0,12},{1,13},{2,14},{3,15},{4,8},{5,9},{6,10},{7,11},{8,4},{9,5},... | collective-permute-start | bytes 49160 | tf_op jit(solution)/shard_map/ppermute | solution.py:648
  33.1 4.9 %collective-permute-start.10 = (f32[2,8,128]{2,1,0:T(8,128)S(1)}, f32[2,8,128]{2,1,0:T(8,128)S(1)}, u32[]{:S(2)}, u32[]{:S(2)}) collective-permute-start(f32[2,8,128]{2,1,0:T(8,128)S(1)} %add.60), channel_id=1, source_target_pairs={{0,96},{16,112},{32,64},{48,80},{64,32},{80,48},{96,0},{112,16},{1... | collective-permute-start | bytes 24584 | tf_op jit(solution)/shard_map/ppermute | solution.py:648

commit v5 on v4

--- a/solution.py
+++ b/solution.py
@@ -164,7 +164,7 @@
     cut_x = min(REACH, nx)
     cut = min(REACH, nz)
     group = 8
-    parts = 8
+    parts = 4
     part = nx // parts
 
     def body(v_hbm, xu_ref, xd_ref, zu_ref, zd_ref, v_ref, sems):
@@ -295,6 +295,19 @@
             done(half - hi * unroll, (hi - lo) * unroll)
 
 
+def rim_terms(rim, base, field, zl, zr, own_l, own_r):
+    cells = [r[6 + field % 3] for r in (zl, own_l, own_r, zr)]
+    if field >= 3:
+        cells = [c * r[8] for c, r in zip(cells, (zl, own_l, own_r, zr))]
+    terms = [cells[1] - cells[0], zl[field], cells[3] - cells[2], zr[field]]
+    for q, term in enumerate(terms):
+        hi = term.astype(BF16).astype(F32)
+        lo = (term - hi).astype(BF16).astype(F32)
+        rim[:, base + q, :] = hi
+        rim[:, base + 4 + q, :] = lo
+        rim[:, base + 8 + q, :] = hi
+
+
 class Outbox:
     def __init__(self, sems):
         self.sems, self.copies = sems, []
@@ -352,24 +365,11 @@
     chunks = nx // sub
     rows = nx * ny
 
-    def body(v_ref, i_ref, xl, xr, zl, zr, own_l, own_r, m_ref, gu, gw, tx, tz, st, px, pz, scratch, rim):
-        used = 12 * len(Z_SUMS)
-        rim[:, used:, :] = jnp.zeros((chunks, LANES - used, LANES), F32)
-        for f in range(6):
-            cells = [r[6 + f % 3] for r in (zl, own_l, own_r, zr)]
-            if f >= 3:
-                cells = [c * r[8] for c, r in zip(cells, (zl, own_l, own_r, zr))]
-            terms = [cells[1] - cells[0], zl[f], cells[3] - cells[2], zr[f]]
-            for q, term in enumerate(terms):
-                hi = term.astype(BF16).astype(F32)
-                lo = (term - hi).astype(BF16).astype(F32)
-                rim[:, 12 * f + q, :] = hi
-                rim[:, 12 * f + 4 + q, :] = lo
-                rim[:, 12 * f + 8 + q, :] = hi
-        for c in range(chunks):
-            st[c * LANES : (c + 1) * LANES] = rim[c].T.astype(BF16)
-
-        g = i_ref[...].reshape(rows, nz) + dot(st[...], m_ref[2])
+    def body(v_ref, i_ref, xl, xr, zl, zr, own_l, own_r, m_ref, gu, gw, tx, tz, px, pz, scratch, rim):
+        rim[:, 12:, :] = jnp.zeros((chunks, 4, LANES), F32)
+        rim_terms(rim, 0, 2, zl, zr, own_l, own_r)
+        st = jnp.concatenate([rim[c].T.astype(BF16) for c in range(chunks)], 0)
+        g = i_ref[...].reshape(rows, nz) + dot(st, m_ref[2, 24:40])
         gw[...] = g.reshape(nx, ny, nz)
 
         def write_x(_, i, g):
@@ -416,33 +416,43 @@
     one = jax.ShapeDtypeStruct(velocity.shape[1:], F32)
     sx = jax.ShapeDtypeStruct((2, ny, nz), F32)
     sz = jax.ShapeDtypeStruct((2, chunks, LANES), F32)
-    st = jax.ShapeDtypeStruct((rows, LANES), BF16)
     small = [*x_halo, *z_halo, rims]
     steps_x = sum(len(below_tests(level)) for level in LEVELS["gx"])
     steps_z = sum(len(below_tests(level)) for level in LEVELS["gz"])
     px = jax.ShapeDtypeStruct((steps_x + 1, ny, nz), F32)
     pz = jax.ShapeDtypeStruct((steps_z + 1, chunks, LANES), F32)
-    outs = [one, one, sx, sz, st, px, pz]
+    outs = [one, one, sx, sz, px, pz]
     return pl.pallas_call(
         body,
         in_specs=[VMEM] * (2 + len(small)),
         out_specs=[VMEM] * len(outs),
         out_shape=outs,
-        scratch_shapes=[pltpu.VMEM((nx, ny, nz), F32), pltpu.VMEM((chunks, LANES, LANES), F32)],
+        scratch_shapes=[pltpu.VMEM((nx, ny, nz), F32), pltpu.VMEM((chunks, 16, LANES), F32)],
         compiler_params=params(),
         name="slopes_first",
         cost_estimate=cost(2, nx * ny * nz),
     )(velocity, inner, *small)
 
 
-def slopes_rest(velocity, inner_u, inner_v, x_halo, st, rims, gw):
+def slopes_rest(velocity, inner_u, inner_v, x_halo, z_halo, rims, gw):
     _, nx, ny, nz = velocity.shape
     rows = nx * ny
     parts = 2
 
-    def body(v_ref, iu_ref, iv_ref, xl, xr, st_ref, m_ref, gw_ref, gv, gx, out, s0, s1, made, sems):
+    chunks = rows // LANES
+
+    def body(*refs):
+        v_ref, iu_ref, iv_ref, xl, xr, zl, zr, own_l, own_r, m_ref, gw_ref = refs[:11]
+        gv, gx, st_ref, out, s0, s1, made, rim, sems = refs[11:]
         box = Outbox(sems)
         box.send(gw_ref, out.at[2])
+        used = 12 * len(Z_SUMS)
+        rim[:, 24:36, :] = jnp.zeros((chunks, 12, LANES), F32)
+        rim[:, used:, :] = jnp.zeros((chunks, LANES - used, LANES), F32)
+        for field in (0, 1, 3, 4, 5):
+            rim_terms(rim, 12 * field, field, zl, zr, own_l, own_r)
+        for c in range(chunks):
+            st_ref[c * LANES : (c + 1) * LANES] = rim[c].T.astype(BF16)
         for c, i_ref in enumerate((iu_ref, iv_ref)):
             for p in range(parts):
                 at = pl.ds(p * nx // parts, nx // parts)
@@ -466,19 +476,25 @@
     one = jax.ShapeDtypeStruct((nx, ny, nz), F32)
     return pl.pallas_call(
         body,
-        in_specs=[VMEM] * 8,
-        out_specs=[VMEM, VMEM, ANY],
-        out_shape=[one, one, jax.ShapeDtypeStruct(velocity.shape, F32)],
+        in_specs=[VMEM] * 11,
+        out_specs=[VMEM, VMEM, VMEM, ANY],
+        out_shape=[
+            one,
+            one,
+            jax.ShapeDtypeStruct((rows, LANES), BF16),
+            jax.ShapeDtypeStruct(velocity.shape, F32),
+        ],
         scratch_shapes=[
             pltpu.VMEM((nx, ny, nz), F32),
             pltpu.VMEM((nx, ny, nz), F32),
             pltpu.VMEM((2, nx, ny, nz), F32),
+            pltpu.VMEM((chunks, LANES, LANES), F32),
             pltpu.SemaphoreType.DMA((8,)),
         ],
         compiler_params=params(),
         name="slopes_rest",
         cost_estimate=cost(3, nx * ny * nz),
-    )(velocity, inner_u, inner_v, *x_halo, st, rims, gw)
+    )(velocity, inner_u, inner_v, *x_halo, *z_halo, rims, gw)
 
 
 def prepare(inner, st, rims, slopes, sums):
@@ -580,7 +596,7 @@
             acc = lax.fori_loop(p * nx // parts // 8, (p + 1) * nx // parts // 8, along_x, acc)
             at = pl.ds(p * nx // parts, nx // parts)
             box.send(made.at[0, at], out.at[0, at])
-        rim[:, 6:, :] = jnp.zeros((chunks, LANES - 6, LANES), F32)
+        rim[:, 6:, :] = jnp.zeros((chunks, 10, LANES), F32)
         for q in range(2):
             for p, part in enumerate(split3(zt[q])):
                 rim[:, 3 * q + p, :] = part.astype(F32)
@@ -588,7 +604,7 @@
             at = pl.ds(p * nx // parts, nx // parts)
             here = range(p * chunks // parts, (p + 1) * chunks // parts)
             st = jnp.concatenate([rim[c].T.astype(BF16) for c in here], 0)
-            g = l_ref[at].reshape(rows // parts, nz) + dot(st, m_ref[1, LANES:])
+            g = l_ref[at].reshape(rows // parts, nz) + dot(st, m_ref[1, LANES : LANES + 16])
             made[1, at] = (scale_z * g).reshape(nx // parts, ny, nz)
             box.send(made.at[1, at], out.at[1, at])
         box.wait()
@@ -600,7 +616,7 @@
         out_specs=ANY,
         out_shape=jax.ShapeDtypeStruct(shape, F32),
         scratch_shapes=[
-            pltpu.VMEM((chunks, LANES, LANES), F32),
+            pltpu.VMEM((chunks, 16, LANES), F32),
             pltpu.VMEM(shape, F32),
             pltpu.SemaphoreType.DMA((16,)),
         ],
@@ -693,7 +709,7 @@
     z_halo = (*swap("gz", zu, zd), zd, zu)
     x_halo = swap("gx", xu, xd)
     in_w, in_u, in_v, *in_c = inner_z(vel, inner_mats)
-    gu, gw, tx, tz, st, spot_x, spot_z = slopes_first(vel, in_w, x_halo, z_halo, rims)
+    gu, gw, tx, tz, spot_x, spot_z = slopes_first(vel, in_w, x_halo, z_halo, rims)
     bx = jnp.zeros_like(tx[0])
     bz = jnp.zeros_like(tz[0])
 
@@ -704,7 +720,7 @@
         parts = {axis: exchange(axis, terms[axis][0], LEVELS[axis][done[axis]]) for axis in axes}
         made = ()
         if filler == "rest":
-            made = slopes_rest(vel, in_u, in_v, x_halo, st, rims, gw)
+            made = slopes_rest(vel, in_u, in_v, x_halo, z_halo, rims, gw)
         elif filler == "flux":
             made = divergence(vel, in_c, x_halo)
         elif filler == "prepare":
@@ -712,7 +728,7 @@
         if filler:
             parts, made = lax.optimization_barrier((parts, made))
         if filler == "rest":
-            gv, gq, grad_z = made
+            gv, gq, st, grad_z = made
         elif filler == "prepare":
             in_c, local, grad_x = made
         elif filler == "flux":

time: 40 us -> 38.6 us (0.965)
  starting transfers between devices: 16.8 us -> 16.2 us
  waiting for transfers between devices: 4.92 us -> 4.43 us
    ppermute x8, starting transfers between devices: 7.26 us -> 6.52 us  [exchange(): parts.append(lax.ppermute(terms, axis, pairs))]
    ppermute x8, waiting for transfers between devices: 4.91 us -> 4.42 us  [exchange(): parts.append(lax.ppermute(terms, axis, pairs))]
    pallas_call x1, Pallas kernels: 1.73 us -> 2.21 us  [slopes_rest(): pl.pallas_call(body, in_specs=[VMEM] * 11, out_specs=[VMEM, VMEM, VMEM, A...]
    pallas_call x1, Pallas kernels: 2.24 us -> 1.81 us  [slopes_first(): pl.pallas_call(body, in_specs=[VMEM] * (2 + len(small)), out_specs=[VMEM]...]
  transfers between devices with their start and end apart: 12 -> 12, of which waited for: 3 -> 3; matrix products, arithmetic and copies ran while one was open for 0% -> 0% of each run, Pallas kernels for 25% -> 27%
where the time goes in v5:
time: 38.6 us; the launch traced here: 38.5 us
  Pallas kernels  17 us (44%)
  starting transfers between devices  16.2 us (42%)
  waiting for transfers between devices  4.43 us (11%)
  between operations  0.83 us (2%)
    ppermute x2, starting transfers between devices, swap(): after = lax.ppermute(down, axis, [((i + 1) % n, i) for i in range(n)])  7.61 us
    ppermute x8, starting transfers between devices, exchange(): parts.append(lax.ppermute(terms, axis, pairs))  6.52 us
    ppermute x8, waiting for transfers between devices, exchange(): parts.append(lax.ppermute(terms, axis, pairs))  4.42 us
    pallas_call x1, Pallas kernels, divergence(): pl.pallas_call(body, in_specs=[VMEM] * 6, out_specs=ANY, out_shape=jax.Sh...  3.19 us
    pallas_call x1, Pallas kernels, inner_z(): pl.pallas_call(body, in_specs=[VMEM, VMEM], out_specs=[VMEM] * 6, out_sha...  3.07 us
    pallas_call x1, Pallas kernels, edges_call(): pl.pallas_call(body, in_specs=[HBM], out_specs=[VMEM] * 5, out_shape=[xs,...  2.86 us
    pallas_call x1, Pallas kernels, slopes_rest(): pl.pallas_call(body, in_specs=[VMEM] * 11, out_specs=[VMEM, VMEM, VMEM, A...  2.21 us
    ppermute x2, starting transfers between devices, swap(): before = lax.ppermute(up, axis, [(i, (i + 1) % n) for i in range(n)])  2.07 us
  transfers between devices with their start and end apart: 12, of which 3 were waited for; matrix products, arithmetic and copies ran while one was open for 0% of the time, Pallas kernels for 27%

profile of v5, /device:TPU:0, one launch (start us, length us, event | category | flops | bytes accessed | tf_op | source)
XLA Modules:
  0.0 38.5 jit_solution(10854344956164375456)
XLA Ops:
  0.6 0.0 copy-start.2
  0.6 0.0 copy-start
  0.7 2.9 %edges.1 = (f32[9,8,128]{2,1,0:T(8,128)S(1)}, f32[9,8,128]{2,1,0:T(8,128)S(1)}, f32[9,16,128]{2,1,0:T(8,128)S(1)}, f32[9,16,128]{2,1,0:T(8,128)S(1)}, f32[3,256,8,128]{3,2,1,0:T(8,128)S(1)}) custom-call(f32[3,256,8,128]{3,2,1,0:T(8,128)} %v_hbm.1), custom_call_target="tpu_custom_call" | custom-call | flops 805306368 | bytes 12582912 | tf_op jit(solution)/shard_map/edges/pallas_call | solution.py:220
  3.5 2.1 %collective-permute-start.2 = (f32[9,16,128]{2,1,0:T(8,128)S(1)}, f32[9,16,128]{2,1,0:T(8,128)S(1)}, u32[]{:S(2)}, u32[]{:S(2)}) collective-permute-start(f32[9,16,128]{2,1,0:T(8,128)S(1)} %get-tuple-element.52.own_r.refs_8_), channel_id=1, source_target_pairs={{0,1},{1,2},{2,3},{3,4},{4,5},{5,6},{6,7},{7,8},{8,9},{9,10},{10,1... | collective-permute-start | bytes 221192 | tf_op jit(solution)/shard_map/ppermute | solution.py:631
  5.6 4.7 %collective-permute-start.3 = (f32[9,16,128]{2,1,0:T(8,128)S(1)}, f32[9,16,128]{2,1,0:T(8,128)S(1)}, u32[]{:S(2)}, u32[]{:S(2)}) collective-permute-start(f32[9,16,128]{2,1,0:T(8,128)S(1)} %get-tuple-element.53.own_l.refs_7_), channel_id=1, source_target_pairs={{1,0},{2,1},{3,2},{4,3},{5,4},{6,5},{7,6},{8,7},{9,8},{10,9},{11,1... | collective-permute-start | bytes 221192 | tf_op jit(solution)/shard_map/ppermute | solution.py:632
  10.2 0.0 collective-permute-start
  10.2 3.0 %collective-permute-start.1 = (f32[9,8,128]{2,1,0:T(8,128)S(1)}, f32[9,8,128]{2,1,0:T(8,128)S(1)}, u32[]{:S(2)}, u32[]{:S(2)}) collective-permute-start(f32[9,8,128]{2,1,0:T(8,128)S(1)} %get-tuple-element.51), channel_id=1, source_target_pairs={{16,0},{32,16},{48,32},{64,48},{80,64},{96,80},{112,96},{0,112},{1... | collective-permute-start | bytes 110600 | tf_op jit(solution)/shard_map/ppermute | solution.py:632
  13.2 3.1 %inner_z.1 = (f32[256,8,128]{2,1,0:T(8,128)S(1)}, f32[256,8,128]{2,1,0:T(8,128)S(1)}, f32[256,8,128]{2,1,0:T(8,128)S(1)}, f32[256,8,128]{2,1,0:T(8,128)S(1)}, f3...) custom-call(f32[3,256,8,128]{3,2,1,0:T(8,128)S(1)} %get-tuple-element.48.v_ref.refs_0_, ...), custom_call_target="tpu_custom_call" | custom-call | flops 805306368 | bytes 12582912 | tf_op jit(solution)/shard_map/inner_z/pallas_call | solution.py:351
  16.3 0.0 collective-permute-done.xl.refs_3_
  16.3 0.0 collective-permute-done.1.xr.refs_4_
  16.3 0.0 collective-permute-done.2.zl.refs_5_
  16.3 0.0 collective-permute-done.3.zr.refs_6_
  16.3 1.8 %slopes_first.1 = (f32[256,8,128]{2,1,0:T(8,128)S(1)}, f32[256,8,128]{2,1,0:T(8,128)S(1)}, f32[2,8,128]{2,1,0:T(8,128)S(1)}, f32[2,16,128]{2,1,0:T(8,128)S(1)}, ...) custom-call(f32[3,256,8,128]{3,2,1,0:T(8,128)S(1)} %get-tuple-element.48.v_ref.refs_0_, ...), custom_call_target="tpu_custom_call" | custom-call | flops 268435456 | bytes 4194304 | tf_op jit(solution)/shard_map/slopes_first/pallas_call | solution.py:425
  18.1 0.1 collective-permute-start.5
  18.2 3.2 %collective-permute-start.6 = (f32[2,16,128]{2,1,0:T(8,128)S(1)}, f32[2,16,128]{2,1,0:T(8,128)S(1)}, u32[]{:S(2)}, u32[]{:S(2)}) collective-permute-start(f32[2,16,128]{2,1,0:T(8,128)S(1)} %get-tuple-element.55), channel_id=1, source_target_pairs={{0,3},{1,0},{2,1},{3,2},{4,7},{5,4},{6,5},{7,6},{8,11},{9,8},{10,9... | collective-permute-start | bytes 49160 | tf_op jit(solution)/shard_map/ppermute | solution.py:664
  21.5 0.0 collective-permute-start.7
  21.5 0.0 collective-permute-start.4
  21.5 2.2 %slopes_rest.1 = (f32[256,8,128]{2,1,0:T(8,128)S(1)}, f32[256,8,128]{2,1,0:T(8,128)S(1)}, bf16[2048,128]{1,0:T(8,128)(2,1)S(1)}, f32[3,256,8,128]{3,2,1,0:T(8,128)}) custom-call(f32[3,256,8,128]{3,2,1,0:T(8,128)S(1)} %get-tuple-element.48.v_ref.refs_0_, f32[256,8,128]{2,1,0:T(8,128)S(1)} %get-tuple-element.56.refs_1_, ...), custom_call_target="tpu_custom_call" | custom-call | flops 402653184 | bytes 6291456 | tf_op jit(solution)/shard_map/slopes_rest/pallas_call | solution.py:477
  23.7 0.0 collective-permute-done.4
  23.7 0.0 collective-permute-done.5
  23.7 3.0 %collective-permute-done.7 = f32[2,16,128]{2,1,0:T(8,128)S(1)} collective-permute-done((f32[2,16,128]{2,1,0:T(8,128)S(1)}, f32[2,16,128]{2,1,0:T(8,128)S(1)}, u32[]{:S(2)}, u32[]{:S(2)}) %collective-permute-start.7) | collective-permute-done | bytes 16416 | tf_op jit(solution)/shard_map/ppermute | solution.py:664
  26.7 0.0 collective-permute-start.9
  26.7 0.4 collective-permute-start.8
  27.1 2.0 %prepare.1 = (f32[256,8,128]{2,1,0:T(8,128)S(1)}, f32[256,8,128]{2,1,0:T(8,128)S(1)}, f32[256,8,128]{2,1,0:T(8,128)S(1)}, f32[256,8,128]{2,1,0:T(8,128)S(1)}, f32[3,256,8,128]{3,2,1,0:T(8,128)}) custom-call(f32[256,8,128]{2,1,0:T(8,128)S(1)} %get-tuple-element.67.refs_0_, f32[256,8,128]{2,1,0:T(8,128)S(1)} %get-tuple-element.68.refs_1_, ...), custom_call_target="tpu_custom_call" | custom-call | flops 402653184 | bytes 6291456 | tf_op jit(solution)/shard_map/prepare/pallas_call | solution.py:519
  29.1 1.3 %collective-permute-done.8 = f32[2,8,128]{2,1,0:T(8,128)S(1)} collective-permute-done((f32[2,8,128]{2,1,0:T(8,128)S(1)}, f32[2,8,128]{2,1,0:T(8,128)S(1)}, u32[]{:S(2)}, u32[]{:S(2)}) %collective-permute-start.8) | collective-permute-done | bytes 8224 | tf_op jit(solution)/shard_map/ppermute | solution.py:664
  30.5 0.0 collective-permute-done.9
  30.5 1.3 %collective-permute-start.11 = (f32[2,16,128]{2,1,0:T(8,128)S(1)}, f32[2,16,128]{2,1,0:T(8,128)S(1)}, u32[]{:S(2)}, u32[]{:S(2)}) collective-permute-start(f32[2,16,128]{2,1,0:T(8,128)S(1)} %add.61), channel_id=1, source_target_pairs={{0,12},{1,13},{2,14},{3,15},{4,8},{5,9},{6,10},{7,11},{8,4},{9,5},... | collective-permute-start | bytes 49160 | tf_op jit(solution)/shard_map/ppermute | solution.py:664
  31.8 1.5 %collective-permute-start.10 = (f32[2,8,128]{2,1,0:T(8,128)S(1)}, f32[2,8,128]{2,1,0:T(8,128)S(1)}, u32[]{:S(2)}, u32[]{:S(2)}) collective-permute-start(f32[2,8,128]{2,1,0:T(8,128)S(1)} %add.60), channel_id=1, source_target_pairs={{0,96},{16,112},{32,64},{48,80},{64,32},{80,48},{96,0},{112,16},{1... | collective-permute-start | bytes 24584 | tf_op jit(solution)/shard_map/ppermute | solution.py:664
  33.3 3.2 %divergence.1 = f32[3,256,8,128]{3,2,1,0:T(8,128)} custom-call(f32[3,256,8,128]{3,2,1,0:T(8,128)S(1)} %get-tuple-element.48.v_ref.refs_0_, f32[9,8,128]{2,1,0:T(8,128)S(1)} %collective-permute-done.xl.refs_3_, f32[9,8,128]{2,1,0:T(8,128)S(1)} %collective-permute-done.1.xr.refs_4_, f32[256,8,128]{2,1,0:T(8,128)S(1)} %get-tuple-element.83.rest_0_, ...), custom_call_target="tpu_custom_call" | custom-call | flops 805306368 | bytes 12582912 | tf_op jit(solution)/shard_map/divergence/pallas_call | solution.py:561
  36.5 0.1 collective-permute-done.10
  36.6 0.0 collective-permute-done.11
  36.7 1.8 %rebuild.1 = f32[2,256,8,128]{3,2,1,0:T(8,128)} custom-call(f32[256,8,128]{2,1,0:T(8,128)S(1)} %get-tuple-element.87.l_ref, f32[256,8,128]{2,1,0:T(8,128)S(1)} %get-tuple-element.58.refs_10_.w_ref, f32[2,8,128]{2,1,0:T(8,128)S(1)} %pad_maximum_fusion.1.xt, f32[2,16,128]{2,1,0:T(8,128)S(1)} %pad_maximum_fusion.zt, bf16[2,256,128]{2,1,0:T(8,128)(2,1)S(1)} %copy-done.1), custom_call_target="tpu_custom_call" | custom-call | flops 268435456 | bytes 4194304 | tf_op jit(solution)/shard_map/rebuild/pallas_call | solution.py:613
  (15 shorter events, 0.1 us)
Async XLA Ops:
  0.6 12.6 %copy-start.2 = (bf16[2,128,128]{2,1,0:T(8,128)(2,1)S(1)}, bf16[2,128,128]{2,1,0:T(8,128)(2,1)}, u32[]{:S(2)}) copy-start(bf16[2,128,128]{2,1,0:T(8,128)(2,1)} %constant.13.clone.m_ref) | copy-start | bytes 196612
  0.6 15.7 %copy-start = (bf16[6,128,128]{2,1,0:T(8,128)(2,1)S(1)}, bf16[6,128,128]{2,1,0:T(8,128)(2,1)}, u32[]{:S(2)}) copy-start(bf16[6,128,128]{2,1,0:T(8,128)(2,1)} %constant.14.clone.m_ref.refs_9_.refs_7_) | copy-start | bytes 589828
  3.5 12.8 %collective-permute-start.2 = (f32[9,16,128]{2,1,0:T(8,128)S(1)}, f32[9,16,128]{2,1,0:T(8,128)S(1)}, u32[]{:S(2)}, u32[]{:S(2)}) collective-permute-start(f32[9,16,128]{2,1,0:T(8,128)S(1)} %get-tuple-element.52.own_r.refs_8_), channel_id=1, source_target_pairs={{0,1},{1,2},{2,3},{3,4},{4,5},{5,6},{6,7},{7,8},{8,9},{9,10},{10,1... | collective-permute-start | bytes 221192 | tf_op jit(solution)/shard_map/ppermute | solution.py:631
  5.6 10.7 %collective-permute-start.3 = (f32[9,16,128]{2,1,0:T(8,128)S(1)}, f32[9,16,128]{2,1,0:T(8,128)S(1)}, u32[]{:S(2)}, u32[]{:S(2)}) collective-permute-start(f32[9,16,128]{2,1,0:T(8,128)S(1)} %get-tuple-element.53.own_l.refs_7_), channel_id=1, source_target_pairs={{1,0},{2,1},{3,2},{4,3},{5,4},{6,5},{7,6},{8,7},{9,8},{10,9},{11,1... | collective-permute-start | bytes 221192 | tf_op jit(solution)/shard_map/ppermute | solution.py:632
  10.2 6.0 %collective-permute-start = (f32[9,8,128]{2,1,0:T(8,128)S(1)}, f32[9,8,128]{2,1,0:T(8,128)S(1)}, u32[]{:S(2)}, u32[]{:S(2)}) collective-permute-start(f32[9,8,128]{2,1,0:T(8,128)S(1)} %get-tuple-element.50), channel_id=1, source_target_pairs={{0,16},{16,32},{32,48},{48,64},{64,80},{80,96},{96,112},{112,0},{1... | collective-permute-start | bytes 110600 | tf_op jit(solution)/shard_map/ppermute | solution.py:631
  10.2 6.0 %collective-permute-start.1 = (f32[9,8,128]{2,1,0:T(8,128)S(1)}, f32[9,8,128]{2,1,0:T(8,128)S(1)}, u32[]{:S(2)}, u32[]{:S(2)}) collective-permute-start(f32[9,8,128]{2,1,0:T(8,128)S(1)} %get-tuple-element.51), channel_id=1, source_target_pairs={{16,0},{32,16},{48,32},{64,48},{80,64},{96,80},{112,96},{0,112},{1... | collective-permute-start | bytes 110600 | tf_op jit(solution)/shard_map/ppermute | solution.py:632
  18.1 5.5 %collective-permute-start.5 = (f32[2,16,128]{2,1,0:T(8,128)S(1)}, f32[2,16,128]{2,1,0:T(8,128)S(1)}, u32[]{:S(2)}, u32[]{:S(2)}) collective-permute-start(f32[2,16,128]{2,1,0:T(8,128)S(1)} %get-tuple-element.55), channel_id=1, source_target_pairs={{0,1},{1,2},{2,3},{3,0},{4,5},{5,6},{6,7},{7,4},{8,9},{9,10},{10,1... | collective-permute-start | bytes 49160 | tf_op jit(solution)/shard_map/ppermute | solution.py:664
  18.2 5.5 %collective-permute-start.6 = (f32[2,16,128]{2,1,0:T(8,128)S(1)}, f32[2,16,128]{2,1,0:T(8,128)S(1)}, u32[]{:S(2)}, u32[]{:S(2)}) collective-permute-start(f32[2,16,128]{2,1,0:T(8,128)S(1)} %get-tuple-element.55), channel_id=1, source_target_pairs={{0,3},{1,0},{2,1},{3,2},{4,7},{5,4},{6,5},{7,6},{8,11},{9,8},{10,9... | collective-permute-start | bytes 49160 | tf_op jit(solution)/shard_map/ppermute | solution.py:664
  21.5 5.2 %collective-permute-start.7 = (f32[2,16,128]{2,1,0:T(8,128)S(1)}, f32[2,16,128]{2,1,0:T(8,128)S(1)}, u32[]{:S(2)}, u32[]{:S(2)}) collective-permute-start(f32[2,16,128]{2,1,0:T(8,128)S(1)} %get-tuple-element.55), channel_id=1, source_target_pairs={{0,2},{1,3},{2,0},{3,1},{4,6},{5,7},{6,4},{7,5},{8,10},{9,11},{10,... | collective-permute-start | bytes 49160 | tf_op jit(solution)/shard_map/ppermute | solution.py:664
  21.5 2.2 %collective-permute-start.4 = (f32[2,8,128]{2,1,0:T(8,128)S(1)}, f32[2,8,128]{2,1,0:T(8,128)S(1)}, u32[]{:S(2)}, u32[]{:S(2)}) collective-permute-start(f32[2,8,128]{2,1,0:T(8,128)S(1)} %get-tuple-element.54), channel_id=1, source_target_pairs={{0,16},{16,0},{32,48},{48,32},{64,80},{80,64},{96,112},{112,96},{1... | collective-permute-start | bytes 24584 | tf_op jit(solution)/shard_map/ppermute | solution.py:664
  21.5 5.6 %copy-start.1 = (bf16[2,256,128]{2,1,0:T(8,128)(2,1)S(1)}, bf16[2,256,128]{2,1,0:T(8,128)(2,1)}, u32[]{:S(2)}) copy-start(bf16[2,256,128]{2,1,0:T(8,128)(2,1)} %constant.15.clone.refs_8_.m_ref) | copy-start | bytes 393220
  26.7 3.8 %collective-permute-start.9 = (f32[2,16,128]{2,1,0:T(8,128)S(1)}, f32[2,16,128]{2,1,0:T(8,128)S(1)}, u32[]{:S(2)}, u32[]{:S(2)}) collective-permute-start(f32[2,16,128]{2,1,0:T(8,128)S(1)} %add_add_fusion), channel_id=1, source_target_pairs={{0,4},{1,5},{2,6},{3,7},{4,0},{5,1},{6,2},{7,3},{8,12},{9,13},{10,... | collective-permute-start | bytes 49160 | tf_op jit(solution)/shard_map/ppermute | solution.py:664
  26.7 3.7 %collective-permute-start.8 = (f32[2,8,128]{2,1,0:T(8,128)S(1)}, f32[2,8,128]{2,1,0:T(8,128)S(1)}, u32[]{:S(2)}, u32[]{:S(2)}) collective-permute-start(f32[2,8,128]{2,1,0:T(8,128)S(1)} %add.56), channel_id=1, source_target_pairs={{0,32},{16,48},{32,0},{48,16},{64,96},{80,112},{96,64},{112,80},{1... | collective-permute-start | bytes 24584 | tf_op jit(solution)/shard_map/ppermute | solution.py:664
  30.5 6.2 %collective-permute-start.11 = (f32[2,16,128]{2,1,0:T(8,128)S(1)}, f32[2,16,128]{2,1,0:T(8,128)S(1)}, u32[]{:S(2)}, u32[]{:S(2)}) collective-permute-start(f32[2,16,128]{2,1,0:T(8,128)S(1)} %add.61), channel_id=1, source_target_pairs={{0,12},{1,13},{2,14},{3,15},{4,8},{5,9},{6,10},{7,11},{8,4},{9,5},... | collective-permute-start | bytes 49160 | tf_op jit(solution)/shard_map/ppermute | solution.py:664
  31.8 4.9 %collective-permute-start.10 = (f32[2,8,128]{2,1,0:T(8,128)S(1)}, f32[2,8,128]{2,1,0:T(8,128)S(1)}, u32[]{:S(2)}, u32[]{:S(2)}) collective-permute-start(f32[2,8,128]{2,1,0:T(8,128)S(1)} %add.60), channel_id=1, source_target_pairs={{0,96},{16,112},{32,64},{48,80},{64,32},{80,48},{96,0},{112,16},{1... | collective-permute-start | bytes 24584 | tf_op jit(solution)/shard_map/ppermute | solution.py:664

commit v6 on v5

--- a/solution.py
+++ b/solution.py
@@ -443,21 +443,19 @@
 
     def body(*refs):
         v_ref, iu_ref, iv_ref, xl, xr, zl, zr, own_l, own_r, m_ref, gw_ref = refs[:11]
-        gv, gx, st_ref, out, s0, s1, made, rim, sems = refs[11:]
+        gv, gx, st_ref, out, s0, s1, made, rim, flux_rim, sems = refs[11:]
         box = Outbox(sems)
         box.send(gw_ref, out.at[2])
-        used = 12 * len(Z_SUMS)
-        rim[:, 24:36, :] = jnp.zeros((chunks, 12, LANES), F32)
-        rim[:, used:, :] = jnp.zeros((chunks, LANES - used, LANES), F32)
-        for field in (0, 1, 3, 4, 5):
+        rim[:, 24:32, :] = jnp.zeros((chunks, 8, LANES), F32)
+        for field in (0, 1):
             rim_terms(rim, 12 * field, field, zl, zr, own_l, own_r)
-        for c in range(chunks):
-            st_ref[c * LANES : (c + 1) * LANES] = rim[c].T.astype(BF16)
+        st = jnp.concatenate([rim[c].T.astype(BF16) for c in range(chunks)], 0)
         for c, i_ref in enumerate((iu_ref, iv_ref)):
             for p in range(parts):
                 at = pl.ds(p * nx // parts, nx // parts)
                 local = i_ref[at].reshape(rows // parts, nz)
-                g = local + dot(st_ref[pl.ds(p * rows // parts, rows // parts)], m_ref[c])
+                st_p = st[p * rows // parts : (p + 1) * rows // parts]
+                g = local + dot(st_p, m_ref[c, :32])
                 made[c, at] = g.reshape(nx // parts, ny, nz)
                 box.send(made.at[c, at], out.at[c, at])
 
@@ -471,6 +469,12 @@
             nx,
             [(xl[c], xl[6 + c], xr[c], xr[6 + c]) for c in (1, 2)],
         )
+        flux_rim[:, :4, :] = jnp.zeros((chunks, 4, LANES), F32)
+        flux_rim[:, 40:, :] = jnp.zeros((chunks, 8, LANES), F32)
+        for field in (3, 4, 5):
+            rim_terms(flux_rim, 12 * field - 32, field, zl, zr, own_l, own_r)
+        for c in range(chunks):
+            st_ref[c * LANES : (c + 1) * LANES] = flux_rim[c].T.astype(BF16)
         box.wait()
 
     one = jax.ShapeDtypeStruct((nx, ny, nz), F32)
@@ -481,14 +485,15 @@
         out_shape=[
             one,
             one,
-            jax.ShapeDtypeStruct((rows, LANES), BF16),
+            jax.ShapeDtypeStruct((rows, 48), BF16),
             jax.ShapeDtypeStruct(velocity.shape, F32),
         ],
         scratch_shapes=[
             pltpu.VMEM((nx, ny, nz), F32),
             pltpu.VMEM((nx, ny, nz), F32),
             pltpu.VMEM((2, nx, ny, nz), F32),
-            pltpu.VMEM((chunks, LANES, LANES), F32),
+            pltpu.VMEM((chunks, 32, LANES), F32),
+            pltpu.VMEM((chunks, 48, LANES), F32),
             pltpu.SemaphoreType.DMA((8,)),
         ],
         compiler_params=params(),
@@ -511,7 +516,7 @@
         g = dot(jnp.concatenate([hi, mid], 1), t_ref[0]) + dot(lo, t_ref[1, :LANES])
         local[...] = g.reshape(nx, ny, nz)
         for c in range(3):
-            g = i_refs[c][...].reshape(rows, nz) + dot(st_ref[...], m_ref[3 + c])
+            g = i_refs[c][...].reshape(rows, nz) + dot(st_ref[...], m_ref[3 + c, 32:80])
             c_refs[c][...] = g.reshape(nx, ny, nz)
         box.wait()
 
@@ -575,7 +580,7 @@
     sub = LANES // ny
     chunks = nx // sub
     rows = nx * ny
-    parts = 4
+    parts = 8
     scale_x = -1.0 / math.sqrt(total_x)
     scale_z = -1.0 / math.sqrt(total_z)
 

time: 38.6 us -> 38.6 us (level)
  Pallas kernels: 17 us -> 16.6 us
  transfers between devices with their start and end apart: 12 -> 12, of which waited for: 3 -> 3; matrix products, arithmetic and copies ran while one was open for 0% -> 0% of each run, Pallas kernels for 27% -> 26%
where the time goes in v6:
time: 38.6 us; the launch traced here: 38.5 us
  Pallas kernels  16.6 us (43%)
  starting transfers between devices  16.2 us (42%)
  waiting for transfers between devices  4.79 us (12%)
  between operations  0.83 us (2%)
    ppermute x2, starting transfers between devices, swap(): after = lax.ppermute(down, axis, [((i + 1) % n, i) for i in range(n)])  7.61 us
    ppermute x8, starting transfers between devices, exchange(): parts.append(lax.ppermute(terms, axis, pairs))  6.52 us
    ppermute x8, waiting for transfers between devices, exchange(): parts.append(lax.ppermute(terms, axis, pairs))  4.78 us
    pallas_call x1, Pallas kernels, divergence(): pl.pallas_call(body, in_specs=[VMEM] * 6, out_specs=ANY, out_shape=jax.Sh...  3.19 us
    pallas_call x1, Pallas kernels, inner_z(): pl.pallas_call(body, in_specs=[VMEM, VMEM], out_specs=[VMEM] * 6, out_sha...  3.07 us
    pallas_call x1, Pallas kernels, edges_call(): pl.pallas_call(body, in_specs=[HBM], out_specs=[VMEM] * 5, out_shape=[xs,...  2.86 us
    pallas_call x1, Pallas kernels, slopes_rest(): pl.pallas_call(body, in_specs=[VMEM] * 11, out_specs=[VMEM, VMEM, VMEM, A...  2.2 us
    ppermute x2, starting transfers between devices, swap(): before = lax.ppermute(up, axis, [(i, (i + 1) % n) for i in range(n)])  2.07 us
  transfers between devices with their start and end apart: 12, of which 3 were waited for; matrix products, arithmetic and copies ran while one was open for 0% of the time, Pallas kernels for 26%

profile of v6, /device:TPU:0, one launch (start us, length us, event | category | flops | bytes accessed | tf_op | source)
XLA Modules:
  0.0 38.5 jit_solution(11514131737260477518)
XLA Ops:
  0.6 0.0 copy-start.2
  0.6 0.0 copy-start
  0.7 2.9 %edges.1 = (f32[9,8,128]{2,1,0:T(8,128)S(1)}, f32[9,8,128]{2,1,0:T(8,128)S(1)}, f32[9,16,128]{2,1,0:T(8,128)S(1)}, f32[9,16,128]{2,1,0:T(8,128)S(1)}, f32[3,256,8,128]{3,2,1,0:T(8,128)S(1)}) custom-call(f32[3,256,8,128]{3,2,1,0:T(8,128)} %v_hbm.1), custom_call_target="tpu_custom_call" | custom-call | flops 805306368 | bytes 12582912 | tf_op jit(solution)/shard_map/edges/pallas_call | solution.py:220
  3.5 2.1 %collective-permute-start.2 = (f32[9,16,128]{2,1,0:T(8,128)S(1)}, f32[9,16,128]{2,1,0:T(8,128)S(1)}, u32[]{:S(2)}, u32[]{:S(2)}) collective-permute-start(f32[9,16,128]{2,1,0:T(8,128)S(1)} %get-tuple-element.52.own_r.refs_8_), channel_id=1, source_target_pairs={{0,1},{1,2},{2,3},{3,4},{4,5},{5,6},{6,7},{7,8},{8,9},{9,10},{10,1... | collective-permute-start | bytes 221192 | tf_op jit(solution)/shard_map/ppermute | solution.py:636
  5.6 4.7 %collective-permute-start.3 = (f32[9,16,128]{2,1,0:T(8,128)S(1)}, f32[9,16,128]{2,1,0:T(8,128)S(1)}, u32[]{:S(2)}, u32[]{:S(2)}) collective-permute-start(f32[9,16,128]{2,1,0:T(8,128)S(1)} %get-tuple-element.53.own_l.refs_7_), channel_id=1, source_target_pairs={{1,0},{2,1},{3,2},{4,3},{5,4},{6,5},{7,6},{8,7},{9,8},{10,9},{11,1... | collective-permute-start | bytes 221192 | tf_op jit(solution)/shard_map/ppermute | solution.py:637
  10.2 0.0 collective-permute-start
  10.2 3.0 %collective-permute-start.1 = (f32[9,8,128]{2,1,0:T(8,128)S(1)}, f32[9,8,128]{2,1,0:T(8,128)S(1)}, u32[]{:S(2)}, u32[]{:S(2)}) collective-permute-start(f32[9,8,128]{2,1,0:T(8,128)S(1)} %get-tuple-element.51), channel_id=1, source_target_pairs={{16,0},{32,16},{48,32},{64,48},{80,64},{96,80},{112,96},{0,112},{1... | collective-permute-start | bytes 110600 | tf_op jit(solution)/shard_map/ppermute | solution.py:637
  13.2 3.1 %inner_z.1 = (f32[256,8,128]{2,1,0:T(8,128)S(1)}, f32[256,8,128]{2,1,0:T(8,128)S(1)}, f32[256,8,128]{2,1,0:T(8,128)S(1)}, f32[256,8,128]{2,1,0:T(8,128)S(1)}, f3...) custom-call(f32[3,256,8,128]{3,2,1,0:T(8,128)S(1)} %get-tuple-element.48.v_ref.refs_0_, ...), custom_call_target="tpu_custom_call" | custom-call | flops 805306368 | bytes 12582912 | tf_op jit(solution)/shard_map/inner_z/pallas_call | solution.py:351
  16.3 0.0 collective-permute-done.xl.refs_3_
  16.3 0.0 collective-permute-done.1.xr.refs_4_
  16.3 0.0 collective-permute-done.2.zl.refs_5_
  16.3 0.0 collective-permute-done.3.zr.refs_6_
  16.3 1.8 %slopes_first.1 = (f32[256,8,128]{2,1,0:T(8,128)S(1)}, f32[256,8,128]{2,1,0:T(8,128)S(1)}, f32[2,8,128]{2,1,0:T(8,128)S(1)}, f32[2,16,128]{2,1,0:T(8,128)S(1)}, ...) custom-call(f32[3,256,8,128]{3,2,1,0:T(8,128)S(1)} %get-tuple-element.48.v_ref.refs_0_, ...), custom_call_target="tpu_custom_call" | custom-call | flops 268435456 | bytes 4194304 | tf_op jit(solution)/shard_map/slopes_first/pallas_call | solution.py:425
  18.1 0.1 collective-permute-start.5
  18.2 3.2 %collective-permute-start.6 = (f32[2,16,128]{2,1,0:T(8,128)S(1)}, f32[2,16,128]{2,1,0:T(8,128)S(1)}, u32[]{:S(2)}, u32[]{:S(2)}) collective-permute-start(f32[2,16,128]{2,1,0:T(8,128)S(1)} %get-tuple-element.55), channel_id=1, source_target_pairs={{0,3},{1,0},{2,1},{3,2},{4,7},{5,4},{6,5},{7,6},{8,11},{9,8},{10,9... | collective-permute-start | bytes 49160 | tf_op jit(solution)/shard_map/ppermute | solution.py:669
  21.5 0.0 collective-permute-start.7
  21.5 0.0 collective-permute-start.4
  21.5 2.2 %slopes_rest.1 = (f32[256,8,128]{2,1,0:T(8,128)S(1)}, f32[256,8,128]{2,1,0:T(8,128)S(1)}, bf16[2048,48]{1,0:T(8,128)(2,1)S(1)}, f32[3,256,8,128]{3,2,1,0:T(8,128)}) custom-call(f32[3,256,8,128]{3,2,1,0:T(8,128)S(1)} %get-tuple-element.48.v_ref.refs_0_, f32[256,8,128]{2,1,0:T(8,128)S(1)} %get-tuple-element.56.refs_1_, ...), custom_call_target="tpu_custom_call" | custom-call | flops 402653184 | bytes 6291456 | tf_op jit(solution)/shard_map/slopes_rest/pallas_call | solution.py:481
  23.7 0.0 collective-permute-done.4
  23.7 0.0 collective-permute-done.5
  23.7 0.0 collective-permute-done.6
  23.7 3.0 %collective-permute-done.7 = f32[2,16,128]{2,1,0:T(8,128)S(1)} collective-permute-done((f32[2,16,128]{2,1,0:T(8,128)S(1)}, f32[2,16,128]{2,1,0:T(8,128)S(1)}, u32[]{:S(2)}, u32[]{:S(2)}) %collective-permute-start.7) | collective-permute-done | bytes 16416 | tf_op jit(solution)/shard_map/ppermute | solution.py:669
  26.7 0.0 collective-permute-start.9
  26.7 0.4 collective-permute-start.8
  27.1 1.7 %prepare.1 = (f32[256,8,128]{2,1,0:T(8,128)S(1)}, f32[256,8,128]{2,1,0:T(8,128)S(1)}, f32[256,8,128]{2,1,0:T(8,128)S(1)}, f32[256,8,128]{2,1,0:T(8,128)S(1)}, f32[3,256,8,128]{3,2,1,0:T(8,128)}) custom-call(f32[256,8,128]{2,1,0:T(8,128)S(1)} %get-tuple-element.67.refs_0_, f32[256,8,128]{2,1,0:T(8,128)S(1)} %get-tuple-element.68.refs_1_, ...), custom_call_target="tpu_custom_call" | custom-call | flops 402653184 | bytes 6291456 | tf_op jit(solution)/shard_map/prepare/pallas_call | solution.py:524
  28.8 1.7 %collective-permute-done.8 = f32[2,8,128]{2,1,0:T(8,128)S(1)} collective-permute-done((f32[2,8,128]{2,1,0:T(8,128)S(1)}, f32[2,8,128]{2,1,0:T(8,128)S(1)}, u32[]{:S(2)}, u32[]{:S(2)}) %collective-permute-start.8) | collective-permute-done | bytes 8224 | tf_op jit(solution)/shard_map/ppermute | solution.py:669
  30.5 0.0 collective-permute-done.9
  30.5 1.3 %collective-permute-start.11 = (f32[2,16,128]{2,1,0:T(8,128)S(1)}, f32[2,16,128]{2,1,0:T(8,128)S(1)}, u32[]{:S(2)}, u32[]{:S(2)}) collective-permute-start(f32[2,16,128]{2,1,0:T(8,128)S(1)} %add.61), channel_id=1, source_target_pairs={{0,12},{1,13},{2,14},{3,15},{4,8},{5,9},{6,10},{7,11},{8,4},{9,5},... | collective-permute-start | bytes 49160 | tf_op jit(solution)/shard_map/ppermute | solution.py:669
  31.8 1.5 %collective-permute-start.10 = (f32[2,8,128]{2,1,0:T(8,128)S(1)}, f32[2,8,128]{2,1,0:T(8,128)S(1)}, u32[]{:S(2)}, u32[]{:S(2)}) collective-permute-start(f32[2,8,128]{2,1,0:T(8,128)S(1)} %add.60), channel_id=1, source_target_pairs={{0,96},{16,112},{32,64},{48,80},{64,32},{80,48},{96,0},{112,16},{1... | collective-permute-start | bytes 24584 | tf_op jit(solution)/shard_map/ppermute | solution.py:669
  33.3 3.2 %divergence.1 = f32[3,256,8,128]{3,2,1,0:T(8,128)} custom-call(f32[3,256,8,128]{3,2,1,0:T(8,128)S(1)} %get-tuple-element.48.v_ref.refs_0_, f32[9,8,128]{2,1,0:T(8,128)S(1)} %collective-permute-done.xl.refs_3_, f32[9,8,128]{2,1,0:T(8,128)S(1)} %collective-permute-done.1.xr.refs_4_, f32[256,8,128]{2,1,0:T(8,128)S(1)} %get-tuple-element.83.rest_0_, ...), custom_call_target="tpu_custom_call" | custom-call | flops 805306368 | bytes 12582912 | tf_op jit(solution)/shard_map/divergence/pallas_call | solution.py:566
  36.5 0.1 collective-permute-done.10
  36.7 1.8 %rebuild.1 = f32[2,256,8,128]{3,2,1,0:T(8,128)} custom-call(f32[256,8,128]{2,1,0:T(8,128)S(1)} %get-tuple-element.87.l_ref, f32[256,8,128]{2,1,0:T(8,128)S(1)} %get-tuple-element.58.refs_10_.w_ref, f32[2,8,128]{2,1,0:T(8,128)S(1)} %pad_maximum_fusion.1.xt, f32[2,16,128]{2,1,0:T(8,128)S(1)} %pad_maximum_fusion.zt, bf16[2,256,128]{2,1,0:T(8,128)(2,1)S(1)} %copy-done.1), custom_call_target="tpu_custom_call" | custom-call | flops 268435456 | bytes 4194304 | tf_op jit(solution)/shard_map/rebuild/pallas_call | solution.py:618
  (15 shorter events, 0.1 us)
Async XLA Ops:
  0.6 12.6 %copy-start.2 = (bf16[2,128,128]{2,1,0:T(8,128)(2,1)S(1)}, bf16[2,128,128]{2,1,0:T(8,128)(2,1)}, u32[]{:S(2)}) copy-start(bf16[2,128,128]{2,1,0:T(8,128)(2,1)} %constant.13.clone.m_ref) | copy-start | bytes 196612
  0.6 15.7 %copy-start = (bf16[6,128,128]{2,1,0:T(8,128)(2,1)S(1)}, bf16[6,128,128]{2,1,0:T(8,128)(2,1)}, u32[]{:S(2)}) copy-start(bf16[6,128,128]{2,1,0:T(8,128)(2,1)} %constant.14.clone.m_ref.refs_9_.refs_7_) | copy-start | bytes 589828
  3.5 12.8 %collective-permute-start.2 = (f32[9,16,128]{2,1,0:T(8,128)S(1)}, f32[9,16,128]{2,1,0:T(8,128)S(1)}, u32[]{:S(2)}, u32[]{:S(2)}) collective-permute-start(f32[9,16,128]{2,1,0:T(8,128)S(1)} %get-tuple-element.52.own_r.refs_8_), channel_id=1, source_target_pairs={{0,1},{1,2},{2,3},{3,4},{4,5},{5,6},{6,7},{7,8},{8,9},{9,10},{10,1... | collective-permute-start | bytes 221192 | tf_op jit(solution)/shard_map/ppermute | solution.py:636
  5.6 10.7 %collective-permute-start.3 = (f32[9,16,128]{2,1,0:T(8,128)S(1)}, f32[9,16,128]{2,1,0:T(8,128)S(1)}, u32[]{:S(2)}, u32[]{:S(2)}) collective-permute-start(f32[9,16,128]{2,1,0:T(8,128)S(1)} %get-tuple-element.53.own_l.refs_7_), channel_id=1, source_target_pairs={{1,0},{2,1},{3,2},{4,3},{5,4},{6,5},{7,6},{8,7},{9,8},{10,9},{11,1... | collective-permute-start | bytes 221192 | tf_op jit(solution)/shard_map/ppermute | solution.py:637
  10.2 6.0 %collective-permute-start = (f32[9,8,128]{2,1,0:T(8,128)S(1)}, f32[9,8,128]{2,1,0:T(8,128)S(1)}, u32[]{:S(2)}, u32[]{:S(2)}) collective-permute-start(f32[9,8,128]{2,1,0:T(8,128)S(1)} %get-tuple-element.50), channel_id=1, source_target_pairs={{0,16},{16,32},{32,48},{48,64},{64,80},{80,96},{96,112},{112,0},{1... | collective-permute-start | bytes 110600 | tf_op jit(solution)/shard_map/ppermute | solution.py:636
  10.2 6.0 %collective-permute-start.1 = (f32[9,8,128]{2,1,0:T(8,128)S(1)}, f32[9,8,128]{2,1,0:T(8,128)S(1)}, u32[]{:S(2)}, u32[]{:S(2)}) collective-permute-start(f32[9,8,128]{2,1,0:T(8,128)S(1)} %get-tuple-element.51), channel_id=1, source_target_pairs={{16,0},{32,16},{48,32},{64,48},{80,64},{96,80},{112,96},{0,112},{1... | collective-permute-start | bytes 110600 | tf_op jit(solution)/shard_map/ppermute | solution.py:637
  18.1 5.5 %collective-permute-start.5 = (f32[2,16,128]{2,1,0:T(8,128)S(1)}, f32[2,16,128]{2,1,0:T(8,128)S(1)}, u32[]{:S(2)}, u32[]{:S(2)}) collective-permute-start(f32[2,16,128]{2,1,0:T(8,128)S(1)} %get-tuple-element.55), channel_id=1, source_target_pairs={{0,1},{1,2},{2,3},{3,0},{4,5},{5,6},{6,7},{7,4},{8,9},{9,10},{10,1... | collective-permute-start | bytes 49160 | tf_op jit(solution)/shard_map/ppermute | solution.py:669
  18.2 5.5 %collective-permute-start.6 = (f32[2,16,128]{2,1,0:T(8,128)S(1)}, f32[2,16,128]{2,1,0:T(8,128)S(1)}, u32[]{:S(2)}, u32[]{:S(2)}) collective-permute-start(f32[2,16,128]{2,1,0:T(8,128)S(1)} %get-tuple-element.55), channel_id=1, source_target_pairs={{0,3},{1,0},{2,1},{3,2},{4,7},{5,4},{6,5},{7,6},{8,11},{9,8},{10,9... | collective-permute-start | bytes 49160 | tf_op jit(solution)/shard_map/ppermute | solution.py:669
  21.5 5.2 %collective-permute-start.7 = (f32[2,16,128]{2,1,0:T(8,128)S(1)}, f32[2,16,128]{2,1,0:T(8,128)S(1)}, u32[]{:S(2)}, u32[]{:S(2)}) collective-permute-start(f32[2,16,128]{2,1,0:T(8,128)S(1)} %get-tuple-element.55), channel_id=1, source_target_pairs={{0,2},{1,3},{2,0},{3,1},{4,6},{5,7},{6,4},{7,5},{8,10},{9,11},{10,... | collective-permute-start | bytes 49160 | tf_op jit(solution)/shard_map/ppermute | solution.py:669
  21.5 2.2 %collective-permute-start.4 = (f32[2,8,128]{2,1,0:T(8,128)S(1)}, f32[2,8,128]{2,1,0:T(8,128)S(1)}, u32[]{:S(2)}, u32[]{:S(2)}) collective-permute-start(f32[2,8,128]{2,1,0:T(8,128)S(1)} %get-tuple-element.54), channel_id=1, source_target_pairs={{0,16},{16,0},{32,48},{48,32},{64,80},{80,64},{96,112},{112,96},{1... | collective-permute-start | bytes 24584 | tf_op jit(solution)/shard_map/ppermute | solution.py:669
  21.5 5.6 %copy-start.1 = (bf16[2,256,128]{2,1,0:T(8,128)(2,1)S(1)}, bf16[2,256,128]{2,1,0:T(8,128)(2,1)}, u32[]{:S(2)}) copy-start(bf16[2,256,128]{2,1,0:T(8,128)(2,1)} %constant.15.clone.refs_8_.m_ref) | copy-start | bytes 393220
  26.7 3.8 %collective-permute-start.9 = (f32[2,16,128]{2,1,0:T(8,128)S(1)}, f32[2,16,128]{2,1,0:T(8,128)S(1)}, u32[]{:S(2)}, u32[]{:S(2)}) collective-permute-start(f32[2,16,128]{2,1,0:T(8,128)S(1)} %add_add_fusion), channel_id=1, source_target_pairs={{0,4},{1,5},{2,6},{3,7},{4,0},{5,1},{6,2},{7,3},{8,12},{9,13},{10,... | collective-permute-start | bytes 49160 | tf_op jit(solution)/shard_map/ppermute | solution.py:669
  26.7 3.7 %collective-permute-start.8 = (f32[2,8,128]{2,1,0:T(8,128)S(1)}, f32[2,8,128]{2,1,0:T(8,128)S(1)}, u32[]{:S(2)}, u32[]{:S(2)}) collective-permute-start(f32[2,8,128]{2,1,0:T(8,128)S(1)} %add.56), channel_id=1, source_target_pairs={{0,32},{16,48},{32,0},{48,16},{64,96},{80,112},{96,64},{112,80},{1... | collective-permute-start | bytes 24584 | tf_op jit(solution)/shard_map/ppermute | solution.py:669
  30.5 6.2 %collective-permute-start.11 = (f32[2,16,128]{2,1,0:T(8,128)S(1)}, f32[2,16,128]{2,1,0:T(8,128)S(1)}, u32[]{:S(2)}, u32[]{:S(2)}) collective-permute-start(f32[2,16,128]{2,1,0:T(8,128)S(1)} %add.61), channel_id=1, source_target_pairs={{0,12},{1,13},{2,14},{3,15},{4,8},{5,9},{6,10},{7,11},{8,4},{9,5},... | collective-permute-start | bytes 49160 | tf_op jit(solution)/shard_map/ppermute | solution.py:669
  31.8 4.9 %collective-permute-start.10 = (f32[2,8,128]{2,1,0:T(8,128)S(1)}, f32[2,8,128]{2,1,0:T(8,128)S(1)}, u32[]{:S(2)}, u32[]{:S(2)}) collective-permute-start(f32[2,8,128]{2,1,0:T(8,128)S(1)} %add.60), channel_id=1, source_target_pairs={{0,96},{16,112},{32,64},{48,80},{64,32},{80,48},{96,0},{112,16},{1... | collective-permute-start | bytes 24584 | tf_op jit(solution)/shard_map/ppermute | solution.py:669
